TPU v7x, 128 devices: a whole 4x4x4 slice. The times are simulated.
128 devices in a mesh: seq: 16 (over z, y), head: 8 (over x, core).
Axes of the slice: x: 4, y: 4, z: 4, core: 2. Of those that a mesh axis runs over, the one named last changes fastest.
Arguments:
- ssd_input: bfloat16 [8192, 128, 128], P('seq', 'head'), may hold values from -3 to 3
- log_decay: float32 [8192, 128], P('seq', 'head'), may hold values from -1.6 to 0, as said below
- input_map: float32 [8192, 8, 128], P('seq', 'head'), may hold values from -0.18 to 0.18
- output_map: float32 [8192, 8, 128], P('seq', 'head'), may hold values from -0.18 to 0.18
- ssd_cotangent: bfloat16 [8192, 128, 128], P('seq', 'head'), may hold values from -3 to 3
- queries: bfloat16 [8192, 8, 128], P('seq', 'head'), may hold values from -100 to 100
- key_rows: bfloat16 [8192, 128], P('seq'), may hold values from -4 to 4
- value_rows: bfloat16 [8192, 128], P('seq'), may hold values from -6 to 6
- attn_cotangent: bfloat16 [8192, 8, 128], P('seq', 'head'), may hold values from -6 to 6
- pair_order: int32 [16], replicated, may hold values from 0 to 15, each once
Outputs:
- grad_input: bfloat16 [8192, 128, 128], P('seq', 'head')
- grad_decay: float32 [8192, 128], P('seq', 'head')
- grad_input_map: float32 [8192, 8, 128], P('seq', 'head')
- grad_output_map: float32 [8192, 8, 128], P('seq', 'head')
- grad_queries: bfloat16 [8192, 8, 128], P('seq', 'head')
- grad_keys: bfloat16 [8192, 128], P('seq')
- grad_values: bfloat16 [8192, 128], P('seq')
Inputs may be any that keep to these rules, and one draw needn't show every extreme that they name: `pair_order`: a permutation of 0 to 15. `log_decay`: negative everywhere.
All inputs are finite; a program needn't handle non-finite values.
Results may differ from a plain program's by a relative error of at most 0.035.
Values may be sent and summed in bfloat16 or wider, within the bound.
No kernel may reach another device: no remote copies, remote signals or barrier semaphores. Data moves between devices by JAX's collectives and lax.ppermute only.
A program may use at most 192 MiB of HBM per device.

v0:
```python
import jax
import jax.numpy as jnp
from jax import lax
from jax.sharding import PartitionSpec as P

BLOCK = 128


HIGHEST = lax.Precision.HIGHEST
NEG_FILL = -1e30
TILE_PAIRS = ((0, 0), (1, 0), (1, 1))


def carried_in(array, axis, join, neutral, backward):
    count = lax.axis_size(axis)
    place = lax.axis_index(axis)
    ahead = count - 1 - place if backward else place
    gathered = jax.tree.map(
        lambda a, kind: lax.all_gather(a.astype(kind), axis), array, (jnp.bfloat16, jnp.bfloat16)
    )
    state = jax.tree.map(lambda a, e: jnp.zeros_like(a) + jnp.asarray(e, a.dtype), array, neutral)

    def one(step, state):
        source = count - 1 - step if backward else step
        return join(
            state,
            jax.tree.map(
                lambda a, own: lax.dynamic_index_in_dim(a, source, 0, False).astype(own.dtype),
                gathered,
                array,
            ),
        )

    return lax.fori_loop(0, ahead, one, state)


def through_bf16(values):
    return lax.optimization_barrier(values.astype(jnp.bfloat16)).astype(jnp.float32)


def block_advance(state_now, inputs):
    x_block, a_block, b_block, c_block = inputs
    cumulative = jnp.cumsum(a_block, axis=0)
    block_len = a_block.shape[0]
    causal_mask = (jnp.arange(block_len)[:, None] >= jnp.arange(block_len)[None, :])[
        :, :, None, None
    ]
    decay_grid = jnp.exp(
        jnp.where(causal_mask, cumulative[:, None] - cumulative[None, :], NEG_FILL)
    )
    inner_prod = jnp.einsum("tgn,sgn->tsg", c_block, b_block, precision=HIGHEST)
    weight_grid = (inner_prod[:, :, :, None] * decay_grid).astype(jnp.bfloat16)
    local_part = jnp.einsum(
        "tsge,sgep->tgep", weight_grid, x_block, preferred_element_type=jnp.float32
    )
    c_scaled = (c_block[:, :, None, :] * jnp.exp(cumulative)[..., None]).astype(jnp.bfloat16)
    carried_part = jnp.einsum(
        "tgen,genp->tgep",
        c_scaled,
        state_now.astype(jnp.bfloat16),
        preferred_element_type=jnp.float32,
    )
    block_out = (local_part + carried_part).astype(jnp.bfloat16)
    tail_decay = jnp.exp(cumulative[-1][None] - cumulative)
    b_scaled = (b_block[:, :, None, :] * tail_decay[..., None]).astype(jnp.bfloat16)
    fresh_state = jnp.einsum(
        "tgen,tgep->genp", b_scaled, x_block, preferred_element_type=jnp.float32
    )
    return (jnp.exp(cumulative[-1])[..., None, None] * state_now + fresh_state, block_out)


def blocked(values):
    return values.reshape((values.shape[0] // BLOCK, BLOCK) + values.shape[1:])


def run_blocks(x_seq, a_seq, b_seq, c_seq, state_start):
    state_end, block_outs = lax.scan(
        block_advance, state_start, (blocked(x_seq), blocked(a_seq), blocked(b_seq), blocked(c_seq))
    )
    return (block_outs.reshape(x_seq.shape), state_end)


def local_state(x_local, a_local, b_local):
    cumulative = jnp.cumsum(blocked(a_local), axis=1)
    block_total = cumulative[:, -1]
    tail_decay = jnp.exp(block_total[:, None] - cumulative)
    b_scaled = (blocked(b_local)[:, :, :, None, :] * tail_decay[..., None]).astype(jnp.bfloat16)
    fresh_state = jnp.einsum(
        "ctgen,ctgep->cgenp", b_scaled, blocked(x_local), preferred_element_type=jnp.float32
    )
    own_total = jnp.sum(block_total, axis=0)
    later_decay = own_total[None] - jnp.cumsum(block_total, axis=0)
    return (
        jnp.einsum("cge,cgenp->genp", jnp.exp(later_decay), fresh_state, precision=HIGHEST),
        own_total,
    )


def output_pull(a_local, c_local, dy_local):
    cumulative = jnp.cumsum(blocked(a_local), axis=1)
    block_total = cumulative[:, -1]
    earlier_decay = jnp.cumsum(block_total, axis=0) - block_total
    c_scaled = (blocked(c_local)[:, :, :, None, :] * jnp.exp(cumulative)[..., None]).astype(
        jnp.bfloat16
    )
    pulled = jnp.einsum(
        "ctgen,ctgep->cgenp", c_scaled, blocked(dy_local), preferred_element_type=jnp.float32
    )
    return jnp.einsum(
        "cge,cgenp->genp", jnp.exp(earlier_decay), through_bf16(pulled), precision=HIGHEST
    )


def affine_combine(earlier, later):
    return (earlier[0] + later[0], jnp.exp(later[0])[..., None, None] * earlier[1] + later[1])


def tile_scores(query_part, query_at, key_part, key_at, scale_factor):
    raw_scores = (
        jnp.einsum("hqd,kd->hqk", query_part, key_part, preferred_element_type=jnp.float32)
        * scale_factor
    )
    return jnp.where(key_at[None, None, :] <= query_at[None, :, None], raw_scores, NEG_FILL)


def run_tile(flag, work, fallback, operand):
    if flag is None:
        return work(operand)
    return lax.cond(flag, work, fallback, operand)


def unchanged(stat_pair):
    return stat_pair


def per_device(
    ssd_input,
    log_decay,
    input_map,
    output_map,
    ssd_cotangent,
    queries,
    key_rows,
    value_rows,
    attn_cotangent,
    pair_order,
):
    seq_count = lax.axis_size("seq")
    seq_pos = lax.axis_index("seq")
    tok_rows, head_count, head_width = ssd_input.shape
    group_count = input_map.shape[1]
    per_group = head_count // group_count
    x_local = ssd_input.reshape(tok_rows, group_count, per_group, head_width)
    a_local = log_decay.reshape(tok_rows, group_count, per_group)
    dy_local = ssd_cotangent.reshape(tok_rows, group_count, per_group, head_width)
    own_state, own_total = local_state(x_local, a_local, input_map)
    own_pull = output_pull(a_local, output_map, dy_local)
    zero_state = jnp.zeros_like(own_state)
    zero_total = jnp.zeros_like(own_total)
    state_in = carried_in(
        (own_total, own_state), "seq", affine_combine, (zero_total, zero_state), False
    )[1]
    later_grad = carried_in(
        (own_total, own_pull), "seq", affine_combine, (zero_total, zero_state), True
    )[1]
    primal, pullback = jax.vjp(run_blocks, x_local, a_local, input_map, output_map, state_in)
    gradients = pullback((dy_local, later_grad))
    grad_input = gradients[0].reshape(tok_rows, head_count, head_width)
    grad_decay = gradients[1].reshape(tok_rows, head_count)
    grad_input_map = gradients[2]
    grad_output_map = gradients[3]
    att_rows, heads_here, att_width = queries.shape
    half_rows = att_rows // 2
    scale_factor = att_width ** (-0.5)
    keys_all, values_all = (
        lax.all_gather(key_rows, "seq", axis=0, tiled=True),
        lax.all_gather(value_rows, "seq", axis=0, tiled=True),
    )
    last_block = 2 * seq_count - 1
    own_first = pair_order[seq_pos]
    query_ids = (own_first, last_block - own_first)
    offsets = jnp.arange(half_rows)
    query_heads = queries.transpose(1, 0, 2)
    grad_heads = attn_cotangent.transpose(1, 0, 2)
    query_parts = (query_heads[:, :half_rows], query_heads[:, half_rows:])
    grad_parts = (grad_heads[:, :half_rows], grad_heads[:, half_rows:])
    query_pos = (query_ids[0] * half_rows + offsets, query_ids[1] * half_rows + offsets)

    def tile_needed(pair_index, other_first):
        if pair_index == 0:
            return other_first <= own_first
        if pair_index == 2:
            return other_first >= own_first
        return None

    def key_tiles(device, key_index):
        start_row = device * att_rows + key_index * half_rows
        return (
            lax.dynamic_slice_in_dim(keys_all, start_row, half_rows, 0),
            lax.dynamic_slice_in_dim(values_all, start_row, half_rows, 0),
        )

    def stat_turn(device, stat_pairs):
        other_first = pair_order[device]
        key_ids = (other_first, last_block - other_first)
        updated = list(stat_pairs)
        for pair_index in range(3):
            query_index, key_index = TILE_PAIRS[pair_index]
            key_part, value_part = key_tiles(device, key_index)
            key_at = key_ids[key_index] * half_rows + offsets

            def refresh(stat_pair, query_index=query_index, key_part=key_part, key_at=key_at):
                scores = tile_scores(
                    query_parts[query_index], query_pos[query_index], key_part, key_at, scale_factor
                )
                row_top = jnp.maximum(stat_pair[0], jnp.max(scores, axis=-1))
                row_total = stat_pair[1] * jnp.exp(stat_pair[0] - row_top) + jnp.sum(
                    jnp.exp(scores - row_top[..., None]), axis=-1
                )
                return (row_top, row_total)

            updated[query_index] = run_tile(
                tile_needed(pair_index, other_first), refresh, unchanged, updated[query_index]
            )
        return tuple(updated)

    stat_start = jnp.full((heads_here, half_rows), NEG_FILL, jnp.float32)
    sum_start = jnp.zeros((heads_here, half_rows), jnp.float32)
    row_stats = lax.fori_loop(
        0, seq_count, stat_turn, ((stat_start, sum_start), (stat_start, sum_start))
    )

    def tile_probs(query_index, key_part, key_at):
        scores = tile_scores(
            query_parts[query_index], query_pos[query_index], key_part, key_at, scale_factor
        )
        return (
            jnp.exp(scores - row_stats[query_index][0][..., None])
            / row_stats[query_index][1][..., None]
        )

    def out_turn(device, out_sums):
        other_first = pair_order[device]
        key_ids = (other_first, last_block - other_first)
        updated = list(out_sums)
        for pair_index in range(3):
            query_index, key_index = TILE_PAIRS[pair_index]
            key_part, value_part = key_tiles(device, key_index)
            key_at = key_ids[key_index] * half_rows + offsets

            def add_out(
                out_sum,
                query_index=query_index,
                key_part=key_part,
                value_part=value_part,
                key_at=key_at,
            ):
                prob_b = tile_probs(query_index, key_part, key_at).astype(jnp.bfloat16)
                return out_sum + jnp.einsum(
                    "hqk,kd->hqd", prob_b, value_part, preferred_element_type=jnp.float32
                )

            updated[query_index] = run_tile(
                tile_needed(pair_index, other_first), add_out, unchanged, updated[query_index]
            )
        return tuple(updated)

    out_zero = jnp.zeros((heads_here, half_rows, att_width), jnp.float32)
    out_sums = lax.fori_loop(0, seq_count, out_turn, (out_zero, out_zero))
    row_delta = tuple(
        (
            jnp.sum(
                grad_parts[index_part].astype(jnp.float32)
                * out_sums[index_part].astype(jnp.bfloat16).astype(jnp.float32),
                axis=-1,
            )
            for index_part in range(2)
        )
    )
    key_count = keys_all.shape[0]
    tile_zero = jnp.zeros((half_rows, att_width), jnp.float32)

    def grad_turn(device, grad_state):
        query_grads = list(grad_state[:2])
        other_first = pair_order[device]
        key_ids = (other_first, last_block - other_first)
        key_halves = [tile_zero, tile_zero]
        value_halves = [tile_zero, tile_zero]
        for pair_index in range(3):
            query_index, key_index = TILE_PAIRS[pair_index]
            key_part, value_part = key_tiles(device, key_index)
            key_at = key_ids[key_index] * half_rows + offsets

            def tile_grads(
                key_piece, query_index=query_index, value_part=value_part, key_at=key_at
            ):
                probs = tile_probs(query_index, key_piece, key_at)
                prob_grad = jnp.einsum(
                    "hqd,kd->hqk",
                    grad_parts[query_index],
                    value_part,
                    preferred_element_type=jnp.float32,
                )
                dscore = (probs * (prob_grad - row_delta[query_index][..., None])).astype(
                    jnp.bfloat16
                )
                query_add = (
                    jnp.einsum("hqk,kd->hqd", dscore, key_piece, preferred_element_type=jnp.float32)
                    * scale_factor
                )
                prob_b = probs.astype(jnp.bfloat16)
                key_add = (
                    jnp.einsum(
                        "hqk,hqd->kd",
                        dscore,
                        query_parts[query_index],
                        preferred_element_type=jnp.float32,
                    )
                    * scale_factor
                )
                value_add = jnp.einsum(
                    "hqk,hqd->kd",
                    prob_b,
                    grad_parts[query_index],
                    preferred_element_type=jnp.float32,
                )
                return (query_add, key_add, value_add)

            def tile_skip(key_piece):
                return (out_zero, tile_zero, tile_zero)

            added = run_tile(tile_needed(pair_index, other_first), tile_grads, tile_skip, key_part)
            query_grads[query_index] = query_grads[query_index] + added[0]
            key_halves[key_index] = key_halves[key_index] + added[1]
            value_halves[key_index] = value_halves[key_index] + added[2]
        key_grad_all = lax.dynamic_update_slice_in_dim(
            grad_state[2], jnp.concatenate(key_halves, axis=0), device * att_rows, 0
        )
        value_grad_all = lax.dynamic_update_slice_in_dim(
            grad_state[3], jnp.concatenate(value_halves, axis=0), device * att_rows, 0
        )
        return (query_grads[0], query_grads[1], key_grad_all, value_grad_all)

    full_zero = jnp.zeros((key_count, att_width), jnp.float32)
    grad_start = (out_zero, out_zero, full_zero, full_zero)
    grad_state = lax.fori_loop(0, seq_count, grad_turn, grad_start)
    grad_queries = (
        jnp.concatenate((grad_state[0], grad_state[1]), axis=1)
        .transpose(1, 0, 2)
        .astype(jnp.bfloat16)
    )
    key_part_sum, value_part_sum = (
        lax.psum_scatter(
            grad_state[2].astype(jnp.bfloat16), "seq", scatter_dimension=0, tiled=True
        ).astype(jnp.float32),
        lax.psum_scatter(
            grad_state[3].astype(jnp.bfloat16), "seq", scatter_dimension=0, tiled=True
        ).astype(jnp.float32),
    )
    key_total, value_total = (
        lax.psum(key_part_sum.astype(jnp.bfloat16), "head").astype(jnp.float32),
        lax.psum(value_part_sum.astype(jnp.bfloat16), "head").astype(jnp.float32),
    )
    grad_keys = key_total.astype(jnp.bfloat16)
    grad_values = value_total.astype(jnp.bfloat16)
    return (
        grad_input,
        grad_decay,
        grad_input_map,
        grad_output_map,
        grad_queries,
        grad_keys,
        grad_values,
    )


def solution(mesh):
    return jax.shard_map(
        per_device,
        mesh=mesh,
        in_specs=(
            P("seq", "head", None),
            P("seq", "head"),
            P("seq", "head", None),
            P("seq", "head", None),
            P("seq", "head", None),
            P("seq", "head", None),
            P("seq", None),
            P("seq", None),
            P("seq", "head", None),
            P(),
        ),
        out_specs=(
            P("seq", "head", None),
            P("seq", "head"),
            P("seq", "head", None),
            P("seq", "head", None),
            P("seq", "head", None),
            P("seq", None),
            P("seq", None),
        ),
        check_vma=False,
    )
```

profile of v0, /device:TPU:1, one launch (start us, length us, event | category | flops | bytes accessed | tf_op | source)
XLA Modules:
  0.0 960.2 jit_solution(16763538976158964652)
XLA Ops:
  12.2 45.4 %all-gather.8.cloned.1.call-done = bf16[8192,128]{1,0:T(8,128)(2,1)} async-done(((bf16[512,128]{1,0:T(8,128)(2,1)}), bf16[8192,128]{1,0:T(8,128)(2,1)}) %all-gather.8.cloned.1.call-update) | async-done | bytes 2097168 | tf_op jit(solution)/shard_map/all_gather | solution.py:176
  57.6 99.3 %while.163 = (s32[]{:T(128)}, f32[1,256]{1,0:T(1,128)S(1)}, f32[1,256]{1,0:T(1,128)S(1)}, f32[1,256]{1,0:T(1,128)S(1)}, f32[1,256]{1,0:T(1,128)S(1)}, /*index=5*...) while((s32[]{:T(128)}, f32[1,256]{1,0:T(1,128)S(1)}, ...), condition=%wide.region_33.34_spmd.clone.clone, body=%wide.region_22.33_spmd.clone.clone.sunk | while | flops 51514128 | bytes 2153009 | solution.py:229
  62.0 1.8 conditional.25
  157.0 102.6 %while.164 = (s32[]{:T(128)}, f32[1,256,128]{2,1,0:T(8,128)S(1)}, f32[1,256,128]{2,1,0:T(8,128)S(1)}, s32[16]{0:T(128)}, s32[]{:T(128)}, /*index=5*/bf16[8192,12...) while((s32[]{:T(128)}, f32[1,256,128]{2,1,0:T(8,128)S(1)}, ...), condition=%wide.region_39.40_spmd.clone.clone, body=%wide.region_34.39_spmd.clone.clone.sunk | while | flops 101942544 | bytes 1661477 | solution.py:269
  161.6 2.0 conditional.27
  259.9 1.5 broadcast_in_dim.303.clone
  261.4 141.0 %while.165 = (s32[]{:T(128)}, f32[1,256,128]{2,1,0:T(8,128)S(1)}, f32[1,256,128]{2,1,0:T(8,128)S(1)}, bf16[8192,128]{1,0:T(8,128)(2,1)S(1)}, bf16[8192,128]{1,0:...) while((s32[]{:T(128)}, f32[1,256,128]{2,1,0:T(8,128)S(1)}, ...), condition=%wide.region_47.48_spmd.clone.clone, body=%wide.region_42.47_spmd.clone.clone.sunk | while | flops 254477584 | bytes 7561892 | solution.py:346
  268.8 4.2 conditional.29
  407.6 9.1 fusion.206
  419.4 3.7 fusion.216
  427.3 123.1 %all-reduce.2 = bf16[256]{0:T(256)(128)(2,1)S(1)} all-reduce(bf16[256]{0:T(256)(128)(2,1)S(1)} %dynamic-update-slice), channel_id=2, replica_groups=mesh['seq'=16,'head'=8] {'seq'}, use_global_device_ids=true, to_apply=%add.2 | all-reduce | flops 256 | bytes 1024
  551.0 2.2 copy.120
  554.8 13.3 %reduce-scatter.3.cloned.1.call-done = bf16[512,128]{1,0:T(8,128)(2,1)} async-done(((bf16[8192,128]{1,0:T(8,128)(2,1)}), bf16[512,128]{1,0:T(8,128)(2,1)}) %reduce-scatter.3.cloned.1.call-update) | async-done | bytes 131088 | tf_op jit(solution)/shard_map/reduce_scatter | solution.py:353
  568.2 77.8 %reduce-scatter.5.cloned.1.call-done = bf16[512,128]{1,0:T(8,128)(2,1)} async-done(((bf16[8192,128]{1,0:T(8,128)(2,1)}), bf16[512,128]{1,0:T(8,128)(2,1)}) %reduce-scatter.5.cloned.1.call-update) | async-done | bytes 131088 | tf_op jit(solution)/shard_map/reduce_scatter | solution.py:356
  646.0 73.6 %all-gather.14.cloned.1.call-done = bf16[256,128,128]{2,1,0:T(8,128)(2,1)} async-done(((bf16[16,128,128]{2,1,0:T(8,128)(2,1)}), bf16[256,128,128]{2,1,0:T(8,128)(2,1)}) %all-gather.14.cloned.1.call-update) | async-done | bytes 8388624 | tf_op jit(solution)/shard_map/all_gather | solution.py:19
  719.7 89.7 %while.161 = (s32[]{:T(128)}, f32[1,16,128,128]{3,2,1,0:T(8,128)S(1)}, f32[4,128,128,1,16]{2,4,3,1,0:T(8,128)}, f32[4,128,128,1,1]{1,2,4,3,0:T(8,128)}, bf16[4,1...) while((s32[]{:T(128)}, ...), condition=%wide.region_9.10_spmd.clone, body=%wide.region_7.9_spmd.clone.sunk | while | flops 96473088 | bytes 11889233 | solution.py:77
  723.5 1.5 fusion.324
  725.0 1.8 bitcast_dynamic-update-slice_fusion.8
  732.6 1.5 copy.224
  736.1 1.3 exponential_dynamic-update-slice_fusion.3
  737.5 2.0 fusion.321
  745.9 1.5 fusion.324
  747.5 1.8 bitcast_dynamic-update-slice_fusion.8
  755.0 1.5 copy.224
  758.6 1.3 exponential_dynamic-update-slice_fusion.3
  759.9 2.0 fusion.321
  768.4 1.5 fusion.324
  769.9 1.8 bitcast_dynamic-update-slice_fusion.8
  777.5 1.5 copy.224
  781.0 1.3 exponential_dynamic-update-slice_fusion.3
  782.3 2.0 fusion.321
  790.7 1.5 fusion.324
  792.3 1.8 bitcast_dynamic-update-slice_fusion.8
  799.9 1.5 copy.224
  804.7 2.1 fusion.321
  811.8 29.8 %while.159 = (s32[]{:T(128)}, f32[1,16,128,128]{3,2,1,0:T(8,128)S(1)}, s32[]{:T(128)}, bf16[16,1,16]{2,1,0:T(2,128)(2,1)}, bf16[16,1,16,128,128]{4,3,2,1,0:T(8,1...) while((s32[]{:T(128)}, f32[1,16,128,128]{3,2,1,0:T(8,128)S(1)}, s32[]{:T(128)}, ...), condition=%wide.region_4.5_spmd, body=%wide.region_3.4_spmd.sunk | while | flops 786454 | bytes 2621747 | solution.py:34
  841.9 1.6 broadcast.582.clone
  844.9 104.5 %while.162 = (s32[]{:T(128)}, f32[1,16,128,128]{2,3,1,0:T(8,128)S(1)}, bf16[4,128,1,16,128]{4,3,1,0,2:T(8,128)(2,1)}, f32[4,128,1,16]{3,2,1,0:T(1,128)S(1)}, f32...) while((s32[]{:T(128)}, ...), condition=%wide.region_21.22_spmd.clone, body=%wide.region_10.21_spmd.clone.sunk | while | flops 460582912 | bytes 29304276 | solution.py:77
  848.7 1.9 fusion.337
  852.2 1.4 multiply_reduce_fusion.9
  854.6 1.6 multiply_reduce_fusion.10
  856.3 2.3 constant_dynamic-slice_fusion.46
  858.6 1.6 copy.236
  864.1 1.4 constant_dynamic-slice_fusion.39
  874.8 1.9 fusion.337
  878.3 1.4 multiply_reduce_fusion.9
  880.7 1.6 multiply_reduce_fusion.10
  882.4 2.3 constant_dynamic-slice_fusion.46
  884.7 1.6 copy.236
  890.2 1.4 constant_dynamic-slice_fusion.39
  901.0 1.9 fusion.337
  904.5 1.4 multiply_reduce_fusion.9
  906.8 1.6 multiply_reduce_fusion.10
  908.6 2.3 constant_dynamic-slice_fusion.46
  910.9 1.6 copy.236
  916.3 1.4 constant_dynamic-slice_fusion.39
  927.1 1.9 fusion.337
  930.6 1.4 multiply_reduce_fusion.9
  933.0 1.6 multiply_reduce_fusion.10
  934.7 2.3 constant_dynamic-slice_fusion.46
  937.0 1.6 copy.236
  942.5 1.4 constant_dynamic-slice_fusion.39
  950.2 1.6 copy.412
  951.7 1.6 copy.413
  (1214 shorter events, 383.1 us)
Async XLA Ops:
  7.2 50.5 %all-gather.8.cloned.1.call-start = ((), (), s32[]{:S(2)}) async-start(), calls=%async_computation.2 | async-start | bytes 2228224 | tf_op jit(solution)/shard_map/all_gather | solution.py:176
  7.9 149.1 %all-gather.10.cloned.1.call-start = ((), (), s32[]{:S(2)}) async-start(), calls=%async_computation.3 | async-start | bytes 2228224 | tf_op jit(solution)/shard_map/all_gather | solution.py:177
  8.6 559.5 %reduce-scatter.3.cloned.1.call-start = ((), (), s32[]{:S(2)}) async-start(), calls=%async_computation.4 | async-start | bytes 2228224 | tf_op jit(solution)/shard_map/reduce_scatter | solution.py:353
  157.0 102.6 %copy-start.15 = (bf16[512,1,128]{2,0,1:T(8,128)(2,1)S(1)}, bf16[512,1,128]{2,0,1:T(8,128)(2,1)}, u32[]{:S(2)}) copy-start(bf16[512,1,128]{2,0,1:T(8,128)(2,1)} %param.44) | copy-start | bytes 393220
  259.8 1.6 copy-start.20
  402.4 1.3 copy-start.6
  402.4 1.3 copy-start.7
  402.4 2.0 copy-start.18
  403.8 3.0 copy-start.2
  403.8 242.2 %reduce-scatter.5.cloned.1.call-start = ((), (), s32[]{:S(2)}) async-start(), calls=%async_computation.5 | async-start | bytes 2228224 | tf_op jit(solution)/shard_map/reduce_scatter | solution.py:356
  403.8 3.1 copy-start.5
  404.4 315.2 %all-gather.14.cloned.1.call-start = ((), (), s32[]{:S(2)}) async-start(), calls=%async_computation.7 | async-start | bytes 8912896 | tf_op jit(solution)/shard_map/all_gather | solution.py:19
  404.5 3.1 copy-start.11
  416.7 1.4 copy-start.4
  416.7 1.9 copy-start.1
  417.7 394.0 %all-gather.12.cloned.1.call-start = ((), (), s32[]{:S(2)}) async-start(), calls=%async_computation.6 | async-start | bytes 8912896 | tf_op jit(solution)/shard_map/all_gather | solution.py:19
  423.1 2.7 copy-start.21
  424.0 526.2 %all-reduce.6.cloned.1.call-start = ((), (), s32[]{:S(2)}) async-start(), calls=%async_computation.8 | async-start | bytes 524288 | tf_op jit(solution)/shard_map/psum | solution.py:361
  424.2 0.8 copy-start.9
  551.0 3.1 copy-start.8
  553.3 166.2 %copy-start.12 = (f32[4,128,1,1,128]{4,3,2,1,0:T(1,128)}, f32[4,128,1,1,128]{4,3,2,1,0:T(1,128)S(1)}, u32[]{:S(2)}) copy-start(f32[4,128,1,1,128]{4,3,2,1,0:T(1,128)S(1)} %broadcast.586) | copy-start | bytes 786436
  721.2 0.6 copy-start.16
  725.0 3.8 copy-start.13
  729.4 2.0 copy-start.14
  729.5 2.0 copy-start.19
  730.5 1.5 copy-start.17
  731.5 10.0 %copy-start.3 = (f32[512,1,128]{2,1,0:T(1,128)S(1)}, f32[512,1,128]{2,1,0:T(1,128)}, u32[]{:S(2)}) copy-start(f32[512,1,128]{2,1,0:T(1,128)} %get-tuple-element.4603) | copy-start | bytes 786436 | tf_op jit(solution)/shard_map/jvp()/while
  743.7 0.6 copy-start.16
  747.5 3.8 copy-start.13
  751.8 2.0 copy-start.14
  751.9 2.0 copy-start.19
  752.9 1.4 copy-start.17
  753.9 10.1 %copy-start.3 = (f32[512,1,128]{2,1,0:T(1,128)S(1)}, f32[512,1,128]{2,1,0:T(1,128)}, u32[]{:S(2)}) copy-start(f32[512,1,128]{2,1,0:T(1,128)} %get-tuple-element.4603) | copy-start | bytes 786436 | tf_op jit(solution)/shard_map/jvp()/while
  766.1 0.6 copy-start.16
  769.9 3.8 copy-start.13
  774.3 2.0 copy-start.14
  774.3 2.0 copy-start.19
  775.4 1.4 copy-start.17
  776.3 10.0 %copy-start.3 = (f32[512,1,128]{2,1,0:T(1,128)S(1)}, f32[512,1,128]{2,1,0:T(1,128)}, u32[]{:S(2)}) copy-start(f32[512,1,128]{2,1,0:T(1,128)} %get-tuple-element.4603) | copy-start | bytes 786436 | tf_op jit(solution)/shard_map/jvp()/while
  788.5 0.6 copy-start.16
  792.3 3.8 copy-start.13
  796.7 2.0 copy-start.14
  796.7 2.0 copy-start.19
  797.8 1.4 copy-start.17
  798.7 10.0 %copy-start.3 = (f32[512,1,128]{2,1,0:T(1,128)S(1)}, f32[512,1,128]{2,1,0:T(1,128)}, u32[]{:S(2)}) copy-start(f32[512,1,128]{2,1,0:T(1,128)} %get-tuple-element.4603) | copy-start | bytes 786436 | tf_op jit(solution)/shard_map/jvp()/while
  809.4 2.3 copy-start
  841.5 3.4 copy-start.10
Sparse Core Ops, SparseCore 0:
  10.1 47.4 all-gather.7
  59.8 44.5 all-gather.9
  403.9 164.2 reduce-scatter.2
  572.2 73.6 reduce-scatter.4
  647.9 71.5 all-gather.13
  721.6 70.4 all-gather.11
  794.5 57.4 all-reduce.5
where the time goes:
time: 975 us; the launch traced here: 960 us
  local copies, waits for them, and re-layouts  243 us (25%)
  waiting for transfers between devices  212 us (22%)
  loops' own time  166 us (17%)
  blocking collectives  123 us (13%)
  matrix products  114 us (12%)
  other arithmetic  85.4 us (9%)
  between operations  16.5 us (2%)
    unnamed x1, blocking collectives  123 us
    reduce_scatter x1, waiting for transfers between devices, per_device(): lax.psum_scatter(grad_state[3].astype(jnp.bfloat16), 'seq', scatter_dimen...  77.8 us
    all_gather x2, waiting for transfers between devices, carried_in(): lax.all_gather(a.astype(kind), axis)  73.6 us
    dynamic_slice x72, local copies, waits for them, and re-layouts, run_blocks(): lax.scan(block_advance, state_start, (blocked(x_seq), blocked(a_seq), blo...  60.9 us
    another operation x1, loops' own time, per_device(): grad_state = lax.fori_loop(0, seq_count, grad_turn, grad_start)  53.6 us
    another operation x1, loops' own time, per_device(): lax.fori_loop(0, seq_count, stat_turn, ((stat_start, sum_start), (stat_st...  53 us
    another operation x1, loops' own time, per_device(): out_sums = lax.fori_loop(0, seq_count, out_turn, (out_zero, out_zero))  52.9 us
    all_gather x1, waiting for transfers between devices, per_device(): lax.all_gather(key_rows, 'seq', axis=0, tiled=True)  45.4 us
  transfers between devices with their start and end apart: 7, of which 4 were waited for; matrix products, arithmetic and copies ran while one was open for 31% of the time, Pallas kernels for 0%

commit v1 on v0

v1 whole, which is shorter than its diff:
```python
import functools

import jax
import jax.numpy as jnp
from jax import lax
from jax.experimental import pallas as pl
from jax.experimental.pallas import tpu as pltpu
from jax.sharding import PartitionSpec as P

BLOCK = 128
BF = jnp.bfloat16
F32 = jnp.float32
HIGHEST = lax.Precision.HIGHEST
NEG = -1e30
LOG2E = 1.4426950408889634
STATE_ROWS = 256
TOTAL_ROWS = 16


def dot(a, b, ca, cb, precision=None):
    return lax.dot_general(
        a, b, (((ca,), (cb,)), ((), ())), precision=precision, preferred_element_type=F32
    )


def iota(shape, dim):
    return lax.broadcasted_iota(jnp.int32, shape, dim)


def pieces(v, count):
    out = []
    for _ in range(count):
        p = v.astype(BF)
        out.append(p)
        v = v - p.astype(F32)
    return out


def ssd_send_kernel(
    info, x_ref, y_ref, at_ref, b_ref, c_ref, k_ref, v_ref,
    send_ref, xh_ref, yh_ref, cum_ref, xs, ys, st, pu, run,
):
    k = pl.program_id(0)
    heads = x_ref.shape[1]

    @pl.when(k == 0)
    def _():
        st[...] = jnp.zeros_like(st)
        pu[...] = jnp.zeros_like(pu)
        run[...] = jnp.zeros_like(run)

    upto = (iota((BLOCK, BLOCK), 0) <= iota((BLOCK, BLOCK), 1)).astype(F32)
    cum = dot(at_ref[...], upto, 1, 0, HIGHEST)
    cum_ref[...] = cum
    total = cum[:, BLOCK - 1 :]
    grow = jnp.exp(cum)
    tail = jnp.exp(total - cum)
    keep = jnp.exp(total)
    before = run[:, :1]
    early = jnp.exp(before)
    run[...] = jnp.broadcast_to(before + total, run.shape)
    bt = b_ref[...].T
    ct = c_ref[...].T
    xs[...] = x_ref[...].astype(F32).reshape(xs.shape)
    ys[...] = y_ref[...].astype(F32).reshape(ys.shape)
    for h in range(heads):
        x = xs[pl.ds(h, BLOCK, stride=heads), :].astype(BF)
        y = ys[pl.ds(h, BLOCK, stride=heads), :].astype(BF)
        xh_ref[h] = x
        yh_ref[h] = y
        bs = (bt * tail[h : h + 1, :]).astype(BF)
        cs = (ct * grow[h : h + 1, :]).astype(BF)
        st[h] = keep[h : h + 1, :] * st[h] + dot(bs, x, 1, 0)
        pu[h] = pu[h] + early[h : h + 1, :] * dot(cs, y, 1, 0).astype(BF).astype(F32)

    @pl.when(k == pl.num_programs(0) - 1)
    def _():
        at = pl.multiple_of(info[1] * 32, 32)
        half = k_ref.shape[0] // 2
        subs = [r[pl.ds(at + o, 32), :] for r in (k_ref, v_ref) for o in (0, half)]
        three = pieces(run[...], 3)
        for h in range(heads):
            send_ref[h, 0:128, :] = st[h].astype(BF)
            send_ref[h, 128:256, :] = pu[h].astype(BF)
            for i, s in enumerate(subs):
                send_ref[h, 256 + 32 * i : 288 + 32 * i, :] = s
            rows = iota((TOTAL_ROWS, 128), 0)
            t = jnp.zeros((TOTAL_ROWS, 128), F32)
            for i, p in enumerate(three):
                t = jnp.where(rows == i, p[h : h + 1, :].astype(F32), t)
            send_ref[h, 384:400, :] = t.astype(BF)


def ssd_send(info, x, y, at, b, c, keys, values):
    tok, heads, width = x.shape
    nb = tok // BLOCK
    blk = pl.BlockSpec((BLOCK, heads, width), lambda k, i: (k, 0, 0))
    mat = pl.BlockSpec((BLOCK, 128), lambda k, i: (k, 0))
    row = pl.BlockSpec((heads, BLOCK), lambda k, i: (0, k))
    hm = pl.BlockSpec((heads, BLOCK, width), lambda k, i: (0, k, 0))
    whole = pl.BlockSpec((tok, 128), lambda k, i: (0, 0))
    rows = STATE_ROWS + 128 + TOTAL_ROWS
    return pl.pallas_call(
        ssd_send_kernel,
        grid_spec=pltpu.PrefetchScalarGridSpec(
            num_scalar_prefetch=1,
            grid=(nb,),
            in_specs=[blk, blk, row, mat, mat, whole, whole],
            out_specs=[pl.BlockSpec((heads, rows, 128), lambda k, i: (0, 0, 0)), hm, hm, row],
            scratch_shapes=[
                pltpu.VMEM((BLOCK * heads, width), F32),
                pltpu.VMEM((BLOCK * heads, width), F32),
                pltpu.VMEM((heads, 128, 128), F32),
                pltpu.VMEM((heads, 128, 128), F32),
                pltpu.VMEM((heads, 128), F32),
            ],
        ),
        out_shape=[
            jax.ShapeDtypeStruct((heads, rows, 128), BF),
            jax.ShapeDtypeStruct((heads, tok, width), BF),
            jax.ShapeDtypeStruct((heads, tok, width), BF),
            jax.ShapeDtypeStruct((heads, tok), F32),
        ],
        compiler_params=pltpu.CompilerParams(vmem_limit_bytes=48 << 20),
        name="ssd_send",
    )(info, x, y, at, b, c, keys, values)


def sort_keys(info, recv, ks, vs):
    for b in range(32):
        src = info[2 + (b if b < 16 else 31 - b)]
        o = 0 if b < 16 else 32
        ks[32 * b : 32 * b + 32, :] = recv[src, 256 + o : 288 + o, :]
        vs[32 * b : 32 * b + 32, :] = recv[src, 320 + o : 352 + o, :]


def item_at(info, i):
    first = info[0]
    n0 = (first + 4) // 4
    late = (i >= n0).astype(jnp.int32)
    g = i - late * n0
    block = jnp.where(late == 1, 31 - first, first)
    kr = iota((128, 256), 0)
    key_at = (g * 4 + kr // 32) * 256 + info[1] * 32 + kr % 32
    bias = jnp.where(key_at <= block * 256 + iota((128, 256), 1), 0.0, NEG)
    return pl.multiple_of(g * 128, 128), pl.multiple_of(late * 256, 256), bias


def attn_stat_kernel(info, recv, qd, stat, ks, vs):
    heads = qd.shape[0]
    scale = LOG2E * 128**-0.5
    sort_keys(info, recv, ks, vs)
    stat[0:heads, :] = jnp.full((heads, 512), NEG, F32)
    stat[heads:, :] = jnp.zeros((2 * heads, 512), F32)

    def item(i, carry):
        kat, rat, bias = item_at(info, i)
        kg = ks[pl.ds(kat, 128), :]
        vg = vs[pl.ds(kat, 128), :]
        for h in range(heads):
            s = dot(kg, qd[h, 0, pl.ds(rat, 256), :], 1, 1) * scale + bias
            dp = dot(vg, qd[h, 1, pl.ds(rat, 256), :], 1, 1)
            old = stat[h : h + 1, pl.ds(rat, 256)]
            top = jnp.maximum(old, jnp.max(s, axis=0, keepdims=True))
            p = jnp.exp2(s - top)
            fix = jnp.exp2(old - top)
            l = heads + h
            d = 2 * heads + h
            stat[h : h + 1, pl.ds(rat, 256)] = top
            stat[l : l + 1, pl.ds(rat, 256)] = fix * stat[
                l : l + 1, pl.ds(rat, 256)
            ] + jnp.sum(p, axis=0, keepdims=True)
            stat[d : d + 1, pl.ds(rat, 256)] = fix * stat[
                d : d + 1, pl.ds(rat, 256)
            ] + jnp.sum(p * dp, axis=0, keepdims=True)
        return carry

    lax.fori_loop(0, 9, item, 0)


VM = pl.BlockSpec(memory_space=pltpu.VMEM)
SM = pl.BlockSpec(memory_space=pltpu.SMEM)


def attn_stat(info, recv, qd):
    heads = qd.shape[0]
    return pl.pallas_call(
        attn_stat_kernel,
        in_specs=[SM, VM, VM],
        out_specs=VM,
        out_shape=jax.ShapeDtypeStruct((3 * heads, 512), F32),
        scratch_shapes=[pltpu.VMEM((1024, 128), BF), pltpu.VMEM((1024, 128), BF)],
        compiler_params=pltpu.CompilerParams(vmem_limit_bytes=48 << 20),
        name="attn_stat",
    )(info, recv, qd)


def attn_grad_kernel(info, recv, qd, stats, send, dqt, ks, vs, dk, dv, lse, delta, dqs):
    heads = qd.shape[0]
    scale = 128**-0.5
    sort_keys(info, recv, ks, vs)
    top = stats[0, 0:heads, :]
    for j in range(1, stats.shape[0]):
        top = jnp.maximum(top, stats[j, 0:heads, :])
    total = jnp.zeros_like(top)
    dsum = jnp.zeros_like(top)
    for j in range(stats.shape[0]):
        f = jnp.exp2(stats[j, 0:heads, :] - top)
        total = total + f * stats[j, heads : 2 * heads, :]
        dsum = dsum + f * stats[j, 2 * heads :, :]
    lse[...] = top + jnp.log2(total)
    delta[...] = dsum / total
    dk[...] = jnp.zeros_like(dk)
    dv[...] = jnp.zeros_like(dv)
    dqs[...] = jnp.zeros_like(dqs)

    def item(i, carry):
        kat, rat, bias = item_at(info, i)
        kg = ks[pl.ds(kat, 128), :]
        vg = vs[pl.ds(kat, 128), :]
        kt = kg.astype(F32).T.astype(BF)
        dkg = dk[pl.ds(kat, 128), :]
        dvg = dv[pl.ds(kat, 128), :]
        for h in range(heads):
            q = qd[h, 0, pl.ds(rat, 256), :]
            do = qd[h, 1, pl.ds(rat, 256), :]
            s = dot(kg, q, 1, 1) * (scale * LOG2E) + bias
            dp = dot(vg, do, 1, 1)
            p = jnp.exp2(s - lse[h : h + 1, pl.ds(rat, 256)])
            ds = (p * (dp - delta[h : h + 1, pl.ds(rat, 256)])).astype(BF)
            dvg = dvg + dot(p.astype(BF), do, 1, 0)
            dkg = dkg + dot(ds, q, 1, 0)
            dqs[h, :, pl.ds(rat, 256)] += dot(kt, ds, 1, 0)
        dk[pl.ds(kat, 128), :] = dkg
        dv[pl.ds(kat, 128), :] = dvg
        return carry

    lax.fori_loop(0, 9, item, 0)
    dqt[...] = (dqs[...] * scale).astype(BF)
    for e in range(16):
        b = info[18 + e]
        for j, (r, f) in enumerate(((dk, scale), (dv, 1.0))):
            lo = r[pl.ds(pl.multiple_of(b * 32, 32), 32), :]
            hi = r[pl.ds(pl.multiple_of((31 - b) * 32, 32), 32), :]
            send[e, 256 + 64 * j : 288 + 64 * j, :] = (lo * f).astype(BF)
            send[e, 288 + 64 * j : 320 + 64 * j, :] = (hi * f).astype(BF)
    n = recv.shape[0]
    state = jnp.zeros((128, 128), F32)
    for e in range(n):
        send[e, 0:128, :] = state.astype(BF)
        if e < n - 1:
            t = recv[e, 384:400, :].astype(F32)
            keep = jnp.exp(t[0:1] + t[1:2] + t[2:3])
            state = keep * state + recv[e, 0:128, :].astype(F32)
    pull = jnp.zeros((128, 128), F32)
    for e in reversed(range(n)):
        send[e, 128:256, :] = pull.astype(BF)
        if e > 0:
            t = recv[e, 384:400, :].astype(F32)
            keep = jnp.exp(t[0:1] + t[1:2] + t[2:3])
            pull = keep * pull + recv[e, 128:256, :].astype(F32)


def attn_grad(info, recv, qd, stats):
    heads = qd.shape[0]
    n = recv.shape[0]
    return pl.pallas_call(
        attn_grad_kernel,
        in_specs=[SM, VM, VM, VM],
        out_specs=[VM, VM],
        out_shape=[
            jax.ShapeDtypeStruct((n, 384, 128), BF),
            jax.ShapeDtypeStruct((heads, 128, 512), BF),
        ],
        scratch_shapes=[
            pltpu.VMEM((1024, 128), BF),
            pltpu.VMEM((1024, 128), BF),
            pltpu.VMEM((1024, 128), F32),
            pltpu.VMEM((1024, 128), F32),
            pltpu.VMEM((heads, 512), F32),
            pltpu.VMEM((heads, 512), F32),
            pltpu.VMEM((heads, 128, 512), F32),
        ],
        compiler_params=pltpu.CompilerParams(vmem_limit_bytes=48 << 20),
        name="attn_grad",
    )(info, recv, qd, stats)


def ssd_grad_kernel(
    xh, yh, states, cum, b_ref, c_ref,
    dx_ref, da_ref, db_ref, dc_ref,
    g_s, dg_s, dct, dbt, bt_s, ct_s, colp, dcol, drow, dxs,
):
    h = pl.program_id(0)
    heads = pl.num_programs(0)
    nb = xh.shape[1] // BLOCK
    rows = iota((BLOCK, BLOCK), 0)
    lanes = iota((BLOCK, BLOCK), 1)

    @pl.when(h == 0)
    def _():
        dg_s[...] = jnp.zeros_like(dg_s)
        dct[...] = jnp.zeros_like(dct)
        dbt[...] = jnp.zeros_like(dbt)
        dcol[...] = jnp.zeros_like(dcol)
        drow[...] = jnp.zeros_like(drow)
        for k in range(nb):
            sl = slice(k * BLOCK, (k + 1) * BLOCK)
            b = b_ref[sl, :]
            c = c_ref[sl, :]
            g_s[k] = jnp.where(rows <= lanes, dot(b, c, 1, 1, HIGHEST), 0.0)
            bt_s[k] = b.T
            ct_s[k] = c.T
            cm = cum[:, sl]
            tl = jnp.exp(cm[:, BLOCK - 1 :] - cm)
            parts = [p.astype(F32) for p in pieces(cm, 3) + pieces(tl, 2)]
            parts.append(jnp.zeros((BLOCK - 5 * heads_of(cum), BLOCK), F32))
            colp[k] = jnp.concatenate(parts, axis=0).T.astype(BF)

    nh = heads_of(cum)
    pr = iota((BLOCK, 2 * BLOCK), 0)
    pc = iota((BLOCK, 2 * BLOCK), 1)
    mine = (pr % nh) == h
    left = jnp.logical_and(pr < 3 * nh, pc < BLOCK)
    right = jnp.logical_and(jnp.logical_and(pr >= 3 * nh, pr < 5 * nh), pc >= BLOCK)
    pick = jnp.where(jnp.logical_and(mine, jnp.logical_or(left, right)), 1.0, 0.0).astype(BF)

    crow = cum[pl.ds(h, 1), :]
    x = [xh[0, k * BLOCK : (k + 1) * BLOCK, :] for k in range(nb)]
    y = [yh[0, k * BLOCK : (k + 1) * BLOCK, :] for k in range(nb)]
    c = [crow[:, k * BLOCK : (k + 1) * BLOCK] for k in range(nb)]
    total = [v[:, BLOCK - 1 :] for v in c]
    keep = [jnp.exp(t) for t in total]
    tail = [jnp.exp(t - v) for t, v in zip(total, c)]
    grow = [jnp.exp(v) for v in c]
    state = [states[0, 0:128, :].astype(F32)]
    for k in range(nb - 1):
        bs = (bt_s[k] * tail[k]).astype(BF)
        state.append(keep[k] * state[k] + dot(bs, x[k], 1, 0))
    pull = states[0, 128:256, :].astype(F32)
    for k in reversed(range(nb)):
        cols = dot(colp[k], pick, 1, 0)
        decay = jnp.exp(jnp.minimum(c[k] - cols[:, :BLOCK], 0.0))
        w = g_s[k] * decay
        dw = dot(x[k], y[k], 1, 1)
        t = dw * decay
        dg_s[k] += t
        z = t * g_s[k]
        sb = state[k].astype(BF)
        pb = pull.astype(BF)
        bs = (b_ref[k * BLOCK : (k + 1) * BLOCK, :] * cols[:, BLOCK:]).astype(BF)
        dx = dot(w.astype(BF), y[k], 1, 0) + dot(bs, pb, 1, 0)
        dxs[pl.ds(k * BLOCK * heads + h, BLOCK, stride=nh), :] = dx
        dcs = dot(sb, y[k], 1, 1) * grow[k]
        dct[k] += dcs
        q = dcs * ct_s[k]
        dbs = dot(pb, x[k], 1, 1) * tail[k]
        dbt[k] += dbs
        v = dbs * bt_s[k]
        vs = jnp.sum(v, axis=0, keepdims=True)
        line = jnp.sum(z + q, axis=0, keepdims=True) - vs
        cross = keep[k] * jnp.sum(state[k] * pull, axis=0, keepdims=True)
        last = jnp.sum(vs + cross, axis=1, keepdims=True)
        line = jnp.where(iota((1, BLOCK), 1) == BLOCK - 1, line + last, line)
        at = slice(k * BLOCK, (k + 1) * BLOCK)
        drow[:, at] = jnp.where(iota((nh, BLOCK), 0) == h, line, drow[:, at])
        zc = jnp.sum(z, axis=1, keepdims=True)
        dcol[k] = jnp.where(lanes == h, zc, dcol[k])
        if k > 0:
            cs = (ct_s[k] * grow[k]).astype(BF)
            pull = keep[k] * pull + dot(cs, y[k], 1, 0).astype(BF).astype(F32)

    @pl.when(h == heads - 1)
    def _():
        late = (rows <= lanes).astype(F32)
        for k in range(nb):
            sl = slice(k * BLOCK, (k + 1) * BLOCK)
            dg = jnp.where(rows <= lanes, dg_s[k], 0.0)
            db_ref[sl, :] = dbt[k].T + dot(dg, c_ref[sl, :], 1, 0, HIGHEST)
            dc_ref[sl, :] = dct[k].T + dot(dg.T, b_ref[sl, :], 1, 0, HIGHEST)
            line = jnp.concatenate(
                [drow[:, sl], jnp.zeros((BLOCK - nh, BLOCK), F32)], axis=0
            ).T - dcol[k]
            da_ref[sl, :] = dot(late, line, 1, 0, HIGHEST)[:, :nh]
            dx_ref[sl] = (
                dxs[k * BLOCK * nh : (k + 1) * BLOCK * nh, :]
                .reshape(BLOCK, nh, 128)
                .astype(BF)
            )


def heads_of(cum):
    return cum.shape[0]


def ssd_grad(xh, yh, states, cum, b, c):
    heads, tok, width = xh.shape
    nb = tok // BLOCK
    rows = states.shape[1]
    per = pl.BlockSpec((1, tok, width), lambda h: (h, 0, 0))
    whole = lambda *s: pl.BlockSpec(s, lambda h: (0,) * len(s))
    sq = pltpu.VMEM((nb, 128, 128), F32)
    return pl.pallas_call(
        ssd_grad_kernel,
        grid=(heads,),
        in_specs=[
            per,
            per,
            pl.BlockSpec((1, rows, 128), lambda h: (h, 0, 0)),
            whole(heads, tok),
            whole(tok, 128),
            whole(tok, 128),
        ],
        out_specs=[
            whole(tok, heads, width),
            whole(tok, heads),
            whole(tok, 128),
            whole(tok, 128),
        ],
        out_shape=[
            jax.ShapeDtypeStruct((tok, heads, width), BF),
            jax.ShapeDtypeStruct((tok, heads), F32),
            jax.ShapeDtypeStruct((tok, 128), F32),
            jax.ShapeDtypeStruct((tok, 128), F32),
        ],
        scratch_shapes=[
            sq, sq, sq, sq, sq, sq,
            pltpu.VMEM((nb, 128, 128), BF),
            sq,
            pltpu.VMEM((heads, tok), F32),
            pltpu.VMEM((tok * heads, width), F32),
        ],
        compiler_params=pltpu.CompilerParams(vmem_limit_bytes=48 << 20),
        name="ssd_grad",
    )(xh, yh, states, cum, b, c)


def per_device(
    ssd_input, log_decay, input_map, output_map, ssd_cotangent,
    queries, key_rows, value_rows, attn_cotangent, pair_order,
):
    tok, heads, width = ssd_input.shape
    b = input_map.reshape(tok, 128)
    c = output_map.reshape(tok, 128)
    own = lax.axis_index("seq")
    place = lax.axis_index("head")
    inverse = jnp.sum(
        jnp.where(pair_order[None, :] == jnp.arange(16)[:, None], jnp.arange(16)[None, :], 0),
        axis=1,
    )
    info = jnp.concatenate(
        [
            jnp.stack([pair_order[own], place.astype(jnp.int32)]),
            inverse.astype(jnp.int32),
            pair_order,
        ]
    )
    qd = lax.all_gather(
        jnp.stack([queries.reshape(tok, 128), attn_cotangent.reshape(tok, 128)]), "head"
    )
    send, xh, yh, cum = ssd_send(
        info, ssd_input, ssd_cotangent, log_decay.T, b, c, key_rows, value_rows
    )
    recv = lax.all_to_all(send, "seq", 0, 0)
    stats = lax.all_gather(attn_stat(info, recv, qd), "head")
    back, dqt = attn_grad(info, recv, qd, stats)
    dq = lax.psum_scatter(dqt, "head", scatter_dimension=0)
    states = lax.all_to_all(back, "seq", 0, 0)
    dkv = jnp.sum(states[:, 256:, :].astype(F32), axis=0).astype(BF)
    dkv = lax.all_gather(dkv, "head").reshape(8, 2, 2, 32, 128).transpose(1, 2, 0, 3, 4)
    dx, da, db, dc = ssd_grad(xh, yh, states, cum, b, c)
    return (
        dx,
        da,
        db.reshape(tok, 1, 128),
        dc.reshape(tok, 1, 128),
        dq.T.reshape(tok, 1, 128),
        dkv[0].reshape(tok, 128),
        dkv[1].reshape(tok, 128),
    )


def solution(mesh):
    tok = P("seq", "head", None)
    return jax.shard_map(
        per_device,
        mesh=mesh,
        in_specs=(
            tok, P("seq", "head"), tok, tok, tok, tok,
            P("seq", None), P("seq", None), tok, P(),
        ),
        out_specs=(tok, P("seq", "head"), tok, tok, tok, P("seq", None), P("seq", None)),
        check_vma=False,
    )
```

time: 975 us -> 171 us (0.18); the launches traced: 960 us -> 170 us
  local copies, waits for them, and re-layouts: 243 us -> 13.3 us
  waiting for transfers between devices: 212 us -> 0.04 us
  loops' own time: 166 us -> 0 us
  matrix products: 114 us -> 0 us
  other arithmetic: 85.4 us -> 3.92 us
  Pallas kernels: 0 us -> 53.5 us
  blocking collectives: 123 us -> 85.4 us
    another operation x103 -> x0, loops' own time: 166 us -> none  [the longest x1 53.6 us: per_device(): grad_state = lax.fori_loop(0, seq_count, grad_turn, grad_start)]
    dynamic_slice x185 -> x1, local copies, waits for them, and re-layouts: 166 us -> 1.24 us  [per_device(): pair_order[own]]
    unnamed x1 -> x0, blocking collectives: 123 us -> none
    all_gather x4 -> x1, waiting for transfers between devices: 119 us -> 0.01 us  [per_device(): lax.all_gather(jnp.stack([queries.reshape(tok, 128), attn_cotangent.resha...]
    dot_general x275 -> x0, matrix products: 114 us -> none  [the longest x66 16.4 us: tile_scores(): jnp.einsum('hqd,kd->hqk', query_part, key_part, preferred_element_type=jn...]
    reduce_scatter x2 -> x1, waiting for transfers between devices: 91.1 us -> 0.01 us  [per_device(): dq = lax.psum_scatter(dqt, 'head', scatter_dimension=0)]
    all_to_all x0 -> x2, blocking collectives: none -> 56 us  [the longest x1 30.9 us: per_device(): recv = lax.all_to_all(send, 'seq', 0, 0)]
    pallas_call x0 -> x4, Pallas kernels: none -> 53.5 us  [the longest x1 21.1 us: ssd_grad(): pl.pallas_call(ssd_grad_kernel, grid=(heads,), in_specs=[per, per, pl.Blo...]
  transfers between devices with their start and end apart: 7 -> 2, of which waited for: 4 -> 0; matrix products, arithmetic and copies ran while one was open for 31% -> 3% of each run, Pallas kernels for 0% -> 18%
where the time goes in v1:
time: 171 us; the launch traced here: 170 us
  blocking collectives  85.4 us (50%)
  Pallas kernels  53.5 us (31%)
  between operations  14.1 us (8%)
  local copies, waits for them, and re-layouts  13.3 us (8%)
  other arithmetic  3.92 us (2%)
    all_to_all x1, blocking collectives, per_device(): recv = lax.all_to_all(send, 'seq', 0, 0)  30.9 us
    all_to_all x1, blocking collectives, per_device(): states = lax.all_to_all(back, 'seq', 0, 0)  25.1 us
    pallas_call x1, Pallas kernels, ssd_grad(): pl.pallas_call(ssd_grad_kernel, grid=(heads,), in_specs=[per, per, pl.Blo...  21.1 us
    pallas_call x1, Pallas kernels, attn_grad(): pl.pallas_call(attn_grad_kernel, in_specs=[SM, VM, VM, VM], out_specs=[VM...  17.9 us
    all_gather x1, blocking collectives, per_device(): stats = lax.all_gather(attn_stat(info, recv, qd), 'head')  15.1 us
    all_gather x1, blocking collectives, per_device(): lax.all_gather(dkv, 'head').reshape(8, 2, 2, 32, 128)  14.2 us
    unnamed x24, local copies, waits for them, and re-layouts  10.7 us
    pallas_call x1, Pallas kernels, ssd_send(): pl.pallas_call(ssd_send_kernel, grid_spec=pltpu.PrefetchScalarGridSpec(nu...  8.71 us
  transfers between devices with their start and end apart: 2, of which 0 were waited for; matrix products, arithmetic and copies ran while one was open for 3% of the time, Pallas kernels for 18%

profile of v1, /device:TPU:1, one launch (start us, length us, event | category | flops | bytes accessed | tf_op | source)
XLA Modules:
  0.0 170.3 jit_solution(2648361279196854964)
XLA Ops:
  7.2 0.0 all-gather.5.cloned.1.call-start
  7.2 1.7 pad_maximum_fusion
  8.9 0.0 all-gather.5.cloned.1.call-update
  8.9 0.0 reduce-scatter.2.cloned.1.call-start
  9.0 1.2 dynamic_slice.3
  10.2 0.8 select_reduce_fusion
  11.0 1.4 pad_add_fusion.info
  12.4 0.0 copy-start.4
  12.4 0.9 copy-done.4
  13.3 0.0 copy-start.6
  13.3 0.9 copy-done.6
  14.3 0.0 copy-start.8
  14.3 0.9 copy-done.8
  15.2 0.0 copy-start.9
  15.2 0.9 copy-done.9
  16.1 0.0 copy-start.10
  16.1 0.8 copy-done.10
  16.9 8.7 %ssd_send.1 = (bf16[16,400,128]{2,1,0:T(8,128)(2,1)S(1)}, bf16[16,512,128]{2,1,0:T(8,128)(2,1)S(1)}, bf16[16,512,128]{2,1,0:T(8,128)(2,1)}, f32[16,512]{1,0:T(8,128)S(1)}) custom-call(s32[34]{0:T(128)S(1)} %pad_add_fusion.info, bf16[512,16,128]{2,1,0:T(8,128)(2,1)} %x_ref.1, bf16[512,16,128]{2,1,0:T(8,128)(2,1)} %y_ref.1, f32[16,512]{1,0:T(8,128)S(1)} %bitcast.31, ...), custom_call_target="tpu_custom_call" | custom-call | tf_op jit(solution)/shard_map/ssd_send/pallas_call | solution.py:103
  25.6 0.0 copy-start.1
  25.6 1.3 copy-done.1
  26.9 30.9 %all_to_all.10.recv = bf16[16,400,128]{2,1,0:T(8,128)(2,1)S(1)} all-to-all(bf16[16,400,128]{2,1,0:T(8,128)(2,1)S(1)} %get-tuple-element.19), channel_id=1, replica_groups=mesh['seq'=16,'head'=8] {'seq'}, dimensions={0} | all-to-all | bytes 3276800 | tf_op jit(solution)/shard_map/all_to_all | solution.py:464
  57.8 0.0 all-gather.5.cloned.1.call-done
  57.8 0.0 copy-start
  57.8 1.6 copy-done
  59.4 5.8 %attn_stat.1 = f32[24,512]{1,0:T(8,128)S(1)} custom-call(s32[34]{0:T(128)S(1)} %pad_add_fusion.info, bf16[16,400,128]{2,1,0:T(8,128)(2,1)S(1)} %all_to_all.10.recv, bf16[8,2,512,128]{3,2,1,0:T(8,128)(2,1)S(1)} %bitcast.25), custom_call_target="tpu_custom_call" | custom-call | tf_op jit(solution)/shard_map/attn_stat/pallas_call | solution.py:187
  65.1 15.1 %all-gather.1 = f32[192,512]{1,0:T(8,128)S(1)} all-gather(f32[24,512]{1,0:T(8,128)S(1)} %attn_stat.1), channel_id=3, replica_groups=mesh['seq'=16,'head'=8] {'head'}, dimensions={0}, use_global_device_ids=true | all-gather | bytes 442368 | tf_op jit(solution)/shard_map/all_gather | solution.py:465
  80.3 17.9 %attn_grad.1 = (bf16[16,384,128]{2,1,0:T(8,128)(2,1)S(1)}, bf16[8,128,512]{2,1,0:T(8,128)(2,1)S(1)}) custom-call(s32[34]{0:T(128)S(1)} %pad_add_fusion.info, bf16[16,400,128]{2,1,0:T(8,128)(2,1)S(1)} %all_to_all.10.recv, bf16[8,2,512,128]{3,2,1,0:T(8,128)(2,1)} %bitcast.24, f32[8,24,512]{2,1,0:T(8,128)S(1)} %bitcast.26), custom_call_target="tpu_custom_call" | custom-call | tf_op jit(solution)/shard_map/attn_grad/pallas_call | solution.py:267
  98.1 0.0 copy-start.3
  98.1 1.0 copy-done.3
  99.1 0.0 copy-start.5
  99.1 0.0 reduce-scatter.2.cloned.1.call-update
  99.1 0.0 copy-start.2
  99.1 0.0 copy-start.7
  99.1 25.1 %all_to_all.11.states = bf16[16,384,128]{2,1,0:T(8,128)(2,1)S(1)} all-to-all(bf16[16,384,128]{2,1,0:T(8,128)(2,1)S(1)} %get-tuple-element.20), channel_id=1, replica_groups=mesh['seq'=16,'head'=8] {'seq'}, dimensions={0} | all-to-all | bytes 3145728 | tf_op jit(solution)/shard_map/all_to_all | solution.py:468
  124.3 0.0 copy-done.5
  124.3 0.0 copy-done.2
  124.3 0.0 copy-done.7
  124.3 21.1 %ssd_grad.1 = (bf16[512,16,128]{2,1,0:T(8,128)(2,1)}, f32[512,16]{1,0:T(8,128)S(1)}, f32[512,128]{1,0:T(8,128)}, f32[512,128]{1,0:T(8,128)}) custom-call(bf16[16,512,128]{2,1,0:T(8,128)(2,1)S(1)} %copy-done.2, bf16[16,512,128]{2,1,0:T(8,128)(2,1)} %get-tuple-element.18.yh, bf16[16,384,128]{2,1,0:T(8,128)(2,1)S(1)} %all_to_all.11.states, ...), custom_call_target="tpu_custom_call" | custom-call | tf_op jit(solution)/shard_map/ssd_grad/pallas_call | solution.py:403
  145.4 0.7 copy.39
  146.1 0.1 slice_reduce_fusion
  146.2 14.2 %all-gather.2 = bf16[1024,128]{1,0:T(8,128)(2,1)S(1)} all-gather(bf16[128,128]{1,0:T(8,128)(2,1)S(1)} %slice_reduce_fusion), channel_id=4, replica_groups=mesh['seq'=16,'head'=8] {'head'}, dimensions={0}, use_global_device_ids=true | all-gather | bytes 294912 | tf_op jit(solution)/shard_map/all_gather | solution.py:470
  160.5 0.7 copy.38
  161.2 0.7 copy.37
  161.8 0.0 reduce-scatter.2.cloned.1.call-done
  161.8 1.7 copy.42
  (1 shorter events, 0.0 us)
Async XLA Ops:
  7.2 50.6 %all-gather.5.cloned.1.call-start = ((), (), s32[]{:S(2)}) async-start(), calls=%async_computation.4 | async-start | bytes 2359296 | tf_op jit(solution)/shard_map/all_gather | solution.py:458
  8.9 152.9 %reduce-scatter.2.cloned.1.call-start = ((), (), s32[]{:S(2)}) async-start(), calls=%async_computation.3 | async-start | bytes 1179648 | tf_op jit(solution)/shard_map/reduce_scatter | solution.py:467
  12.4 1.0 copy-start.4
  13.3 0.9 copy-start.6
  14.3 0.9 copy-start.8
  15.2 0.9 copy-start.9
  16.1 0.8 copy-start.10
  25.6 1.3 copy-start.1
  57.8 1.6 copy-start
  98.1 1.0 copy-start.3
  99.1 25.2 %copy-start.5 = (f32[512,1,128]{2,1,0:T(1,128)S(1)}, f32[512,1,128]{2,1,0:T(1,128)}, u32[]{:S(2)}) copy-start(f32[512,1,128]{2,1,0:T(1,128)} %param.12) | copy-start | bytes 786436
  99.1 25.2 %copy-start.2 = (bf16[16,512,128]{2,1,0:T(8,128)(2,1)S(1)}, bf16[16,512,128]{2,1,0:T(8,128)(2,1)}, u32[]{:S(2)}) copy-start(bf16[16,512,128]{2,1,0:T(8,128)(2,1)} %copy-done.1) | copy-start | bytes 6291460
  99.1 25.1 %copy-start.7 = (f32[512,1,128]{2,1,0:T(1,128)S(1)}, f32[512,1,128]{2,1,0:T(1,128)}, u32[]{:S(2)}) copy-start(f32[512,1,128]{2,1,0:T(1,128)} %param.13) | copy-start | bytes 786436
Sparse Core Ops, SparseCore 0:
  10.3 28.7 all-gather.4
  99.2 25.9 reduce-scatter.1

commit v2 on v1

--- a/solution.py
+++ b/solution.py
@@ -37,8 +37,8 @@
 
 
 def ssd_send_kernel(
-    info, x_ref, y_ref, at_ref, b_ref, c_ref, k_ref, v_ref,
-    send_ref, xh_ref, yh_ref, cum_ref, xs, ys, st, pu, run,
+    x_ref, y_ref, at_ref, b_ref, c_ref, k_ref, v_ref, q_ref, do_ref,
+    send_ref, xh_ref, yh_ref, cum_ref, qd_ref, xs, ys, st, pu, run,
 ):
     k = pl.program_id(0)
     heads = x_ref.shape[1]
@@ -75,7 +75,9 @@
 
     @pl.when(k == pl.num_programs(0) - 1)
     def _():
-        at = pl.multiple_of(info[1] * 32, 32)
+        qd_ref[0] = q_ref[...]
+        qd_ref[1] = do_ref[...]
+        at = pl.multiple_of(lax.axis_index("head") * 32, 32)
         half = k_ref.shape[0] // 2
         subs = [r[pl.ds(at + o, 32), :] for r in (k_ref, v_ref) for o in (0, half)]
         three = pieces(run[...], 3)
@@ -91,22 +93,28 @@
             send_ref[h, 384:400, :] = t.astype(BF)
 
 
-def ssd_send(info, x, y, at, b, c, keys, values):
+def ssd_send(x, y, at, b, c, keys, values, q, do):
     tok, heads, width = x.shape
     nb = tok // BLOCK
-    blk = pl.BlockSpec((BLOCK, heads, width), lambda k, i: (k, 0, 0))
-    mat = pl.BlockSpec((BLOCK, 128), lambda k, i: (k, 0))
-    row = pl.BlockSpec((heads, BLOCK), lambda k, i: (0, k))
-    hm = pl.BlockSpec((heads, BLOCK, width), lambda k, i: (0, k, 0))
-    whole = pl.BlockSpec((tok, 128), lambda k, i: (0, 0))
+    blk = pl.BlockSpec((BLOCK, heads, width), lambda k: (k, 0, 0))
+    mat = pl.BlockSpec((BLOCK, 128), lambda k: (k, 0))
+    row = pl.BlockSpec((heads, BLOCK), lambda k: (0, k))
+    hm = pl.BlockSpec((heads, BLOCK, width), lambda k: (0, k, 0))
+    whole = pl.BlockSpec((tok, 128), lambda k: (0, 0))
     rows = STATE_ROWS + 128 + TOTAL_ROWS
     return pl.pallas_call(
         ssd_send_kernel,
         grid_spec=pltpu.PrefetchScalarGridSpec(
-            num_scalar_prefetch=1,
+            num_scalar_prefetch=0,
             grid=(nb,),
-            in_specs=[blk, blk, row, mat, mat, whole, whole],
-            out_specs=[pl.BlockSpec((heads, rows, 128), lambda k, i: (0, 0, 0)), hm, hm, row],
+            in_specs=[blk, blk, row, mat, mat, whole, whole, whole, whole],
+            out_specs=[
+                pl.BlockSpec((heads, rows, 128), lambda k: (0, 0, 0)),
+                hm,
+                hm,
+                row,
+                pl.BlockSpec((2, tok, 128), lambda k: (0, 0, 0)),
+            ],
             scratch_shapes=[
                 pltpu.VMEM((BLOCK * heads, width), F32),
                 pltpu.VMEM((BLOCK * heads, width), F32),
@@ -120,41 +128,44 @@
             jax.ShapeDtypeStruct((heads, tok, width), BF),
             jax.ShapeDtypeStruct((heads, tok, width), BF),
             jax.ShapeDtypeStruct((heads, tok), F32),
-        ],
-        compiler_params=pltpu.CompilerParams(vmem_limit_bytes=48 << 20),
+            jax.ShapeDtypeStruct((2, tok, 128), BF),
+        ],
+        compiler_params=pltpu.CompilerParams(vmem_limit_bytes=60 << 20),
         name="ssd_send",
-    )(info, x, y, at, b, c, keys, values)
-
-
-def sort_keys(info, recv, ks, vs):
+    )(x, y, at, b, c, keys, values, q, do)
+
+
+def sort_keys(order, inverse, recv, ks, vs):
+    for e in range(16):
+        inverse[order[e]] = e
     for b in range(32):
-        src = info[2 + (b if b < 16 else 31 - b)]
+        src = inverse[b if b < 16 else 31 - b]
         o = 0 if b < 16 else 32
         ks[32 * b : 32 * b + 32, :] = recv[src, 256 + o : 288 + o, :]
         vs[32 * b : 32 * b + 32, :] = recv[src, 320 + o : 352 + o, :]
 
 
-def item_at(info, i):
-    first = info[0]
+def item_at(order, i):
+    first = order[lax.axis_index("seq")]
     n0 = (first + 4) // 4
     late = (i >= n0).astype(jnp.int32)
     g = i - late * n0
     block = jnp.where(late == 1, 31 - first, first)
     kr = iota((128, 256), 0)
-    key_at = (g * 4 + kr // 32) * 256 + info[1] * 32 + kr % 32
+    key_at = (g * 4 + kr // 32) * 256 + lax.axis_index("head") * 32 + kr % 32
     bias = jnp.where(key_at <= block * 256 + iota((128, 256), 1), 0.0, NEG)
     return pl.multiple_of(g * 128, 128), pl.multiple_of(late * 256, 256), bias
 
 
-def attn_stat_kernel(info, recv, qd, stat, ks, vs):
+def attn_stat_kernel(order, recv, qd, stat, ks, vs, inverse):
     heads = qd.shape[0]
     scale = LOG2E * 128**-0.5
-    sort_keys(info, recv, ks, vs)
+    sort_keys(order, inverse, recv, ks, vs)
     stat[0:heads, :] = jnp.full((heads, 512), NEG, F32)
     stat[heads:, :] = jnp.zeros((2 * heads, 512), F32)
 
     def item(i, carry):
-        kat, rat, bias = item_at(info, i)
+        kat, rat, bias = item_at(order, i)
         kg = ks[pl.ds(kat, 128), :]
         vg = vs[pl.ds(kat, 128), :]
         for h in range(heads):
@@ -180,25 +191,51 @@
 
 VM = pl.BlockSpec(memory_space=pltpu.VMEM)
 SM = pl.BlockSpec(memory_space=pltpu.SMEM)
-
-
-def attn_stat(info, recv, qd):
+HB = pl.BlockSpec(memory_space=pltpu.HBM)
+
+
+def attn_stat(order, recv, qd):
     heads = qd.shape[0]
     return pl.pallas_call(
         attn_stat_kernel,
         in_specs=[SM, VM, VM],
         out_specs=VM,
         out_shape=jax.ShapeDtypeStruct((3 * heads, 512), F32),
-        scratch_shapes=[pltpu.VMEM((1024, 128), BF), pltpu.VMEM((1024, 128), BF)],
-        compiler_params=pltpu.CompilerParams(vmem_limit_bytes=48 << 20),
+        scratch_shapes=[
+            pltpu.VMEM((1024, 128), BF),
+            pltpu.VMEM((1024, 128), BF),
+            pltpu.SMEM((16,), jnp.int32),
+        ],
+        compiler_params=pltpu.CompilerParams(vmem_limit_bytes=20 << 20),
         name="attn_stat",
-    )(info, recv, qd)
-
-
-def attn_grad_kernel(info, recv, qd, stats, send, dqt, ks, vs, dk, dv, lse, delta, dqs):
+    )(order, recv, qd)
+
+
+def attn_grad_kernel(
+    order, recv, qd, stats, send, dqt, ks, vs, dk, dv, lse, delta, dqs, inverse, dqo, buf, sem
+):
     heads = qd.shape[0]
     scale = 128**-0.5
-    sort_keys(info, recv, ks, vs)
+    sort_keys(order, inverse, recv, ks, vs)
+    n = recv.shape[0]
+    state = jnp.zeros((128, 128), F32)
+    for e in range(n):
+        buf[e, 0:128, :] = state.astype(BF)
+        if e < n - 1:
+            t = recv[e, 384:400, :].astype(F32)
+            keep = jnp.exp(t[0:1] + t[1:2] + t[2:3])
+            state = keep * state + recv[e, 0:128, :].astype(F32)
+    moves = [pltpu.make_async_copy(buf.at[:, 0:128], send.at[:, 0:128], sem.at[0])]
+    moves[0].start()
+    pull = jnp.zeros((128, 128), F32)
+    for e in reversed(range(n)):
+        buf[e, 128:256, :] = pull.astype(BF)
+        if e > 0:
+            t = recv[e, 384:400, :].astype(F32)
+            keep = jnp.exp(t[0:1] + t[1:2] + t[2:3])
+            pull = keep * pull + recv[e, 128:256, :].astype(F32)
+    moves.append(pltpu.make_async_copy(buf.at[:, 128:256], send.at[:, 128:256], sem.at[1]))
+    moves[1].start()
     top = stats[0, 0:heads, :]
     for j in range(1, stats.shape[0]):
         top = jnp.maximum(top, stats[j, 0:heads, :])
@@ -215,7 +252,7 @@
     dqs[...] = jnp.zeros_like(dqs)
 
     def item(i, carry):
-        kat, rat, bias = item_at(info, i)
+        kat, rat, bias = item_at(order, i)
         kg = ks[pl.ds(kat, 128), :]
         vg = vs[pl.ds(kat, 128), :]
         kt = kg.astype(F32).T.astype(BF)
@@ -236,41 +273,32 @@
         return carry
 
     lax.fori_loop(0, 9, item, 0)
-    dqt[...] = (dqs[...] * scale).astype(BF)
+    dqo[...] = (dqs[...] * scale).astype(BF)
+    moves.append(pltpu.make_async_copy(dqo, dqt, sem.at[2]))
+    moves[2].start()
     for e in range(16):
-        b = info[18 + e]
+        b = order[e]
         for j, (r, f) in enumerate(((dk, scale), (dv, 1.0))):
             lo = r[pl.ds(pl.multiple_of(b * 32, 32), 32), :]
             hi = r[pl.ds(pl.multiple_of((31 - b) * 32, 32), 32), :]
-            send[e, 256 + 64 * j : 288 + 64 * j, :] = (lo * f).astype(BF)
-            send[e, 288 + 64 * j : 320 + 64 * j, :] = (hi * f).astype(BF)
-    n = recv.shape[0]
-    state = jnp.zeros((128, 128), F32)
-    for e in range(n):
-        send[e, 0:128, :] = state.astype(BF)
-        if e < n - 1:
-            t = recv[e, 384:400, :].astype(F32)
-            keep = jnp.exp(t[0:1] + t[1:2] + t[2:3])
-            state = keep * state + recv[e, 0:128, :].astype(F32)
-    pull = jnp.zeros((128, 128), F32)
-    for e in reversed(range(n)):
-        send[e, 128:256, :] = pull.astype(BF)
-        if e > 0:
-            t = recv[e, 384:400, :].astype(F32)
-            keep = jnp.exp(t[0:1] + t[1:2] + t[2:3])
-            pull = keep * pull + recv[e, 128:256, :].astype(F32)
-
-
-def attn_grad(info, recv, qd, stats):
+            buf[e, 256 + 64 * j : 288 + 64 * j, :] = (lo * f).astype(BF)
+            buf[e, 288 + 64 * j : 320 + 64 * j, :] = (hi * f).astype(BF)
+    moves.append(pltpu.make_async_copy(buf.at[:, 256:384], send.at[:, 256:384], sem.at[3]))
+    moves[3].start()
+    for m in moves:
+        m.wait()
+
+
+def attn_grad(order, recv, qd, stats):
     heads = qd.shape[0]
     n = recv.shape[0]
     return pl.pallas_call(
         attn_grad_kernel,
         in_specs=[SM, VM, VM, VM],
-        out_specs=[VM, VM],
+        out_specs=[HB, HB],
         out_shape=[
-            jax.ShapeDtypeStruct((n, 384, 128), BF),
-            jax.ShapeDtypeStruct((heads, 128, 512), BF),
+            pltpu.HBM((n, 384, 128), BF),
+            pltpu.HBM((heads, 128, 512), BF),
         ],
         scratch_shapes=[
             pltpu.VMEM((1024, 128), BF),
@@ -280,10 +308,14 @@
             pltpu.VMEM((heads, 512), F32),
             pltpu.VMEM((heads, 512), F32),
             pltpu.VMEM((heads, 128, 512), F32),
-        ],
-        compiler_params=pltpu.CompilerParams(vmem_limit_bytes=48 << 20),
+            pltpu.SMEM((16,), jnp.int32),
+            pltpu.VMEM((heads, 128, 512), BF),
+            pltpu.VMEM((n, 384, 128), BF),
+            pltpu.SemaphoreType.DMA((4,)),
+        ],
+        compiler_params=pltpu.CompilerParams(vmem_limit_bytes=20 << 20),
         name="attn_grad",
-    )(info, recv, qd, stats)
+    )(order, recv, qd, stats)
 
 
 def ssd_grad_kernel(
@@ -372,16 +404,13 @@
 
     @pl.when(h == heads - 1)
     def _():
-        late = (rows <= lanes).astype(F32)
+        late = (rows >= lanes).astype(F32)
         for k in range(nb):
             sl = slice(k * BLOCK, (k + 1) * BLOCK)
             dg = jnp.where(rows <= lanes, dg_s[k], 0.0)
             db_ref[sl, :] = dbt[k].T + dot(dg, c_ref[sl, :], 1, 0, HIGHEST)
             dc_ref[sl, :] = dct[k].T + dot(dg.T, b_ref[sl, :], 1, 0, HIGHEST)
-            line = jnp.concatenate(
-                [drow[:, sl], jnp.zeros((BLOCK - nh, BLOCK), F32)], axis=0
-            ).T - dcol[k]
-            da_ref[sl, :] = dot(late, line, 1, 0, HIGHEST)[:, :nh]
+            da_ref[:, sl] = dot(drow[:, sl] - dcol[k].T[:nh], late, 1, 0, HIGHEST)
             dx_ref[sl] = (
                 dxs[k * BLOCK * nh : (k + 1) * BLOCK * nh, :]
                 .reshape(BLOCK, nh, 128)
@@ -413,13 +442,13 @@
         ],
         out_specs=[
             whole(tok, heads, width),
-            whole(tok, heads),
+            whole(heads, tok),
             whole(tok, 128),
             whole(tok, 128),
         ],
         out_shape=[
             jax.ShapeDtypeStruct((tok, heads, width), BF),
-            jax.ShapeDtypeStruct((tok, heads), F32),
+            jax.ShapeDtypeStruct((heads, tok), F32),
             jax.ShapeDtypeStruct((tok, 128), F32),
             jax.ShapeDtypeStruct((tok, 128), F32),
         ],
@@ -433,6 +462,26 @@
         compiler_params=pltpu.CompilerParams(vmem_limit_bytes=48 << 20),
         name="ssd_grad",
     )(xh, yh, states, cum, b, c)
+
+
+def finish_kernel(dqt, dkv, dq, dk, dv):
+    dq[...] = dqt[0].astype(F32).T.astype(BF)
+    for h in range(dkv.shape[0]):
+        for j in range(2):
+            to = slice(256 * j + 32 * h, 256 * j + 32 * h + 32)
+            dk[to, :] = dkv[h, 32 * j : 32 * j + 32, :]
+            dv[to, :] = dkv[h, 64 + 32 * j : 96 + 32 * j, :]
+
+
+def finish(dqt, dkv):
+    out = jax.ShapeDtypeStruct((512, 128), BF)
+    return pl.pallas_call(
+        finish_kernel,
+        in_specs=[VM, VM],
+        out_specs=[VM, VM, VM],
+        out_shape=[out, out, out],
+        name="finish",
+    )(dqt, dkv)
 
 
 def per_device(
@@ -442,41 +491,28 @@
     tok, heads, width = ssd_input.shape
     b = input_map.reshape(tok, 128)
     c = output_map.reshape(tok, 128)
-    own = lax.axis_index("seq")
-    place = lax.axis_index("head")
-    inverse = jnp.sum(
-        jnp.where(pair_order[None, :] == jnp.arange(16)[:, None], jnp.arange(16)[None, :], 0),
-        axis=1,
+    send, xh, yh, cum, qd = ssd_send(
+        ssd_input, ssd_cotangent, log_decay.T, b, c, key_rows, value_rows,
+        queries.reshape(tok, 128), attn_cotangent.reshape(tok, 128),
     )
-    info = jnp.concatenate(
-        [
-            jnp.stack([pair_order[own], place.astype(jnp.int32)]),
-            inverse.astype(jnp.int32),
-            pair_order,
-        ]
-    )
-    qd = lax.all_gather(
-        jnp.stack([queries.reshape(tok, 128), attn_cotangent.reshape(tok, 128)]), "head"
-    )
-    send, xh, yh, cum = ssd_send(
-        info, ssd_input, ssd_cotangent, log_decay.T, b, c, key_rows, value_rows
-    )
+    qd = lax.all_gather(qd, "head")
     recv = lax.all_to_all(send, "seq", 0, 0)
-    stats = lax.all_gather(attn_stat(info, recv, qd), "head")
-    back, dqt = attn_grad(info, recv, qd, stats)
-    dq = lax.psum_scatter(dqt, "head", scatter_dimension=0)
+    stats = lax.all_gather(attn_stat(pair_order, recv, qd), "head")
+    back, dqt = attn_grad(pair_order, recv, qd, stats)
+    dqt = lax.psum_scatter(dqt, "head", scatter_dimension=0, tiled=True)
     states = lax.all_to_all(back, "seq", 0, 0)
     dkv = jnp.sum(states[:, 256:, :].astype(F32), axis=0).astype(BF)
-    dkv = lax.all_gather(dkv, "head").reshape(8, 2, 2, 32, 128).transpose(1, 2, 0, 3, 4)
+    dkv = lax.all_gather(dkv, "head")
     dx, da, db, dc = ssd_grad(xh, yh, states, cum, b, c)
+    dq, dk, dv = finish(dqt, dkv)
     return (
         dx,
-        da,
+        da.T,
         db.reshape(tok, 1, 128),
         dc.reshape(tok, 1, 128),
-        dq.T.reshape(tok, 1, 128),
-        dkv[0].reshape(tok, 128),
-        dkv[1].reshape(tok, 128),
+        dq.reshape(tok, 1, 128),
+        dk,
+        dv,
     )
 
 

time: 171 us -> 160 us (0.936)
  local copies, waits for them, and re-layouts: 13.3 us -> 1.62 us
  other arithmetic: 3.92 us -> 0.08 us
  Pallas kernels: 53.5 us -> 56.2 us
  blocking collectives: 85.4 us -> 87.6 us
    unnamed x24 -> x12, local copies, waits for them, and re-layouts: 10.7 us -> 1.62 us
    pallas_call x1 -> x2, Pallas kernels: 17.9 us -> 19.8 us  [the longest x1 18 us: attn_grad(): pl.pallas_call(attn_grad_kernel, in_specs=[SM, VM, VM, VM], out_specs=[HB...]
  transfers between devices with their start and end apart: 2 -> 2, of which waited for: 0 -> 0; matrix products, arithmetic and copies ran while one was open for 3% -> 0% of each run, Pallas kernels for 18% -> 13%
where the time goes in v2:
time: 160 us
  blocking collectives  87.6 us (55%)
  Pallas kernels  56.2 us (35%)
  between operations  14.1 us (9%)
  local copies, waits for them, and re-layouts  1.62 us (1%)
    all_to_all x1, blocking collectives, per_device(): recv = lax.all_to_all(send, 'seq', 0, 0)  31.1 us
    all_to_all x1, blocking collectives, per_device(): states = lax.all_to_all(back, 'seq', 0, 0)  26.4 us
    pallas_call x1, Pallas kernels, ssd_grad(): pl.pallas_call(ssd_grad_kernel, grid=(heads,), in_specs=[per, per, pl.Blo...  21.1 us
    pallas_call x1, Pallas kernels, attn_grad(): pl.pallas_call(attn_grad_kernel, in_specs=[SM, VM, VM, VM], out_specs=[HB...  18 us
    all_gather x1, blocking collectives, per_device(): stats = lax.all_gather(attn_stat(pair_order, recv, qd), 'head')  15.1 us
    all_gather x1, blocking collectives, per_device(): dkv = lax.all_gather(dkv, 'head')  15 us
    pallas_call x1, Pallas kernels, ssd_send(): pl.pallas_call(ssd_send_kernel, grid_spec=pltpu.PrefetchScalarGridSpec(nu...  9.38 us
    pallas_call x1, Pallas kernels, attn_stat(): pl.pallas_call(attn_stat_kernel, in_specs=[SM, VM, VM], out_specs=VM, out...  5.89 us
  transfers between devices with their start and end apart: 2, of which 0 were waited for; matrix products, arithmetic and copies ran while one was open for 0% of the time, Pallas kernels for 13%

profile of v2, /device:TPU:1, one launch (start us, length us, event | category | flops | bytes accessed | tf_op | source)
XLA Modules:
  0.0 159.7 jit_solution(15862650066642988609)
XLA Ops:
  7.2 0.0 all-gather.5.cloned.1.call-start
  7.2 9.4 %ssd_send.1 = (bf16[16,400,128]{2,1,0:T(8,128)(2,1)}, bf16[16,512,128]{2,1,0:T(8,128)(2,1)}, bf16[16,512,128]{2,1,0:T(8,128)(2,1)}, f32[16,512]{1,0:T(8,128)}, bf16[2,512,128]{2,1,0:T(8,128)(2,1)}) custom-call(bf16[512,16,128]{2,1,0:T(8,128)(2,1)} %x_ref.1, bf16[512,16,128]{2,1,0:T(8,128)(2,1)} %y_ref.1, f32[16,512]{1,0:T(8,128)} %bitcast.26, ...), custom_call_target="tpu_custom_call" | custom-call | tf_op jit(solution)/shard_map/ssd_send/pallas_call | solution.py:105
  16.6 0.0 copy-start.5
  16.6 0.0 all-gather.5.cloned.1.call-update
  16.6 0.0 reduce-scatter.2.cloned.1.call-start
  16.7 31.1 %all_to_all.10.recv = bf16[16,400,128]{2,1,0:T(8,128)(2,1)S(1)} all-to-all(bf16[16,400,128]{2,1,0:T(8,128)(2,1)} %get-tuple-element.23), channel_id=1, replica_groups=mesh['seq'=16,'head'=8] {'seq'}, dimensions={0} | all-to-all | bytes 3276800 | tf_op jit(solution)/shard_map/all_to_all | solution.py:499
  47.8 0.0 all-gather.5.cloned.1.call-done
  47.8 0.0 copy-done.5
  47.8 0.0 copy-start
  47.8 1.6 copy-done
  49.4 5.9 %attn_stat.1 = f32[24,512]{1,0:T(8,128)S(1)} custom-call(s32[16]{0:T(128)S(1)} %copy-done.5, bf16[16,400,128]{2,1,0:T(8,128)(2,1)S(1)} %all_to_all.10.recv, bf16[8,2,512,128]{3,2,1,0:T(8,128)(2,1)S(1)} %bitcast.16), custom_call_target="tpu_custom_call" | custom-call | tf_op jit(solution)/shard_map/attn_stat/pallas_call | solution.py:199
  55.3 15.1 %all-gather.1 = f32[192,512]{1,0:T(8,128)S(1)} all-gather(f32[24,512]{1,0:T(8,128)S(1)} %attn_stat.1), channel_id=3, replica_groups=mesh['seq'=16,'head'=8] {'head'}, dimensions={0}, use_global_device_ids=true | all-gather | bytes 442368 | tf_op jit(solution)/shard_map/all_gather | solution.py:500
  70.4 18.0 %attn_grad.1 = (bf16[16,384,128]{2,1,0:T(8,128)(2,1)}, bf16[8,128,512]{2,1,0:T(8,128)(2,1)}) custom-call(s32[16]{0:T(128)S(1)} %copy-done.5, bf16[16,400,128]{2,1,0:T(8,128)(2,1)S(1)} %all_to_all.10.recv, bf16[8,2,512,128]{3,2,1,0:T(8,128)(2,1)S(1)} %bitcast.17, f32[8,24,512]{2,1,0:T(8,128)S(1)} %bitcast.18), custom_call_target="tpu_custom_call" | custom-call | tf_op jit(solution)/shard_map/attn_grad/pallas_call | solution.py:295
  88.5 0.0 copy-start.1
  88.5 0.0 copy-start.2
  88.5 0.0 copy-start.3
  88.5 0.0 copy-start.4
  88.5 0.0 reduce-scatter.2.cloned.1.call-update
  88.5 26.4 %all_to_all.11.states = bf16[16,384,128]{2,1,0:T(8,128)(2,1)S(1)} all-to-all(bf16[16,384,128]{2,1,0:T(8,128)(2,1)} %get-tuple-element.25), channel_id=1, replica_groups=mesh['seq'=16,'head'=8] {'seq'}, dimensions={0} | all-to-all | bytes 3145728 | tf_op jit(solution)/shard_map/all_to_all | solution.py:503
  114.9 0.0 copy-done.1
  114.9 0.0 copy-done.2
  114.9 0.0 copy-done.3
  114.9 0.0 copy-done.4
  114.9 21.1 %ssd_grad.1 = (bf16[512,16,128]{2,1,0:T(8,128)(2,1)}, f32[16,512]{1,0:T(8,128)}, f32[512,128]{1,0:T(8,128)}, f32[512,128]{1,0:T(8,128)}) custom-call(bf16[16,512,128]{2,1,0:T(8,128)(2,1)S(1)} %copy-done.1, bf16[16,512,128]{2,1,0:T(8,128)(2,1)} %get-tuple-element.22.yh, bf16[16,384,128]{2,1,0:T(8,128)(2,1)S(1)} %all_to_all.11.states, ...), custom_call_target="tpu_custom_call" | custom-call | tf_op jit(solution)/shard_map/ssd_grad/pallas_call | solution.py:432
  136.0 0.1 slice_reduce_fusion
  136.1 15.0 %all-gather.2 = bf16[1024,128]{1,0:T(8,128)(2,1)} all-gather(bf16[128,128]{1,0:T(8,128)(2,1)S(1)} %slice_reduce_fusion), channel_id=4, replica_groups=mesh['seq'=16,'head'=8] {'head'}, dimensions={0}, use_global_device_ids=true | all-gather | bytes 294912 | tf_op jit(solution)/shard_map/all_gather | solution.py:505
  151.1 0.0 reduce-scatter.2.cloned.1.call-done.dqt
  151.1 1.8 %finish.1 = (bf16[512,128]{1,0:T(8,128)(2,1)}, bf16[512,128]{1,0:T(8,128)(2,1)}, bf16[512,128]{1,0:T(8,128)(2,1)}) custom-call(bf16[1,128,512]{2,1,0:T(8,128)(2,1)} %reduce-scatter.2.cloned.1.call-done.dqt, bf16[8,128,128]{2,1,0:T(8,128)(2,1)} %bitcast.23), custom_call_target="tpu_custom_call" | custom-call | tf_op jit(solution)/shard_map/finish/pallas_call | solution.py:478
Async XLA Ops:
  7.2 40.6 %all-gather.5.cloned.1.call-start = ((), (), s32[]{:S(2)}) async-start(), calls=%async_computation.4 | async-start | bytes 2359296 | tf_op jit(solution)/shard_map/all_gather | solution.py:498
  16.6 31.2 %copy-start.5 = (s32[16]{0:T(128)S(1)}, s32[16]{0:T(128)}, u32[]{:S(2)}) copy-start(s32[16]{0:T(128)} %order.3) | copy-start | bytes 196
  16.6 134.4 %reduce-scatter.2.cloned.1.call-start = ((), (), s32[]{:S(2)}) async-start(), calls=%async_computation.3 | async-start | bytes 1179648 | tf_op jit(solution)/shard_map/reduce_scatter | solution.py:502
  47.8 1.6 copy-start
  88.5 26.4 %copy-start.1 = (bf16[16,512,128]{2,1,0:T(8,128)(2,1)S(1)}, bf16[16,512,128]{2,1,0:T(8,128)(2,1)}, u32[]{:S(2)}) copy-start(bf16[16,512,128]{2,1,0:T(8,128)(2,1)} %get-tuple-element.21.xh) | copy-start | bytes 6291460
  88.5 26.4 %copy-start.2 = (f32[512,1,128]{2,1,0:T(1,128)S(1)}, f32[512,1,128]{2,1,0:T(1,128)}, u32[]{:S(2)}) copy-start(f32[512,1,128]{2,1,0:T(1,128)} %param.12) | copy-start | bytes 786436
  88.5 26.4 %copy-start.3 = (f32[512,1,128]{2,1,0:T(1,128)S(1)}, f32[512,1,128]{2,1,0:T(1,128)}, u32[]{:S(2)}) copy-start(f32[512,1,128]{2,1,0:T(1,128)} %param.13) | copy-start | bytes 786436
  88.5 26.4 %copy-start.4 = (f32[16,512]{1,0:T(8,128)S(1)}, f32[16,512]{1,0:T(8,128)}, u32[]{:S(2)}) copy-start(f32[16,512]{1,0:T(8,128)} %get-tuple-element.26.cum) | copy-start | bytes 98308
Sparse Core Ops, SparseCore 0:
  16.8 28.7 all-gather.4
  88.7 26.0 reduce-scatter.1

commit v3 on v2

--- a/solution.py
+++ b/solution.py
@@ -38,7 +38,7 @@
 
 def ssd_send_kernel(
     x_ref, y_ref, at_ref, b_ref, c_ref, k_ref, v_ref, q_ref, do_ref,
-    send_ref, xh_ref, yh_ref, cum_ref, qd_ref, xs, ys, st, pu, run,
+    send_ref, xh_ref, yh_ref, cum_ref, qd_ref, st, pu, run,
 ):
     k = pl.program_id(0)
     heads = x_ref.shape[1]
@@ -61,11 +61,11 @@
     run[...] = jnp.broadcast_to(before + total, run.shape)
     bt = b_ref[...].T
     ct = c_ref[...].T
-    xs[...] = x_ref[...].astype(F32).reshape(xs.shape)
-    ys[...] = y_ref[...].astype(F32).reshape(ys.shape)
+    xt = jnp.swapaxes(x_ref[...], 0, 1)
+    yt = jnp.swapaxes(y_ref[...], 0, 1)
     for h in range(heads):
-        x = xs[pl.ds(h, BLOCK, stride=heads), :].astype(BF)
-        y = ys[pl.ds(h, BLOCK, stride=heads), :].astype(BF)
+        x = xt[h]
+        y = yt[h]
         xh_ref[h] = x
         yh_ref[h] = y
         bs = (bt * tail[h : h + 1, :]).astype(BF)
@@ -116,8 +116,6 @@
                 pl.BlockSpec((2, tok, 128), lambda k: (0, 0, 0)),
             ],
             scratch_shapes=[
-                pltpu.VMEM((BLOCK * heads, width), F32),
-                pltpu.VMEM((BLOCK * heads, width), F32),
                 pltpu.VMEM((heads, 128, 128), F32),
                 pltpu.VMEM((heads, 128, 128), F32),
                 pltpu.VMEM((heads, 128), F32),
@@ -145,48 +143,44 @@
         vs[32 * b : 32 * b + 32, :] = recv[src, 320 + o : 352 + o, :]
 
 
-def item_at(order, i):
+def item_at(order, size, i):
     first = order[lax.axis_index("seq")]
-    n0 = (first + 4) // 4
+    per = size // 32
+    n0 = (first + per) // per
     late = (i >= n0).astype(jnp.int32)
     g = i - late * n0
     block = jnp.where(late == 1, 31 - first, first)
-    kr = iota((128, 256), 0)
-    key_at = (g * 4 + kr // 32) * 256 + lax.axis_index("head") * 32 + kr % 32
-    bias = jnp.where(key_at <= block * 256 + iota((128, 256), 1), 0.0, NEG)
-    return pl.multiple_of(g * 128, 128), pl.multiple_of(late * 256, 256), bias
+    kr = iota((size, 256), 0)
+    key_at = (g * per + kr // 32) * 256 + lax.axis_index("head") * 32 + kr % 32
+    bias = jnp.where(key_at <= block * 256 + iota((size, 256), 1), 0.0, NEG)
+    return pl.multiple_of(g * size, size), pl.multiple_of(late * 256, 256), bias
 
 
 def attn_stat_kernel(order, recv, qd, stat, ks, vs, inverse):
     heads = qd.shape[0]
     scale = LOG2E * 128**-0.5
     sort_keys(order, inverse, recv, ks, vs)
-    stat[0:heads, :] = jnp.full((heads, 512), NEG, F32)
-    stat[heads:, :] = jnp.zeros((2 * heads, 512), F32)
+    stat[0] = jnp.full((heads, 512), NEG, F32)
+    stat[1:] = jnp.zeros((2, heads, 512), F32)
 
     def item(i, carry):
-        kat, rat, bias = item_at(order, i)
-        kg = ks[pl.ds(kat, 128), :]
-        vg = vs[pl.ds(kat, 128), :]
+        kat, rat, bias = item_at(order, 256, i)
+        kg = ks[pl.ds(kat, 256), :]
+        vg = vs[pl.ds(kat, 256), :]
         for h in range(heads):
             s = dot(kg, qd[h, 0, pl.ds(rat, 256), :], 1, 1) * scale + bias
             dp = dot(vg, qd[h, 1, pl.ds(rat, 256), :], 1, 1)
-            old = stat[h : h + 1, pl.ds(rat, 256)]
+            at = (slice(h, h + 1), pl.ds(rat, 256))
+            old = stat[0, *at]
             top = jnp.maximum(old, jnp.max(s, axis=0, keepdims=True))
             p = jnp.exp2(s - top)
             fix = jnp.exp2(old - top)
-            l = heads + h
-            d = 2 * heads + h
-            stat[h : h + 1, pl.ds(rat, 256)] = top
-            stat[l : l + 1, pl.ds(rat, 256)] = fix * stat[
-                l : l + 1, pl.ds(rat, 256)
-            ] + jnp.sum(p, axis=0, keepdims=True)
-            stat[d : d + 1, pl.ds(rat, 256)] = fix * stat[
-                d : d + 1, pl.ds(rat, 256)
-            ] + jnp.sum(p * dp, axis=0, keepdims=True)
+            stat[0, *at] = top
+            stat[1, *at] = fix * stat[1, *at] + jnp.sum(p, axis=0, keepdims=True)
+            stat[2, *at] = fix * stat[2, *at] + jnp.sum(p * dp, axis=0, keepdims=True)
         return carry
 
-    lax.fori_loop(0, 9, item, 0)
+    lax.fori_loop(0, 5, item, 0)
 
 
 VM = pl.BlockSpec(memory_space=pltpu.VMEM)
@@ -200,7 +194,7 @@
         attn_stat_kernel,
         in_specs=[SM, VM, VM],
         out_specs=VM,
-        out_shape=jax.ShapeDtypeStruct((3 * heads, 512), F32),
+        out_shape=jax.ShapeDtypeStruct((3, heads, 512), F32),
         scratch_shapes=[
             pltpu.VMEM((1024, 128), BF),
             pltpu.VMEM((1024, 128), BF),
@@ -212,7 +206,7 @@
 
 
 def attn_grad_kernel(
-    order, recv, qd, stats, send, dqt, ks, vs, dk, dv, lse, delta, dqs, inverse, dqo, buf, sem
+    order, recv, qd, s0, s1, s2, s3, send, dqt, ks, vs, dk, dv, lse, delta, dqs, inverse, dqo, buf, sem
 ):
     heads = qd.shape[0]
     scale = 128**-0.5
@@ -236,15 +230,14 @@
             pull = keep * pull + recv[e, 128:256, :].astype(F32)
     moves.append(pltpu.make_async_copy(buf.at[:, 128:256], send.at[:, 128:256], sem.at[1]))
     moves[1].start()
-    top = stats[0, 0:heads, :]
-    for j in range(1, stats.shape[0]):
-        top = jnp.maximum(top, stats[j, 0:heads, :])
+    stats = (s0, s1, s2, s3)
+    top = functools.reduce(jnp.maximum, [r[0] for r in stats])
     total = jnp.zeros_like(top)
     dsum = jnp.zeros_like(top)
-    for j in range(stats.shape[0]):
-        f = jnp.exp2(stats[j, 0:heads, :] - top)
-        total = total + f * stats[j, heads : 2 * heads, :]
-        dsum = dsum + f * stats[j, 2 * heads :, :]
+    for r in stats:
+        f = jnp.exp2(r[0] - top)
+        total = total + f * r[1]
+        dsum = dsum + f * r[2]
     lse[...] = top + jnp.log2(total)
     delta[...] = dsum / total
     dk[...] = jnp.zeros_like(dk)
@@ -252,12 +245,12 @@
     dqs[...] = jnp.zeros_like(dqs)
 
     def item(i, carry):
-        kat, rat, bias = item_at(order, i)
-        kg = ks[pl.ds(kat, 128), :]
-        vg = vs[pl.ds(kat, 128), :]
+        kat, rat, bias = item_at(order, 512, i)
+        kg = ks[pl.ds(kat, 512), :]
+        vg = vs[pl.ds(kat, 512), :]
         kt = kg.astype(F32).T.astype(BF)
-        dkg = dk[pl.ds(kat, 128), :]
-        dvg = dv[pl.ds(kat, 128), :]
+        dkg = dk[pl.ds(kat, 512), :]
+        dvg = dv[pl.ds(kat, 512), :]
         for h in range(heads):
             q = qd[h, 0, pl.ds(rat, 256), :]
             do = qd[h, 1, pl.ds(rat, 256), :]
@@ -268,11 +261,11 @@
             dvg = dvg + dot(p.astype(BF), do, 1, 0)
             dkg = dkg + dot(ds, q, 1, 0)
             dqs[h, :, pl.ds(rat, 256)] += dot(kt, ds, 1, 0)
-        dk[pl.ds(kat, 128), :] = dkg
-        dv[pl.ds(kat, 128), :] = dvg
+        dk[pl.ds(kat, 512), :] = dkg
+        dv[pl.ds(kat, 512), :] = dvg
         return carry
 
-    lax.fori_loop(0, 9, item, 0)
+    lax.fori_loop(0, 3, item, 0)
     dqo[...] = (dqs[...] * scale).astype(BF)
     moves.append(pltpu.make_async_copy(dqo, dqt, sem.at[2]))
     moves[2].start()
@@ -289,12 +282,12 @@
         m.wait()
 
 
-def attn_grad(order, recv, qd, stats):
+def attn_grad(order, recv, qd, *stats):
     heads = qd.shape[0]
     n = recv.shape[0]
     return pl.pallas_call(
         attn_grad_kernel,
-        in_specs=[SM, VM, VM, VM],
+        in_specs=[SM] + [VM] * 6,
         out_specs=[HB, HB],
         out_shape=[
             pltpu.HBM((n, 384, 128), BF),
@@ -315,7 +308,7 @@
         ],
         compiler_params=pltpu.CompilerParams(vmem_limit_bytes=20 << 20),
         name="attn_grad",
-    )(order, recv, qd, stats)
+    )(order, recv, qd, *stats)
 
 
 def ssd_grad_kernel(
@@ -323,13 +316,13 @@
     dx_ref, da_ref, db_ref, dc_ref,
     g_s, dg_s, dct, dbt, bt_s, ct_s, colp, dcol, drow, dxs,
 ):
-    h = pl.program_id(0)
-    heads = pl.num_programs(0)
+    base = pl.program_id(0) * 8
+    heads = pl.num_programs(0) * 8
     nb = xh.shape[1] // BLOCK
     rows = iota((BLOCK, BLOCK), 0)
     lanes = iota((BLOCK, BLOCK), 1)
 
-    @pl.when(h == 0)
+    @pl.when(base == 0)
     def _():
         dg_s[...] = jnp.zeros_like(dg_s)
         dct[...] = jnp.zeros_like(dct)
@@ -345,64 +338,60 @@
             ct_s[k] = c.T
             cm = cum[:, sl]
             tl = jnp.exp(cm[:, BLOCK - 1 :] - cm)
-            parts = [p.astype(F32) for p in pieces(cm, 3) + pieces(tl, 2)]
-            parts.append(jnp.zeros((BLOCK - 5 * heads_of(cum), BLOCK), F32))
-            colp[k] = jnp.concatenate(parts, axis=0).T.astype(BF)
+            gap = jnp.zeros((BLOCK // 2 - heads_of(cum), BLOCK), F32)
+            colp[k] = jnp.concatenate([cm, gap, tl, gap], axis=0).T
 
     nh = heads_of(cum)
-    pr = iota((BLOCK, 2 * BLOCK), 0)
-    pc = iota((BLOCK, 2 * BLOCK), 1)
-    mine = (pr % nh) == h
-    left = jnp.logical_and(pr < 3 * nh, pc < BLOCK)
-    right = jnp.logical_and(jnp.logical_and(pr >= 3 * nh, pr < 5 * nh), pc >= BLOCK)
-    pick = jnp.where(jnp.logical_and(mine, jnp.logical_or(left, right)), 1.0, 0.0).astype(BF)
-
-    crow = cum[pl.ds(h, 1), :]
-    x = [xh[0, k * BLOCK : (k + 1) * BLOCK, :] for k in range(nb)]
-    y = [yh[0, k * BLOCK : (k + 1) * BLOCK, :] for k in range(nb)]
-    c = [crow[:, k * BLOCK : (k + 1) * BLOCK] for k in range(nb)]
-    total = [v[:, BLOCK - 1 :] for v in c]
-    keep = [jnp.exp(t) for t in total]
-    tail = [jnp.exp(t - v) for t, v in zip(total, c)]
-    grow = [jnp.exp(v) for v in c]
-    state = [states[0, 0:128, :].astype(F32)]
-    for k in range(nb - 1):
-        bs = (bt_s[k] * tail[k]).astype(BF)
-        state.append(keep[k] * state[k] + dot(bs, x[k], 1, 0))
-    pull = states[0, 128:256, :].astype(F32)
-    for k in reversed(range(nb)):
-        cols = dot(colp[k], pick, 1, 0)
-        decay = jnp.exp(jnp.minimum(c[k] - cols[:, :BLOCK], 0.0))
-        w = g_s[k] * decay
-        dw = dot(x[k], y[k], 1, 1)
-        t = dw * decay
-        dg_s[k] += t
-        z = t * g_s[k]
-        sb = state[k].astype(BF)
-        pb = pull.astype(BF)
-        bs = (b_ref[k * BLOCK : (k + 1) * BLOCK, :] * cols[:, BLOCK:]).astype(BF)
-        dx = dot(w.astype(BF), y[k], 1, 0) + dot(bs, pb, 1, 0)
-        dxs[pl.ds(k * BLOCK * heads + h, BLOCK, stride=nh), :] = dx
-        dcs = dot(sb, y[k], 1, 1) * grow[k]
-        dct[k] += dcs
-        q = dcs * ct_s[k]
-        dbs = dot(pb, x[k], 1, 1) * tail[k]
-        dbt[k] += dbs
-        v = dbs * bt_s[k]
-        vs = jnp.sum(v, axis=0, keepdims=True)
-        line = jnp.sum(z + q, axis=0, keepdims=True) - vs
-        cross = keep[k] * jnp.sum(state[k] * pull, axis=0, keepdims=True)
-        last = jnp.sum(vs + cross, axis=1, keepdims=True)
-        line = jnp.where(iota((1, BLOCK), 1) == BLOCK - 1, line + last, line)
-        at = slice(k * BLOCK, (k + 1) * BLOCK)
-        drow[:, at] = jnp.where(iota((nh, BLOCK), 0) == h, line, drow[:, at])
-        zc = jnp.sum(z, axis=1, keepdims=True)
-        dcol[k] = jnp.where(lanes == h, zc, dcol[k])
-        if k > 0:
+    turned = [pltpu.roll(colp[k], lax.rem(BLOCK - base, BLOCK), 1) for k in range(nb)]
+    for hh in range(8):
+        h = base + hh
+        crow = cum[pl.ds(h, 1), :]
+        x = [xh[hh, k * BLOCK : (k + 1) * BLOCK, :] for k in range(nb)]
+        y = [yh[hh, k * BLOCK : (k + 1) * BLOCK, :] for k in range(nb)]
+        c = [crow[:, k * BLOCK : (k + 1) * BLOCK] for k in range(nb)]
+        total = [v[:, BLOCK - 1 :] for v in c]
+        keep = [jnp.exp(t) for t in total]
+        tail = [jnp.exp(t - v) for t, v in zip(total, c)]
+        grow = [jnp.exp(v) for v in c]
+        state = [states[hh, 0:128, :].astype(F32)]
+        for k in range(nb - 1):
+            bs = (bt_s[k] * tail[k]).astype(BF)
+            state.append(keep[k] * state[k] + dot(bs, x[k], 1, 0))
+        pull = states[hh, 128:256, :].astype(F32)
+        for k in reversed(range(nb)):
+            decay = jnp.exp(jnp.minimum(c[k] - turned[k][:, hh : hh + 1], 0.0))
+            w = g_s[k] * decay
+            sb = state[k].astype(BF)
+            xy = dot(jnp.concatenate([x[k], sb], axis=0), y[k], 1, 1)
+            dw = xy[:BLOCK]
+            t = dw * decay
+            dg_s[k] += t
+            z = t * g_s[k]
+            pb = pull.astype(BF)
+            bs = (b_ref[k * BLOCK : (k + 1) * BLOCK, :] * turned[k][:, 64 + hh : 65 + hh]).astype(BF)
             cs = (ct_s[k] * grow[k]).astype(BF)
-            pull = keep[k] * pull + dot(cs, y[k], 1, 0).astype(BF).astype(F32)
-
-    @pl.when(h == heads - 1)
+            wy = dot(jnp.concatenate([w.astype(BF), cs], axis=0), y[k], 1, 0)
+            dx = wy[:BLOCK] + dot(bs, pb, 1, 0)
+            dxs[pl.ds(k * BLOCK * heads + h, BLOCK, stride=nh), :] = dx
+            dcs = xy[BLOCK:] * grow[k]
+            dct[k] += dcs
+            q = dcs * ct_s[k]
+            dbs = dot(pb, x[k], 1, 1) * tail[k]
+            dbt[k] += dbs
+            v = dbs * bt_s[k]
+            vs = jnp.sum(v, axis=0, keepdims=True)
+            line = jnp.sum(z + q, axis=0, keepdims=True) - vs
+            cross = keep[k] * jnp.sum(state[k] * pull, axis=0, keepdims=True)
+            last = jnp.sum(vs + cross, axis=1, keepdims=True)
+            line = jnp.where(iota((1, BLOCK), 1) == BLOCK - 1, line + last, line)
+            at = slice(k * BLOCK, (k + 1) * BLOCK)
+            drow[:, at] = jnp.where(iota((nh, BLOCK), 0) == h, line, drow[:, at])
+            zc = jnp.sum(z, axis=1, keepdims=True)
+            dcol[k] = jnp.where(lanes == h, zc, dcol[k])
+            if k > 0:
+                pull = keep[k] * pull + wy[BLOCK:].astype(BF).astype(F32)
+
+    @pl.when(base == heads - 8)
     def _():
         late = (rows >= lanes).astype(F32)
         for k in range(nb):
@@ -426,16 +415,16 @@
     heads, tok, width = xh.shape
     nb = tok // BLOCK
     rows = states.shape[1]
-    per = pl.BlockSpec((1, tok, width), lambda h: (h, 0, 0))
+    per = pl.BlockSpec((8, tok, width), lambda h: (h, 0, 0))
     whole = lambda *s: pl.BlockSpec(s, lambda h: (0,) * len(s))
     sq = pltpu.VMEM((nb, 128, 128), F32)
     return pl.pallas_call(
         ssd_grad_kernel,
-        grid=(heads,),
+        grid=(heads // 8,),
         in_specs=[
             per,
             per,
-            pl.BlockSpec((1, rows, 128), lambda h: (h, 0, 0)),
+            pl.BlockSpec((8, rows, 128), lambda h: (h, 0, 0)),
             whole(heads, tok),
             whole(tok, 128),
             whole(tok, 128),
@@ -454,34 +443,50 @@
         ],
         scratch_shapes=[
             sq, sq, sq, sq, sq, sq,
-            pltpu.VMEM((nb, 128, 128), BF),
+            sq,
             sq,
             pltpu.VMEM((heads, tok), F32),
             pltpu.VMEM((tok * heads, width), F32),
         ],
         compiler_params=pltpu.CompilerParams(vmem_limit_bytes=48 << 20),
+        cost_estimate=pl.CostEstimate(
+            flops=6 * 10**9, bytes_accessed=10**7, transcendentals=10**6
+        ),
         name="ssd_grad",
     )(xh, yh, states, cum, b, c)
 
 
-def finish_kernel(dqt, dkv, dq, dk, dv):
+def finish_kernel(dqt, *refs):
+    parts, (dq, dk, dv) = refs[:8], refs[8:]
     dq[...] = dqt[0].astype(F32).T.astype(BF)
-    for h in range(dkv.shape[0]):
+    place = lax.axis_index("head")
+    for m, r in enumerate(parts):
+        h = place ^ m
         for j in range(2):
-            to = slice(256 * j + 32 * h, 256 * j + 32 * h + 32)
-            dk[to, :] = dkv[h, 32 * j : 32 * j + 32, :]
-            dv[to, :] = dkv[h, 64 + 32 * j : 96 + 32 * j, :]
-
-
-def finish(dqt, dkv):
+            to = pl.ds(pl.multiple_of(256 * j + 32 * h, 32), 32)
+            dk[to, :] = r[32 * j : 32 * j + 32, :]
+            dv[to, :] = r[64 + 32 * j : 96 + 32 * j, :]
+
+
+def finish(dqt, parts):
     out = jax.ShapeDtypeStruct((512, 128), BF)
     return pl.pallas_call(
         finish_kernel,
-        in_specs=[VM, VM],
+        in_specs=[VM] * 9,
         out_specs=[VM, VM, VM],
         out_shape=[out, out, out],
         name="finish",
-    )(dqt, dkv)
+    )(dqt, *parts)
+
+
+def swap(v, m):
+    return lax.ppermute(v, "head", [(i, i ^ m) for i in range(8)])
+
+
+def join(a, b):
+    top = jnp.maximum(a[0], b[0])
+    f, g = jnp.exp2(a[0] - top), jnp.exp2(b[0] - top)
+    return jnp.stack([top, f * a[1] + g * b[1], f * a[2] + g * b[2]])
 
 
 def per_device(
@@ -497,14 +502,15 @@
     )
     qd = lax.all_gather(qd, "head")
     recv = lax.all_to_all(send, "seq", 0, 0)
-    stats = lax.all_gather(attn_stat(pair_order, recv, qd), "head")
-    back, dqt = attn_grad(pair_order, recv, qd, stats)
+    stat = attn_stat(pair_order, recv, qd)
+    stat = join(stat, swap(stat, 1))
+    back, dqt = attn_grad(pair_order, recv, qd, stat, *[swap(stat, m) for m in (2, 6, 4)])
     dqt = lax.psum_scatter(dqt, "head", scatter_dimension=0, tiled=True)
     states = lax.all_to_all(back, "seq", 0, 0)
     dkv = jnp.sum(states[:, 256:, :].astype(F32), axis=0).astype(BF)
-    dkv = lax.all_gather(dkv, "head")
+    parts = [dkv] + [swap(dkv, m) for m in range(1, 8)]
     dx, da, db, dc = ssd_grad(xh, yh, states, cum, b, c)
-    dq, dk, dv = finish(dqt, dkv)
+    dq, dk, dv = finish(dqt, parts)
     return (
         dx,
         da.T,

time: 160 us -> 136 us (0.85)
  blocking collectives: 87.6 us -> 31.1 us
  waiting for transfers between devices: 0.04 us -> 24.9 us
  starting transfers between devices: 0.08 us -> 21.1 us
  Pallas kernels: 56.2 us -> 39.9 us
  local copies, waits for them, and re-layouts: 1.62 us -> 3.81 us
    all_gather x2 -> x0, blocking collectives: 30.1 us -> none  [the longest x1 15.1 us: per_device(): stats = lax.all_gather(attn_stat(pair_order, recv, qd), 'head')]
    all_to_all x1 -> x0, blocking collectives: 26.4 us -> none  [per_device(): states = lax.all_to_all(back, 'seq', 0, 0)]
    all_to_all x0 -> x1, waiting for transfers between devices: none -> 20 us  [per_device(): states = lax.all_to_all(back, 'seq', 0, 0)]
    ppermute x0 -> x11, starting transfers between devices: none -> 17.2 us  [swap(): return lax.ppermute(v, 'head', [(i, i ^ m) for i in range(8)])]
    pallas_call x3, Pallas kernels: 40.9 us -> 26.4 us  [the longest x1 13.9 us: ssd_grad(): pl.pallas_call(ssd_grad_kernel, grid=(heads // 8,), in_specs=[per, per, p...]
    ppermute x0 -> x11, waiting for transfers between devices: none -> 4.19 us  [swap(): return lax.ppermute(v, 'head', [(i, i ^ m) for i in range(8)])]
    all_to_all x0 -> x1, starting transfers between devices: none -> 3.85 us  [per_device(): states = lax.all_to_all(back, 'seq', 0, 0)]
    unnamed x12 -> x28, local copies, waits for them, and re-layouts: 1.62 us -> 3.81 us
  transfers between devices with their start and end apart: 2 -> 14, of which waited for: 0 -> 4; matrix products, arithmetic and copies ran while one was open for 0% -> 0% of each run, Pallas kernels for 13% -> 10%
where the time goes in v3:
time: 136 us; the launch traced here: 135 us
  Pallas kernels  39.9 us (29%)
  blocking collectives  31.1 us (23%)
  waiting for transfers between devices  24.9 us (18%)
  starting transfers between devices  21.1 us (16%)
  between operations  14.3 us (11%)
  local copies, waits for them, and re-layouts  3.81 us (3%)
    all_to_all x1, blocking collectives, per_device(): recv = lax.all_to_all(send, 'seq', 0, 0)  31.1 us
    all_to_all x1, waiting for transfers between devices, per_device(): states = lax.all_to_all(back, 'seq', 0, 0)  20 us
    ppermute x11, starting transfers between devices, swap(): return lax.ppermute(v, 'head', [(i, i ^ m) for i in range(8)])  17.2 us
    pallas_call x1, Pallas kernels, ssd_grad(): pl.pallas_call(ssd_grad_kernel, grid=(heads // 8,), in_specs=[per, per, p...  13.9 us
    pallas_call x1, Pallas kernels, attn_grad(): pl.pallas_call(attn_grad_kernel, in_specs=[SM] + [VM] * 6, out_specs=[HB,...  10.7 us
    pallas_call x1, Pallas kernels, ssd_send(): pl.pallas_call(ssd_send_kernel, grid_spec=pltpu.PrefetchScalarGridSpec(nu...  8.22 us
    pallas_call x1, Pallas kernels, attn_stat(): pl.pallas_call(attn_stat_kernel, in_specs=[SM, VM, VM], out_specs=VM, out...  5.27 us
    ppermute x11, waiting for transfers between devices, swap(): return lax.ppermute(v, 'head', [(i, i ^ m) for i in range(8)])  4.19 us
  transfers between devices with their start and end apart: 14, of which 4 were waited for; matrix products, arithmetic and copies ran while one was open for 0% of the time, Pallas kernels for 10%

profile of v3, /device:TPU:1, one launch (start us, length us, event | category | flops | bytes accessed | tf_op | source)
XLA Modules:
  0.0 135.3 jit_solution(12861584739087165493)
XLA Ops:
  7.2 0.0 all-gather.3.cloned.1.call-start
  7.2 8.2 %ssd_send.1 = (bf16[16,400,128]{2,1,0:T(8,128)(2,1)}, bf16[16,512,128]{2,1,0:T(8,128)(2,1)}, bf16[16,512,128]{2,1,0:T(8,128)(2,1)}, f32[16,512]{1,0:T(8,128)}, bf16[2,512,128]{2,1,0:T(8,128)(2,1)}) custom-call(bf16[512,16,128]{2,1,0:T(8,128)(2,1)} %x_ref.1, bf16[512,16,128]{2,1,0:T(8,128)(2,1)} %y_ref.1, f32[16,512]{1,0:T(8,128)} %bitcast.22, ...), custom_call_target="tpu_custom_call" | custom-call | tf_op jit(solution)/shard_map/ssd_send/pallas_call | solution.py:105
  15.4 0.0 copy-start.3
  15.5 0.0 all-gather.3.cloned.1.call-update
  15.5 31.1 %all_to_all.10.recv = bf16[16,400,128]{2,1,0:T(8,128)(2,1)S(1)} all-to-all(bf16[16,400,128]{2,1,0:T(8,128)(2,1)} %get-tuple-element.23), channel_id=1, replica_groups=mesh['seq'=16,'head'=8] {'seq'}, dimensions={0} | all-to-all | bytes 3276800 | tf_op jit(solution)/shard_map/all_to_all | solution.py:504
  46.6 0.0 all-gather.3.cloned.1.call-done
  46.6 0.0 copy-done.3
  46.6 0.0 copy-start
  46.6 1.6 %copy-done = bf16[16,512,128]{2,1,0:T(8,128)(2,1)S(1)} copy-done((bf16[16,512,128]{2,1,0:T(8,128)(2,1)S(1)}, bf16[16,512,128]{2,1,0:T(8,128)(2,1)}, u32[]{:S(2)}) %copy-start) | copy-done | bytes 2097176
  48.2 5.3 %attn_stat.1 = f32[3,8,512]{2,1,0:T(8,128)S(1)} custom-call(s32[16]{0:T(128)S(1)} %copy-done.3, bf16[16,400,128]{2,1,0:T(8,128)(2,1)S(1)} %all_to_all.10.recv, bf16[8,2,512,128]{3,2,1,0:T(8,128)(2,1)S(1)} %bitcast.14), custom_call_target="tpu_custom_call" | custom-call | tf_op jit(solution)/shard_map/attn_stat/pallas_call | solution.py:193
  53.5 2.0 %collective-permute-start = (f32[3,8,512]{2,1,0:T(8,128)S(1)}, f32[3,8,512]{2,1,0:T(8,128)S(1)}, u32[]{:S(2)}, u32[]{:S(2)}) collective-permute-start(f32[3,8,512]{2,1,0:T(8,128)S(1)} %attn_stat.1), channel_id=1, source_target_pairs={{0,1},{1,0},{2,3},{3,2},{4,5},{5,4},{6,7},{7,6},{8,9},{9,8},{10,11... | collective-permute-start | bytes 147464 | tf_op jit(solution)/shard_map/ppermute | solution.py:483
  55.5 0.9 collective-permute-done
  56.5 2.8 %collective-permute-start.3 = (f32[3,8,512]{2,1,0:T(8,128)S(1)}, f32[3,8,512]{2,1,0:T(8,128)S(1)}, u32[]{:S(2)}, u32[]{:S(2)}) collective-permute-start(f32[3,8,512]{2,1,0:T(8,128)S(1)} %pad_maximum_fusion.s0), channel_id=1, source_target_pairs={{0,4},{1,5},{2,6},{3,7},{4,0},{5,1},{6,2},{7,3},{8,12},{9,13},{10,... | collective-permute-start | bytes 147464 | tf_op jit(solution)/shard_map/ppermute | solution.py:483
  59.3 0.9 collective-permute-start.2
  60.1 0.0 collective-permute-start.1
  60.1 0.9 collective-permute-done.3.s3
  61.0 2.4 %collective-permute-done.2.s2 = f32[3,8,512]{2,1,0:T(8,128)S(1)} collective-permute-done((f32[3,8,512]{2,1,0:T(8,128)S(1)}, f32[3,8,512]{2,1,0:T(8,128)S(1)}, u32[]{:S(2)}, u32[]{:S(2)}) %collective-permute-start.2) | collective-permute-done | bytes 49184 | tf_op jit(solution)/shard_map/ppermute | solution.py:483
  63.4 0.0 collective-permute-done.1.s1
  63.4 10.7 %attn_grad.1 = (bf16[16,384,128]{2,1,0:T(8,128)(2,1)}, bf16[8,128,512]{2,1,0:T(8,128)(2,1)}) custom-call(s32[16]{0:T(128)S(1)} %copy-done.3, bf16[16,400,128]{2,1,0:T(8,128)(2,1)S(1)} %all_to_all.10.recv, bf16[8,2,512,128]{3,2,1,0:T(8,128)(2,1)S(1)} %bitcast.15, f32[3,8,512]{2,1,0:T(8,128)S(1)} %pad_maximum_fusion.s0, ...), custom_call_target="tpu_custom_call" | custom-call | tf_op jit(solution)/shard_map/attn_grad/pallas_call | solution.py:288
  74.1 0.0 copy-start.1
  74.2 0.0 copy-start.2
  74.2 0.0 copy-start.5
  74.2 3.9 %all-to-all-start.1 = ((bf16[16,384,128]{2,1,0:T(8,128)(2,1)}), bf16[16,384,128]{2,1,0:T(8,128)(2,1)S(1)}, u32[]{:S(2)}, u32[]{:S(2)}) async-start(bf16[16,384,128]{2,1,0:T(8,128)(2,1)} %get-tuple-element.25), calls=%async_computation.1 | async-start | bytes 3145728 | tf_op jit(solution)/shard_map/all_to_all | solution.py:509
  78.0 0.0 reduce-scatter.2.cloned.1.call-start
  78.1 0.7 reduce-scatter.2.cloned.1.call-update
  78.8 20.0 %all-to-all-done.1.states = bf16[16,384,128]{2,1,0:T(8,128)(2,1)S(1)} async-done(((bf16[16,384,128]{2,1,0:T(8,128)(2,1)}), bf16[16,384,128]{2,1,0:T(8,128)(2,1)S(1)}, u32[]{:S(2)}, u32[]{:S(2)}) %all-to-all-start.1) | async-done | bytes 1572896 | tf_op jit(solution)/shard_map/all_to_all | solution.py:509
  98.8 0.1 slice_reduce_fusion.refs_0_
  98.9 0.0 copy-start.6
  98.9 5.6 %collective-permute-start.10 = (bf16[128,128]{1,0:T(8,128)(2,1)S(1)}, bf16[128,128]{1,0:T(8,128)(2,1)S(1)}, u32[]{:S(2)}, u32[]{:S(2)}) collective-permute-start(bf16[128,128]{1,0:T(8,128)(2,1)S(1)} %slice_reduce_fusion.refs_0_), channel_id=1, source_target_pairs={{0,7},{1,6},{2,5},{3,4},{4,3},{5,2},{6,1},{7,0},{8,15},{9,14},{10,... | collective-permute-start | bytes 98312 | tf_op jit(solution)/shard_map/ppermute | solution.py:483
  104.4 0.9 collective-permute-start.9
  105.3 0.7 collective-permute-start.8
  106.0 1.8 %collective-permute-start.7 = (bf16[128,128]{1,0:T(8,128)(2,1)S(1)}, bf16[128,128]{1,0:T(8,128)(2,1)S(1)}, u32[]{:S(2)}, u32[]{:S(2)}) collective-permute-start(bf16[128,128]{1,0:T(8,128)(2,1)S(1)} %slice_reduce_fusion.refs_0_), channel_id=1, source_target_pairs={{0,4},{1,5},{2,6},{3,7},{4,0},{5,1},{6,2},{7,3},{8,12},{9,13},{10,... | collective-permute-start | bytes 98312 | tf_op jit(solution)/shard_map/ppermute | solution.py:483
  107.8 1.1 collective-permute-start.6
  108.8 0.0 collective-permute-done.10.refs_7_
  108.8 0.0 copy-start.7
  108.8 1.5 %collective-permute-start.5 = (bf16[128,128]{1,0:T(8,128)(2,1)S(1)}, bf16[128,128]{1,0:T(8,128)(2,1)S(1)}, u32[]{:S(2)}, u32[]{:S(2)}) collective-permute-start(bf16[128,128]{1,0:T(8,128)(2,1)S(1)} %slice_reduce_fusion.refs_0_), channel_id=1, source_target_pairs={{0,2},{1,3},{2,0},{3,1},{4,6},{5,7},{6,4},{7,5},{8,10},{9,11},{10,... | collective-permute-start | bytes 98312 | tf_op jit(solution)/shard_map/ppermute | solution.py:483
  110.4 0.0 collective-permute-done.9.refs_6_
  110.4 0.0 collective-permute-start.4
  110.4 0.0 copy-done.1
  110.4 0.0 copy-done.2
  110.4 0.0 copy-done.5
  110.4 0.0 copy-start.4
  110.4 1.6 %copy-done.4 = bf16[16,512,128]{2,1,0:T(8,128)(2,1)S(1)} copy-done((bf16[16,512,128]{2,1,0:T(8,128)(2,1)S(1)}, bf16[16,512,128]{2,1,0:T(8,128)(2,1)}, u32[]{:S(2)}) %copy-start.4) | copy-done | bytes 2097176
  112.0 13.9 %ssd_grad.1 = (bf16[512,16,128]{2,1,0:T(8,128)(2,1)}, f32[16,512]{1,0:T(8,128)}, f32[512,128]{1,0:T(8,128)}, f32[512,128]{1,0:T(8,128)}) custom-call(bf16[16,512,128]{2,1,0:T(8,128)(2,1)S(1)} %copy-done.4, bf16[16,512,128]{2,1,0:T(8,128)(2,1)} %get-tuple-element.22.yh, bf16[16,384,128]{2,1,0:T(8,128)(2,1)S(1)} %all-to-all-done.1.states, ...), custom_call_target="tpu_custom_call" | custom-call | flops 6000000000 | bytes 10000000 | tf_op jit(solution)/shard_map/ssd_grad/pallas_call | solution.py:421
  125.9 0.0 copy-done.6
  125.9 0.0 copy-done.7
  125.9 0.0 copy-done.8
  125.9 0.0 collective-permute-done.8.refs_5_
  125.9 0.0 copy-start.9
  126.0 0.0 collective-permute-done.7.refs_4_
  126.0 0.0 copy-start.10
  126.0 0.0 collective-permute-done.6.refs_3_
  126.0 0.0 copy-start.11
  126.0 0.0 collective-permute-done.5.refs_2_
  126.0 0.0 copy-start.12
  126.0 0.0 collective-permute-done.4.refs_1_
  126.0 0.0 copy-start.13
  126.0 0.0 reduce-scatter.2.cloned.1.call-done.dqt
  126.1 0.5 copy-done.9
  126.6 0.0 copy-done.10
  126.6 0.0 copy-done.11
  126.6 0.0 copy-done.12
  126.6 0.0 copy-done.13
  126.6 1.8 %finish.1 = (bf16[512,128]{1,0:T(8,128)(2,1)}, bf16[512,128]{1,0:T(8,128)(2,1)}, bf16[512,128]{1,0:T(8,128)(2,1)}) custom-call(bf16[1,128,512]{2,1,0:T(8,128)(2,1)} %reduce-scatter.2.cloned.1.call-done.dqt, bf16[128,128]{1,0:T(8,128)(2,1)} %copy-done.6, bf16[128,128]{1,0:T(8,128)(2,1)} %copy-done.13, bf16[128,128]{1,0:T(8,128)(2,1)} %copy-done.12, ...), custom_call_target="tpu_custom_call" | custom-call | tf_op jit(solution)/shard_map/finish/pallas_call | solution.py:473
  (4 shorter events, 0.0 us)
Async XLA Ops:
  7.2 39.4 %all-gather.3.cloned.1.call-start = ((), (), s32[]{:S(2)}) async-start(), calls=%async_computation.4 | async-start | bytes 2359296 | tf_op jit(solution)/shard_map/all_gather | solution.py:503
  15.4 31.2 %copy-start.3 = (s32[16]{0:T(128)S(1)}, s32[16]{0:T(128)}, u32[]{:S(2)}) copy-start(s32[16]{0:T(128)} %order.3) | copy-start | bytes 196
  46.6 1.6 %copy-start = (bf16[16,512,128]{2,1,0:T(8,128)(2,1)S(1)}, bf16[16,512,128]{2,1,0:T(8,128)(2,1)}, u32[]{:S(2)}) copy-start(bf16[16,512,128]{2,1,0:T(8,128)(2,1)} %all-gather.3.cloned.1.call-done) | copy-start | bytes 6291460
  53.5 2.9 %collective-permute-start = (f32[3,8,512]{2,1,0:T(8,128)S(1)}, f32[3,8,512]{2,1,0:T(8,128)S(1)}, u32[]{:S(2)}, u32[]{:S(2)}) collective-permute-start(f32[3,8,512]{2,1,0:T(8,128)S(1)} %attn_stat.1), channel_id=1, source_target_pairs={{0,1},{1,0},{2,3},{3,2},{4,5},{5,4},{6,7},{7,6},{8,9},{9,8},{10,11... | collective-permute-start | bytes 147464 | tf_op jit(solution)/shard_map/ppermute | solution.py:483
  56.5 4.5 %collective-permute-start.3 = (f32[3,8,512]{2,1,0:T(8,128)S(1)}, f32[3,8,512]{2,1,0:T(8,128)S(1)}, u32[]{:S(2)}, u32[]{:S(2)}) collective-permute-start(f32[3,8,512]{2,1,0:T(8,128)S(1)} %pad_maximum_fusion.s0), channel_id=1, source_target_pairs={{0,4},{1,5},{2,6},{3,7},{4,0},{5,1},{6,2},{7,3},{8,12},{9,13},{10,... | collective-permute-start | bytes 147464 | tf_op jit(solution)/shard_map/ppermute | solution.py:483
  59.3 4.2 %collective-permute-start.2 = (f32[3,8,512]{2,1,0:T(8,128)S(1)}, f32[3,8,512]{2,1,0:T(8,128)S(1)}, u32[]{:S(2)}, u32[]{:S(2)}) collective-permute-start(f32[3,8,512]{2,1,0:T(8,128)S(1)} %pad_maximum_fusion.s0), channel_id=1, source_target_pairs={{0,6},{1,7},{2,4},{3,5},{4,2},{5,3},{6,0},{7,1},{8,14},{9,15},{10,... | collective-permute-start | bytes 147464 | tf_op jit(solution)/shard_map/ppermute | solution.py:483
  60.1 3.3 %collective-permute-start.1 = (f32[3,8,512]{2,1,0:T(8,128)S(1)}, f32[3,8,512]{2,1,0:T(8,128)S(1)}, u32[]{:S(2)}, u32[]{:S(2)}) collective-permute-start(f32[3,8,512]{2,1,0:T(8,128)S(1)} %pad_maximum_fusion.s0), channel_id=1, source_target_pairs={{0,2},{1,3},{2,0},{3,1},{4,6},{5,7},{6,4},{7,5},{8,10},{9,11},{10,... | collective-permute-start | bytes 147464 | tf_op jit(solution)/shard_map/ppermute | solution.py:483
  74.1 36.2 %copy-start.1 = (f32[512,1,128]{2,1,0:T(1,128)S(1)}, f32[512,1,128]{2,1,0:T(1,128)}, u32[]{:S(2)}) copy-start(f32[512,1,128]{2,1,0:T(1,128)} %param.12) | copy-start | bytes 786436
  74.2 36.2 %copy-start.2 = (f32[512,1,128]{2,1,0:T(1,128)S(1)}, f32[512,1,128]{2,1,0:T(1,128)}, u32[]{:S(2)}) copy-start(f32[512,1,128]{2,1,0:T(1,128)} %param.13) | copy-start | bytes 786436
  74.2 36.2 %copy-start.5 = (f32[16,512]{1,0:T(8,128)S(1)}, f32[16,512]{1,0:T(8,128)}, u32[]{:S(2)}) copy-start(f32[16,512]{1,0:T(8,128)} %get-tuple-element.26.cum) | copy-start | bytes 98308
  74.2 24.6 %all-to-all-start.1 = ((bf16[16,384,128]{2,1,0:T(8,128)(2,1)}), bf16[16,384,128]{2,1,0:T(8,128)(2,1)S(1)}, u32[]{:S(2)}, u32[]{:S(2)}) async-start(bf16[16,384,128]{2,1,0:T(8,128)(2,1)} %get-tuple-element.25), calls=%async_computation.1 | async-start | bytes 3145728 | tf_op jit(solution)/shard_map/all_to_all | solution.py:509
  78.0 48.0 %reduce-scatter.2.cloned.1.call-start = ((), (), s32[]{:S(2)}) async-start(), calls=%async_computation.3 | async-start | bytes 1179648 | tf_op jit(solution)/shard_map/reduce_scatter | solution.py:508
  98.9 27.1 %copy-start.6 = (bf16[128,128]{1,0:T(8,128)(2,1)}, bf16[128,128]{1,0:T(8,128)(2,1)S(1)}, u32[]{:S(2)}) copy-start(bf16[128,128]{1,0:T(8,128)(2,1)S(1)} %slice_reduce_fusion.refs_0_) | copy-start | bytes 98308
  98.9 10.0 %collective-permute-start.10 = (bf16[128,128]{1,0:T(8,128)(2,1)S(1)}, bf16[128,128]{1,0:T(8,128)(2,1)S(1)}, u32[]{:S(2)}, u32[]{:S(2)}) collective-permute-start(bf16[128,128]{1,0:T(8,128)(2,1)S(1)} %slice_reduce_fusion.refs_0_), channel_id=1, source_target_pairs={{0,7},{1,6},{2,5},{3,4},{4,3},{5,2},{6,1},{7,0},{8,15},{9,14},{10,... | collective-permute-start | bytes 98312 | tf_op jit(solution)/shard_map/ppermute | solution.py:483
  104.4 5.9 %collective-permute-start.9 = (bf16[128,128]{1,0:T(8,128)(2,1)S(1)}, bf16[128,128]{1,0:T(8,128)(2,1)S(1)}, u32[]{:S(2)}, u32[]{:S(2)}) collective-permute-start(bf16[128,128]{1,0:T(8,128)(2,1)S(1)} %slice_reduce_fusion.refs_0_), channel_id=1, source_target_pairs={{0,6},{1,7},{2,4},{3,5},{4,2},{5,3},{6,0},{7,1},{8,14},{9,15},{10,... | collective-permute-start | bytes 98312 | tf_op jit(solution)/shard_map/ppermute | solution.py:483
  105.3 20.6 %collective-permute-start.8 = (bf16[128,128]{1,0:T(8,128)(2,1)S(1)}, bf16[128,128]{1,0:T(8,128)(2,1)S(1)}, u32[]{:S(2)}, u32[]{:S(2)}) collective-permute-start(bf16[128,128]{1,0:T(8,128)(2,1)S(1)} %slice_reduce_fusion.refs_0_), channel_id=1, source_target_pairs={{0,5},{1,4},{2,7},{3,6},{4,1},{5,0},{6,3},{7,2},{8,13},{9,12},{10,... | collective-permute-start | bytes 98312 | tf_op jit(solution)/shard_map/ppermute | solution.py:483
  106.0 20.0 %collective-permute-start.7 = (bf16[128,128]{1,0:T(8,128)(2,1)S(1)}, bf16[128,128]{1,0:T(8,128)(2,1)S(1)}, u32[]{:S(2)}, u32[]{:S(2)}) collective-permute-start(bf16[128,128]{1,0:T(8,128)(2,1)S(1)} %slice_reduce_fusion.refs_0_), channel_id=1, source_target_pairs={{0,4},{1,5},{2,6},{3,7},{4,0},{5,1},{6,2},{7,3},{8,12},{9,13},{10,... | collective-permute-start | bytes 98312 | tf_op jit(solution)/shard_map/ppermute | solution.py:483
  107.8 18.2 %collective-permute-start.6 = (bf16[128,128]{1,0:T(8,128)(2,1)S(1)}, bf16[128,128]{1,0:T(8,128)(2,1)S(1)}, u32[]{:S(2)}, u32[]{:S(2)}) collective-permute-start(bf16[128,128]{1,0:T(8,128)(2,1)S(1)} %slice_reduce_fusion.refs_0_), channel_id=1, source_target_pairs={{0,3},{1,2},{2,1},{3,0},{4,7},{5,6},{6,5},{7,4},{8,11},{9,10},{10,... | collective-permute-start | bytes 98312 | tf_op jit(solution)/shard_map/ppermute | solution.py:483
  108.8 17.1 %copy-start.7 = (bf16[128,128]{1,0:T(8,128)(2,1)}, bf16[128,128]{1,0:T(8,128)(2,1)S(1)}, u32[]{:S(2)}) copy-start(bf16[128,128]{1,0:T(8,128)(2,1)S(1)} %collective-permute-done.10.refs_7_) | copy-start | bytes 98308
  108.8 17.2 %collective-permute-start.5 = (bf16[128,128]{1,0:T(8,128)(2,1)S(1)}, bf16[128,128]{1,0:T(8,128)(2,1)S(1)}, u32[]{:S(2)}, u32[]{:S(2)}) collective-permute-start(bf16[128,128]{1,0:T(8,128)(2,1)S(1)} %slice_reduce_fusion.refs_0_), channel_id=1, source_target_pairs={{0,2},{1,3},{2,0},{3,1},{4,6},{5,7},{6,4},{7,5},{8,10},{9,11},{10,... | collective-permute-start | bytes 98312 | tf_op jit(solution)/shard_map/ppermute | solution.py:483
  110.4 15.6 %copy-start.8 = (bf16[128,128]{1,0:T(8,128)(2,1)}, bf16[128,128]{1,0:T(8,128)(2,1)S(1)}, u32[]{:S(2)}) copy-start(bf16[128,128]{1,0:T(8,128)(2,1)S(1)} %collective-permute-done.9.refs_6_) | copy-start | bytes 98308
  110.4 15.7 %collective-permute-start.4 = (bf16[128,128]{1,0:T(8,128)(2,1)S(1)}, bf16[128,128]{1,0:T(8,128)(2,1)S(1)}, u32[]{:S(2)}, u32[]{:S(2)}) collective-permute-start(bf16[128,128]{1,0:T(8,128)(2,1)S(1)} %slice_reduce_fusion.refs_0_), channel_id=1, source_target_pairs={{0,1},{1,0},{2,3},{3,2},{4,5},{5,4},{6,7},{7,6},{8,9},{9,8},{10,11... | collective-permute-start | bytes 98312 | tf_op jit(solution)/shard_map/ppermute | solution.py:483
  110.4 1.6 %copy-start.4 = (bf16[16,512,128]{2,1,0:T(8,128)(2,1)S(1)}, bf16[16,512,128]{2,1,0:T(8,128)(2,1)}, u32[]{:S(2)}) copy-start(bf16[16,512,128]{2,1,0:T(8,128)(2,1)} %get-tuple-element.21.xh) | copy-start | bytes 6291460
  125.9 0.6 copy-start.9
  126.0 0.6 copy-start.10
  126.0 0.6 copy-start.11
  126.0 0.6 copy-start.12
  126.0 0.6 copy-start.13
Sparse Core Ops, SparseCore 0:
  15.6 28.7 all-gather.2
  81.3 32.1 reduce-scatter.1

commit v4 on v3

--- a/solution.py
+++ b/solution.py
@@ -129,8 +129,46 @@
             jax.ShapeDtypeStruct((2, tok, 128), BF),
         ],
         compiler_params=pltpu.CompilerParams(vmem_limit_bytes=60 << 20),
+        cost_estimate=pl.CostEstimate(
+            flops=3 * 10**9, bytes_accessed=10**7, transcendentals=10**5
+        ),
         name="ssd_send",
     )(x, y, at, b, c, keys, values, q, do)
+
+
+VM = pl.BlockSpec(memory_space=pltpu.VMEM)
+SM = pl.BlockSpec(memory_space=pltpu.SMEM)
+HB = pl.BlockSpec(memory_space=pltpu.HBM)
+
+
+def scan_kernel(recv, back):
+    n = recv.shape[0]
+    state = jnp.zeros((128, 128), F32)
+    for e in range(n):
+        back[e, 0:128, :] = state.astype(BF)
+        if e < n - 1:
+            t = recv[e, 384:400, :].astype(F32)
+            keep = jnp.exp(t[0:1] + t[1:2] + t[2:3])
+            state = keep * state + recv[e, 0:128, :].astype(F32)
+    pull = jnp.zeros((128, 128), F32)
+    for e in reversed(range(n)):
+        back[e, 128:256, :] = pull.astype(BF)
+        if e > 0:
+            t = recv[e, 384:400, :].astype(F32)
+            keep = jnp.exp(t[0:1] + t[1:2] + t[2:3])
+            pull = keep * pull + recv[e, 128:256, :].astype(F32)
+
+
+def scan(recv):
+    n = recv.shape[0]
+    return pl.pallas_call(
+        scan_kernel,
+        in_specs=[VM],
+        out_specs=VM,
+        out_shape=jax.ShapeDtypeStruct((n, 256, 128), BF),
+        compiler_params=pltpu.CompilerParams(vmem_limit_bytes=20 << 20),
+        name="scan",
+    )(recv)
 
 
 def sort_keys(order, inverse, recv, ks, vs):
@@ -156,8 +194,9 @@
     return pl.multiple_of(g * size, size), pl.multiple_of(late * 256, 256), bias
 
 
-def attn_stat_kernel(order, recv, qd, stat, ks, vs, inverse):
-    heads = qd.shape[0]
+def attn_stat_kernel(order, recv, *refs):
+    qd, (stat, ks, vs, inverse) = refs[:8], refs[8:]
+    heads = len(qd)
     scale = LOG2E * 128**-0.5
     sort_keys(order, inverse, recv, ks, vs)
     stat[0] = jnp.full((heads, 512), NEG, F32)
@@ -168,8 +207,8 @@
         kg = ks[pl.ds(kat, 256), :]
         vg = vs[pl.ds(kat, 256), :]
         for h in range(heads):
-            s = dot(kg, qd[h, 0, pl.ds(rat, 256), :], 1, 1) * scale + bias
-            dp = dot(vg, qd[h, 1, pl.ds(rat, 256), :], 1, 1)
+            s = dot(kg, qd[h][0, pl.ds(rat, 256), :], 1, 1) * scale + bias
+            dp = dot(vg, qd[h][1, pl.ds(rat, 256), :], 1, 1)
             at = (slice(h, h + 1), pl.ds(rat, 256))
             old = stat[0, *at]
             top = jnp.maximum(old, jnp.max(s, axis=0, keepdims=True))
@@ -183,16 +222,11 @@
     lax.fori_loop(0, 5, item, 0)
 
 
-VM = pl.BlockSpec(memory_space=pltpu.VMEM)
-SM = pl.BlockSpec(memory_space=pltpu.SMEM)
-HB = pl.BlockSpec(memory_space=pltpu.HBM)
-
-
 def attn_stat(order, recv, qd):
-    heads = qd.shape[0]
+    heads = len(qd)
     return pl.pallas_call(
         attn_stat_kernel,
-        in_specs=[SM, VM, VM],
+        in_specs=[SM] + [VM] * 9,
         out_specs=VM,
         out_shape=jax.ShapeDtypeStruct((3, heads, 512), F32),
         scratch_shapes=[
@@ -201,43 +235,29 @@
             pltpu.SMEM((16,), jnp.int32),
         ],
         compiler_params=pltpu.CompilerParams(vmem_limit_bytes=20 << 20),
+        cost_estimate=pl.CostEstimate(
+            flops=4 * 10**9, bytes_accessed=5 * 10**6, transcendentals=10**6
+        ),
         name="attn_stat",
-    )(order, recv, qd)
-
-
-def attn_grad_kernel(
-    order, recv, qd, s0, s1, s2, s3, send, dqt, ks, vs, dk, dv, lse, delta, dqs, inverse, dqo, buf, sem
-):
-    heads = qd.shape[0]
+    )(order, recv, *qd)
+
+
+def attn_grad_kernel(order, recv, *refs):
+    qd, stats, send, dqt = refs[:8], refs[8:12], refs[12], refs[13:21]
+    ks, vs, dk, dv, lse, delta, dqs, inverse, dqo, buf, sem = refs[21:]
+    heads = len(qd)
     scale = 128**-0.5
     sort_keys(order, inverse, recv, ks, vs)
-    n = recv.shape[0]
-    state = jnp.zeros((128, 128), F32)
-    for e in range(n):
-        buf[e, 0:128, :] = state.astype(BF)
-        if e < n - 1:
-            t = recv[e, 384:400, :].astype(F32)
-            keep = jnp.exp(t[0:1] + t[1:2] + t[2:3])
-            state = keep * state + recv[e, 0:128, :].astype(F32)
-    moves = [pltpu.make_async_copy(buf.at[:, 0:128], send.at[:, 0:128], sem.at[0])]
-    moves[0].start()
-    pull = jnp.zeros((128, 128), F32)
-    for e in reversed(range(n)):
-        buf[e, 128:256, :] = pull.astype(BF)
-        if e > 0:
-            t = recv[e, 384:400, :].astype(F32)
-            keep = jnp.exp(t[0:1] + t[1:2] + t[2:3])
-            pull = keep * pull + recv[e, 128:256, :].astype(F32)
-    moves.append(pltpu.make_async_copy(buf.at[:, 128:256], send.at[:, 128:256], sem.at[1]))
-    moves[1].start()
-    stats = (s0, s1, s2, s3)
-    top = functools.reduce(jnp.maximum, [r[0] for r in stats])
+    tables = [[r[i] for i in range(3)] for r in stats]
+    for m, v in zip((2, 6, 4), tables[1:]):
+        v[:] = [turn_rows(x, m) for x in v]
+    top = functools.reduce(jnp.maximum, [v[0] for v in tables])
     total = jnp.zeros_like(top)
     dsum = jnp.zeros_like(top)
-    for r in stats:
-        f = jnp.exp2(r[0] - top)
-        total = total + f * r[1]
-        dsum = dsum + f * r[2]
+    for v in tables:
+        f = jnp.exp2(v[0] - top)
+        total = total + f * v[1]
+        dsum = dsum + f * v[2]
     lse[...] = top + jnp.log2(total)
     delta[...] = dsum / total
     dk[...] = jnp.zeros_like(dk)
@@ -252,8 +272,8 @@
         dkg = dk[pl.ds(kat, 512), :]
         dvg = dv[pl.ds(kat, 512), :]
         for h in range(heads):
-            q = qd[h, 0, pl.ds(rat, 256), :]
-            do = qd[h, 1, pl.ds(rat, 256), :]
+            q = qd[h][0, pl.ds(rat, 256), :]
+            do = qd[h][1, pl.ds(rat, 256), :]
             s = dot(kg, q, 1, 1) * (scale * LOG2E) + bias
             dp = dot(vg, do, 1, 1)
             p = jnp.exp2(s - lse[h : h + 1, pl.ds(rat, 256)])
@@ -267,32 +287,30 @@
 
     lax.fori_loop(0, 3, item, 0)
     dqo[...] = (dqs[...] * scale).astype(BF)
-    moves.append(pltpu.make_async_copy(dqo, dqt, sem.at[2]))
-    moves[2].start()
+    moves = [pltpu.make_async_copy(dqo.at[h], dqt[h], sem.at[h]) for h in range(heads)]
+    for m in moves:
+        m.start()
     for e in range(16):
         b = order[e]
         for j, (r, f) in enumerate(((dk, scale), (dv, 1.0))):
             lo = r[pl.ds(pl.multiple_of(b * 32, 32), 32), :]
             hi = r[pl.ds(pl.multiple_of((31 - b) * 32, 32), 32), :]
-            buf[e, 256 + 64 * j : 288 + 64 * j, :] = (lo * f).astype(BF)
-            buf[e, 288 + 64 * j : 320 + 64 * j, :] = (hi * f).astype(BF)
-    moves.append(pltpu.make_async_copy(buf.at[:, 256:384], send.at[:, 256:384], sem.at[3]))
-    moves[3].start()
+            buf[e, 64 * j : 32 + 64 * j, :] = (lo * f).astype(BF)
+            buf[e, 32 + 64 * j : 64 + 64 * j, :] = (hi * f).astype(BF)
+    moves.append(pltpu.make_async_copy(buf, send, sem.at[heads]))
+    moves[-1].start()
     for m in moves:
         m.wait()
 
 
 def attn_grad(order, recv, qd, *stats):
-    heads = qd.shape[0]
+    heads = len(qd)
     n = recv.shape[0]
     return pl.pallas_call(
         attn_grad_kernel,
-        in_specs=[SM] + [VM] * 6,
-        out_specs=[HB, HB],
-        out_shape=[
-            pltpu.HBM((n, 384, 128), BF),
-            pltpu.HBM((heads, 128, 512), BF),
-        ],
+        in_specs=[SM] + [VM] * 13,
+        out_specs=[HB] * 9,
+        out_shape=[pltpu.HBM((n, 128, 128), BF)] + [pltpu.HBM((128, 512), BF)] * 8,
         scratch_shapes=[
             pltpu.VMEM((1024, 128), BF),
             pltpu.VMEM((1024, 128), BF),
@@ -303,12 +321,15 @@
             pltpu.VMEM((heads, 128, 512), F32),
             pltpu.SMEM((16,), jnp.int32),
             pltpu.VMEM((heads, 128, 512), BF),
-            pltpu.VMEM((n, 384, 128), BF),
-            pltpu.SemaphoreType.DMA((4,)),
+            pltpu.VMEM((n, 128, 128), BF),
+            pltpu.SemaphoreType.DMA((heads + 1,)),
         ],
         compiler_params=pltpu.CompilerParams(vmem_limit_bytes=20 << 20),
+        cost_estimate=pl.CostEstimate(
+            flops=8 * 10**9, bytes_accessed=6 * 10**6, transcendentals=10**6
+        ),
         name="attn_grad",
-    )(order, recv, qd, *stats)
+    )(order, recv, *qd, *stats)
 
 
 def ssd_grad_kernel(
@@ -456,9 +477,10 @@
     )(xh, yh, states, cum, b, c)
 
 
-def finish_kernel(dqt, *refs):
-    parts, (dq, dk, dv) = refs[:8], refs[8:]
-    dq[...] = dqt[0].astype(F32).T.astype(BF)
+def finish_kernel(*refs):
+    dqt, parts, (dq, dk, dv) = refs[:8], refs[8:16], refs[16:]
+    total = functools.reduce(jnp.add, [r[...].astype(F32) for r in dqt])
+    dq[...] = total.T.astype(BF)
     place = lax.axis_index("head")
     for m, r in enumerate(parts):
         h = place ^ m
@@ -472,21 +494,42 @@
     out = jax.ShapeDtypeStruct((512, 128), BF)
     return pl.pallas_call(
         finish_kernel,
-        in_specs=[VM] * 9,
+        in_specs=[VM] * 16,
         out_specs=[VM, VM, VM],
         out_shape=[out, out, out],
         name="finish",
-    )(dqt, *parts)
+    )(*dqt, *parts)
 
 
 def swap(v, m):
     return lax.ppermute(v, "head", [(i, i ^ m) for i in range(8)])
 
 
+def turn_rows(v, m):
+    return jnp.concatenate([v[j ^ m : (j ^ m) + 1] for j in range(v.shape[0])], axis=0)
+
+
+def join_kernel(a, b, o):
+    other = [turn_rows(b[i], 1) for i in range(3)]
+    top = jnp.maximum(a[0], other[0])
+    f, g = jnp.exp2(a[0] - top), jnp.exp2(other[0] - top)
+    o[0] = top
+    o[1] = f * a[1] + g * other[1]
+    o[2] = f * a[2] + g * other[2]
+
+
 def join(a, b):
-    top = jnp.maximum(a[0], b[0])
-    f, g = jnp.exp2(a[0] - top), jnp.exp2(b[0] - top)
-    return jnp.stack([top, f * a[1] + g * b[1], f * a[2] + g * b[2]])
+    return pl.pallas_call(
+        join_kernel,
+        in_specs=[VM, VM],
+        out_specs=VM,
+        out_shape=jax.ShapeDtypeStruct(a.shape, F32),
+        name="join",
+    )(a, b)
+
+
+def after(value, other):
+    return lax.optimization_barrier((value, other))[0]
 
 
 def per_device(
@@ -500,16 +543,19 @@
         ssd_input, ssd_cotangent, log_decay.T, b, c, key_rows, value_rows,
         queries.reshape(tok, 128), attn_cotangent.reshape(tok, 128),
     )
-    qd = lax.all_gather(qd, "head")
     recv = lax.all_to_all(send, "seq", 0, 0)
-    stat = attn_stat(pair_order, recv, qd)
-    stat = join(stat, swap(stat, 1))
-    back, dqt = attn_grad(pair_order, recv, qd, stat, *[swap(stat, m) for m in (2, 6, 4)])
-    dqt = lax.psum_scatter(dqt, "head", scatter_dimension=0, tiled=True)
-    states = lax.all_to_all(back, "seq", 0, 0)
-    dkv = jnp.sum(states[:, 256:, :].astype(F32), axis=0).astype(BF)
+    qds = [qd] + [swap(qd, m) for m in range(1, 8)]
+    turned = scan(recv)
+    states = lax.all_to_all(turned, "seq", 0, 0)
+    first = attn_stat(pair_order, after(recv, turned), qds)
+    stat = join(first, swap(first, 1))
+    back, *dqt = attn_grad(pair_order, recv, qds, stat, *[swap(stat, m) for m in (2, 6, 4)])
+    back = after(back, states)
+    dx, da, db, dc = ssd_grad(after(xh, back), yh, states, cum, b, c)
+    back = lax.all_to_all(back, "seq", 0, 0)
+    dqt = [dqt[0]] + [swap(dqt[m], m) for m in range(1, 8)]
+    dkv = jnp.sum(after(back, da).astype(F32), axis=0).astype(BF)
     parts = [dkv] + [swap(dkv, m) for m in range(1, 8)]
-    dx, da, db, dc = ssd_grad(xh, yh, states, cum, b, c)
     dq, dk, dv = finish(dqt, parts)
     return (
         dx,

time: 136 us -> 132 us (0.971)
  blocking collectives: 31.1 us -> 0 us
  starting transfers between devices: 21.1 us -> 51.7 us
  between operations: 14.3 us -> 0.99 us
  local copies, waits for them, and re-layouts: 3.81 us -> 9.14 us
  Pallas kernels: 39.9 us -> 43.1 us
    all_to_all x1 -> x0, blocking collectives: 31.1 us -> none  [per_device(): recv = lax.all_to_all(send, 'seq', 0, 0)]
    ppermute x11 -> x25, waiting for transfers between devices: 4.19 us -> 25.7 us  [swap(): return lax.ppermute(v, 'head', [(i, i ^ m) for i in range(8)])]
    all_to_all x1 -> x3, waiting for transfers between devices: 20 us -> 0.01 us  [the longest x1 0.01 us: per_device(): states = lax.all_to_all(turned, 'seq', 0, 0)]
    all_to_all x1 -> x3, starting transfers between devices: 3.85 us -> 22.6 us  [the longest x1 8.74 us: per_device(): recv = lax.all_to_all(send, 'seq', 0, 0)]
    ppermute x11 -> x25, starting transfers between devices: 17.2 us -> 29.1 us  [swap(): return lax.ppermute(v, 'head', [(i, i ^ m) for i in range(8)])]
    unnamed x28 -> x60, local copies, waits for them, and re-layouts: 3.81 us -> 9.14 us
    pallas_call x3 -> x5, Pallas kernels: 17.8 us -> 22.2 us  [the longest x1 11.2 us: attn_grad(): pl.pallas_call(attn_grad_kernel, in_specs=[SM] + [VM] * 13, out_specs=[HB...]
  transfers between devices with their start and end apart: 14 -> 28, of which waited for: 4 -> 7; matrix products, arithmetic and copies ran while one was open for 0% -> 0% of each run, Pallas kernels for 10% -> 25%
where the time goes in v4:
time: 132 us; the launch traced here: 131 us
  starting transfers between devices  51.7 us (39%)
  Pallas kernels  43.1 us (33%)
  waiting for transfers between devices  25.7 us (19%)
  local copies, waits for them, and re-layouts  9.14 us (7%)
    ppermute x25, starting transfers between devices, swap(): return lax.ppermute(v, 'head', [(i, i ^ m) for i in range(8)])  29.1 us
    ppermute x25, waiting for transfers between devices, swap(): return lax.ppermute(v, 'head', [(i, i ^ m) for i in range(8)])  25.7 us
    pallas_call x1, Pallas kernels, ssd_grad(): pl.pallas_call(ssd_grad_kernel, grid=(heads // 8,), in_specs=[per, per, p...  12.7 us
    pallas_call x1, Pallas kernels, attn_grad(): pl.pallas_call(attn_grad_kernel, in_specs=[SM] + [VM] * 13, out_specs=[HB...  11.2 us
    unnamed x60, local copies, waits for them, and re-layouts  9.14 us
    all_to_all x1, starting transfers between devices, per_device(): recv = lax.all_to_all(send, 'seq', 0, 0)  8.74 us
    pallas_call x1, Pallas kernels, ssd_send(): pl.pallas_call(ssd_send_kernel, grid_spec=pltpu.PrefetchScalarGridSpec(nu...  8.22 us
    all_to_all x1, starting transfers between devices, per_device(): states = lax.all_to_all(turned, 'seq', 0, 0)  6.94 us
  transfers between devices with their start and end apart: 28, of which 7 were waited for; matrix products, arithmetic and copies ran while one was open for 0% of the time, Pallas kernels for 25%

profile of v4, /device:TPU:1, one launch (start us, length us, event | category | flops | bytes accessed | tf_op | source)
XLA Modules:
  0.0 130.8 jit_solution(10453865665827600369)
XLA Ops:
  0.6 8.2 %ssd_send.1 = (bf16[16,400,128]{2,1,0:T(8,128)(2,1)}, bf16[16,512,128]{2,1,0:T(8,128)(2,1)}, bf16[16,512,128]{2,1,0:T(8,128)(2,1)}, f32[16,512]{1,0:T(8,128)}, bf16[2,512,128]{2,1,0:T(8,128)(2,1)}) custom-call(bf16[512,16,128]{2,1,0:T(8,128)(2,1)} %x_ref.1, bf16[512,16,128]{2,1,0:T(8,128)(2,1)} %y_ref.1, f32[16,512]{1,0:T(8,128)} %bitcast.20, ...), custom_call_target="tpu_custom_call" | custom-call | flops 3000000000 | bytes 10000000 | tf_op jit(solution)/shard_map/ssd_send/pallas_call | solution.py:105
  8.9 0.0 copy-start.4
  8.9 8.7 %all-to-all-start = ((bf16[16,400,128]{2,1,0:T(8,128)(2,1)}), bf16[16,400,128]{2,1,0:T(8,128)(2,1)S(1)}, u32[]{:S(2)}, u32[]{:S(2)}) async-start(bf16[16,400,128]{2,1,0:T(8,128)(2,1)} %get-tuple-element.33), calls=%async_computation | async-start | bytes 3276800 | tf_op jit(solution)/shard_map/all_to_all | solution.py:546
  17.6 0.0 copy-start.11
  17.6 3.4 %collective-permute-start.6 = (bf16[2,512,128]{2,1,0:T(8,128)(2,1)S(1)}, bf16[2,512,128]{2,1,0:T(8,128)(2,1)S(1)}, u32[]{:S(2)}, u32[]{:S(2)}) collective-permute-start(bf16[2,512,128]{2,1,0:T(8,128)(2,1)S(1)} %copy-done.4), channel_id=1, source_target_pairs={{0,7},{1,6},{2,5},{3,4},{4,3},{5,2},{6,1},{7,0},{8,15},{9,14},{10,... | collective-permute-start | bytes 786440 | tf_op jit(solution)/shard_map/ppermute | solution.py:505
  21.0 0.2 collective-permute-start.5
  21.2 1.3 collective-permute-start.4
  22.5 1.9 %collective-permute-start.3 = (bf16[2,512,128]{2,1,0:T(8,128)(2,1)S(1)}, bf16[2,512,128]{2,1,0:T(8,128)(2,1)}, u32[]{:S(2)}, u32[]{:S(2)}) collective-permute-start(bf16[2,512,128]{2,1,0:T(8,128)(2,1)S(1)} %copy-done.4), channel_id=1, source_target_pairs={{0,4},{1,5},{2,6},{3,7},{4,0},{5,1},{6,2},{7,3},{8,12},{9,13},{10,... | collective-permute-start | bytes 786440 | tf_op jit(solution)/shard_map/ppermute | solution.py:505
  24.4 0.4 collective-permute-start.2
  24.8 14.5 %collective-permute-done.6.refs_7_ = bf16[2,512,128]{2,1,0:T(8,128)(2,1)S(1)} collective-permute-done((bf16[2,512,128]{2,1,0:T(8,128)(2,1)S(1)}, bf16[2,512,128]{2,1,0:T(8,128)(2,1)S(1)}, u32[]{:S(2)}, u32[]{:S(2)}) %collective-permute-start.6) | collective-permute-done | bytes 262176 | tf_op jit(solution)/shard_map/ppermute | solution.py:505
  39.2 0.3 collective-permute-start.1
  39.5 5.4 %collective-permute-done.5.refs_6_ = bf16[2,512,128]{2,1,0:T(8,128)(2,1)S(1)} collective-permute-done((bf16[2,512,128]{2,1,0:T(8,128)(2,1)S(1)}, bf16[2,512,128]{2,1,0:T(8,128)(2,1)S(1)}, u32[]{:S(2)}, u32[]{:S(2)}) %collective-permute-start.5) | collective-permute-done | bytes 262176 | tf_op jit(solution)/shard_map/ppermute | solution.py:505
  44.9 0.5 collective-permute-start
  45.4 1.3 scan.1
  46.6 6.9 %all-to-all-start.1 = ((bf16[16,256,128]{2,1,0:T(8,128)(2,1)}), bf16[16,256,128]{2,1,0:T(8,128)(2,1)S(1)}, u32[]{:S(2)}, u32[]{:S(2)}) async-start(bf16[16,256,128]{2,1,0:T(8,128)(2,1)} %scan.1), calls=%async_computation.1 | async-start | bytes 2097152 | tf_op jit(solution)/shard_map/all_to_all | solution.py:549
  53.6 0.0 collective-permute-done.4.refs_5_
  53.6 0.0 collective-permute-done.3.refs_4_
  53.6 0.0 collective-permute-done.1.refs_2_
  53.6 0.0 collective-permute-done.refs_1_
  53.6 0.0 copy-start.6
  53.6 0.9 copy-done.6
  54.6 0.9 copy-done.9
  55.5 6.1 %attn_stat.1.a = f32[3,8,512]{2,1,0:T(8,128)S(1)} custom-call(s32[16]{0:T(128)S(1)} %copy-done.11, bf16[16,400,128]{2,1,0:T(8,128)(2,1)S(1)} %all-to-all-done.recv, bf16[2,512,128]{2,1,0:T(8,128)(2,1)S(1)} %copy-done.4, bf16[2,512,128]{2,1,0:T(8,128)(2,1)} %collective-permute-done.refs_1_, bf16[2,512,128]{2,1,0:T(8,128)(2,1)} %collective-permute-done.1.refs_2_, ...), custom_call_target="tpu_custom_call" | custom-call | flops 4000000000 | bytes 5000000 | tf_op jit(solution)/shard_map/attn_stat/pallas_call | solution.py:227
  61.6 0.0 copy-start.1
  61.6 0.4 collective-permute-start.7
  62.0 1.1 collective-permute-done.7.b
  63.1 1.5 %join.1.refs_8_ = f32[3,8,512]{2,1,0:T(8,128)} custom-call(f32[3,8,512]{2,1,0:T(8,128)} %copy-done.1, f32[3,8,512]{2,1,0:T(8,128)} %collective-permute-done.7.b), custom_call_target="tpu_custom_call" | custom-call | tf_op jit(solution)/shard_map/join/pallas_call | solution.py:522
  64.5 1.1 collective-permute-start.10
  65.7 1.4 %collective-permute-start.9 = (f32[3,8,512]{2,1,0:T(8,128)}, f32[3,8,512]{2,1,0:T(8,128)S(1)}, u32[]{:S(2)}, u32[]{:S(2)}) collective-permute-start(f32[3,8,512]{2,1,0:T(8,128)} %join.1.refs_8_), channel_id=1, source_target_pairs={{0,6},{1,7},{2,4},{3,5},{4,2},{5,3},{6,0},{7,1},{8,14},{9,15},{10,... | collective-permute-start | bytes 147464 | tf_op jit(solution)/shard_map/ppermute | solution.py:505
  67.0 0.2 collective-permute-start.8
  67.2 2.0 %collective-permute-done.10.refs_11_ = f32[3,8,512]{2,1,0:T(8,128)S(1)} collective-permute-done((f32[3,8,512]{2,1,0:T(8,128)}, f32[3,8,512]{2,1,0:T(8,128)S(1)}, u32[]{:S(2)}, u32[]{:S(2)}) %collective-permute-start.10) | collective-permute-done | bytes 49184 | tf_op jit(solution)/shard_map/ppermute | solution.py:505
  69.2 1.6 %collective-permute-done.9.refs_10_ = f32[3,8,512]{2,1,0:T(8,128)S(1)} collective-permute-done((f32[3,8,512]{2,1,0:T(8,128)}, f32[3,8,512]{2,1,0:T(8,128)S(1)}, u32[]{:S(2)}, u32[]{:S(2)}) %collective-permute-start.9) | collective-permute-done | bytes 49184 | tf_op jit(solution)/shard_map/ppermute | solution.py:505
  70.8 0.0 collective-permute-done.8.refs_9_
  70.8 0.8 copy-done
  71.6 0.9 copy-done.7
  72.5 0.9 copy-done.10
  73.5 11.2 %attn_grad.1 = (bf16[16,128,128]{2,1,0:T(8,128)(2,1)}, bf16[128,512]{1,0:T(8,128)(2,1)}, bf16[128,512]{1,0:T(8,128)(2,1)}, bf16[128,512]{1,0:T(8,128)(2,1)}, bf1...) custom-call(s32[16]{0:T(128)S(1)} %copy-done.11, ...), custom_call_target="tpu_custom_call" | custom-call | flops 8000000000 | bytes 6000000 | tf_op jit(solution)/shard_map/attn_grad/pallas_call | solution.py:309
  84.7 1.6 %collective-permute-start.11 = (bf16[128,512]{1,0:T(8,128)(2,1)}, bf16[128,512]{1,0:T(8,128)(2,1)S(1)}, u32[]{:S(2)}, u32[]{:S(2)}) collective-permute-start(bf16[128,512]{1,0:T(8,128)(2,1)} %get-tuple-element.46), channel_id=1, source_target_pairs={{0,1},{1,0},{2,3},{3,2},{4,5},{5,4},{6,7},{7,6},{8,9},{9,8},{10,11... | collective-permute-start | bytes 393224 | tf_op jit(solution)/shard_map/ppermute | solution.py:505
  86.2 0.1 collective-permute-start.12
  86.3 1.6 %collective-permute-start.13 = (bf16[128,512]{1,0:T(8,128)(2,1)}, bf16[128,512]{1,0:T(8,128)(2,1)S(1)}, u32[]{:S(2)}, u32[]{:S(2)}) collective-permute-start(bf16[128,512]{1,0:T(8,128)(2,1)} %get-tuple-element.48), channel_id=1, source_target_pairs={{0,3},{1,2},{2,1},{3,0},{4,7},{5,6},{6,5},{7,4},{8,11},{9,10},{10,... | collective-permute-start | bytes 393224 | tf_op jit(solution)/shard_map/ppermute | solution.py:505
  88.0 1.6 %collective-permute-start.14 = (bf16[128,512]{1,0:T(8,128)(2,1)}, bf16[128,512]{1,0:T(8,128)(2,1)S(1)}, u32[]{:S(2)}, u32[]{:S(2)}) collective-permute-start(bf16[128,512]{1,0:T(8,128)(2,1)} %get-tuple-element.49), channel_id=1, source_target_pairs={{0,4},{1,5},{2,6},{3,7},{4,0},{5,1},{6,2},{7,3},{8,12},{9,13},{10,... | collective-permute-start | bytes 393224 | tf_op jit(solution)/shard_map/ppermute | solution.py:505
  89.5 1.7 %collective-permute-start.15 = (bf16[128,512]{1,0:T(8,128)(2,1)}, bf16[128,512]{1,0:T(8,128)(2,1)S(1)}, u32[]{:S(2)}, u32[]{:S(2)}) collective-permute-start(bf16[128,512]{1,0:T(8,128)(2,1)} %get-tuple-element.50), channel_id=1, source_target_pairs={{0,5},{1,4},{2,7},{3,6},{4,1},{5,0},{6,3},{7,2},{8,13},{9,12},{10,... | collective-permute-start | bytes 393224 | tf_op jit(solution)/shard_map/ppermute | solution.py:505
  91.3 0.0 all-to-all-done.1.states
  91.3 6.9 %all-to-all-start.2 = ((bf16[16,128,128]{2,1,0:T(8,128)(2,1)}), bf16[16,128,128]{2,1,0:T(8,128)(2,1)S(1)}, u32[]{:S(2)}, u32[]{:S(2)}) async-start(bf16[16,128,128]{2,1,0:T(8,128)(2,1)} %get-tuple-element.37), calls=%async_computation.2 | async-start | bytes 1048576 | tf_op jit(solution)/shard_map/all_to_all | solution.py:555
  98.2 1.4 %collective-permute-start.16 = (bf16[128,512]{1,0:T(8,128)(2,1)}, bf16[128,512]{1,0:T(8,128)(2,1)S(1)}, u32[]{:S(2)}, u32[]{:S(2)}) collective-permute-start(bf16[128,512]{1,0:T(8,128)(2,1)} %get-tuple-element.51), channel_id=1, source_target_pairs={{0,6},{1,7},{2,4},{3,5},{4,2},{5,3},{6,0},{7,1},{8,14},{9,15},{10,... | collective-permute-start | bytes 393224 | tf_op jit(solution)/shard_map/ppermute | solution.py:505
  99.6 1.9 %collective-permute-start.17 = (bf16[128,512]{1,0:T(8,128)(2,1)}, bf16[128,512]{1,0:T(8,128)(2,1)S(1)}, u32[]{:S(2)}, u32[]{:S(2)}) collective-permute-start(bf16[128,512]{1,0:T(8,128)(2,1)} %get-tuple-element.52), channel_id=1, source_target_pairs={{0,7},{1,6},{2,5},{3,4},{4,3},{5,2},{6,1},{7,0},{8,15},{9,14},{10,... | collective-permute-start | bytes 393224 | tf_op jit(solution)/shard_map/ppermute | solution.py:505
  101.5 1.6 %copy-done.12 = bf16[16,512,128]{2,1,0:T(8,128)(2,1)S(1)} copy-done((bf16[16,512,128]{2,1,0:T(8,128)(2,1)S(1)}, bf16[16,512,128]{2,1,0:T(8,128)(2,1)}, u32[]{:S(2)}) %copy-start.12) | copy-done | bytes 2097176
  103.1 1.6 %copy-done.13 = bf16[16,512,128]{2,1,0:T(8,128)(2,1)S(1)} copy-done((bf16[16,512,128]{2,1,0:T(8,128)(2,1)S(1)}, bf16[16,512,128]{2,1,0:T(8,128)(2,1)}, u32[]{:S(2)}) %copy-start.13) | copy-done | bytes 2097176
  104.7 0.8 copy-done.14
  105.4 12.7 %ssd_grad.1 = (bf16[512,16,128]{2,1,0:T(8,128)(2,1)}, f32[16,512]{1,0:T(8,128)}, f32[512,128]{1,0:T(8,128)}, f32[512,128]{1,0:T(8,128)}) custom-call(bf16[16,512,128]{2,1,0:T(8,128)(2,1)S(1)} %copy-done.12, bf16[16,512,128]{2,1,0:T(8,128)(2,1)S(1)} %copy-done.13, bf16[16,256,128]{2,1,0:T(8,128)(2,1)S(1)} %all-to-all-done.1.states, f32[16,512]{1,0:T(8,128)S(1)} %copy-done.14, ...), custom_call_target="tpu_custom_call" | custom-call | flops 6000000000 | bytes 10000000 | tf_op jit(solution)/shard_map/ssd_grad/pallas_call | solution.py:442
  118.1 0.1 reduce_sum.12.refs_8_
  118.2 0.0 collective-permute-done.13.refs_3_
  118.3 1.2 collective-permute-start.24
  119.4 0.0 collective-permute-done.14.refs_4_
  119.4 1.4 %collective-permute-start.23 = (bf16[128,128]{1,0:T(8,128)(2,1)S(1)}, bf16[128,128]{1,0:T(8,128)(2,1)S(1)}, u32[]{:S(2)}, u32[]{:S(2)}) collective-permute-start(bf16[128,128]{1,0:T(8,128)(2,1)S(1)} %reduce_sum.12.refs_8_), channel_id=1, source_target_pairs={{0,6},{1,7},{2,4},{3,5},{4,2},{5,3},{6,0},{7,1},{8,14},{9,15},{10,... | collective-permute-start | bytes 98312 | tf_op jit(solution)/shard_map/ppermute | solution.py:505
  120.8 3.7 %collective-permute-start.21 = (bf16[128,128]{1,0:T(8,128)(2,1)S(1)}, bf16[128,128]{1,0:T(8,128)(2,1)S(1)}, u32[]{:S(2)}, u32[]{:S(2)}) collective-permute-start(bf16[128,128]{1,0:T(8,128)(2,1)S(1)} %reduce_sum.12.refs_8_), channel_id=1, source_target_pairs={{0,4},{1,5},{2,6},{3,7},{4,0},{5,1},{6,2},{7,3},{8,12},{9,13},{10,... | collective-permute-start | bytes 98312 | tf_op jit(solution)/shard_map/ppermute | solution.py:505
  124.6 1.2 collective-permute-start.19
  125.8 0.9 collective-permute-start.18
  126.7 0.1 collective-permute-done.21.refs_12_
  126.8 1.1 collective-permute-done.20.refs_11_
  128.0 0.5 copy-done.27
  128.5 0.0 copy-done.28
  128.5 0.0 copy-done.29
  128.6 2.2 %finish.1 = (bf16[512,128]{1,0:T(8,128)(2,1)}, bf16[512,128]{1,0:T(8,128)(2,1)}, bf16[512,128]{1,0:T(8,128)(2,1)}) custom-call(bf16[128,512]{1,0:T(8,128)(2,1)} %get-tuple-element.45.refs_0_, bf16[128,512]{1,0:T(8,128)(2,1)} %copy-done.15, bf16[128,512]{1,0:T(8,128)(2,1)} %copy-done.16, bf16[128,512]{1,0:T(8,128)(2,1)} %copy-done.17, ...), custom_call_target="tpu_custom_call" | custom-call | tf_op jit(solution)/shard_map/finish/pallas_call | solution.py:495
  (60 shorter events, 0.1 us)
Async XLA Ops:
  8.9 8.8 %copy-start.4 = (bf16[2,512,128]{2,1,0:T(8,128)(2,1)S(1)}, bf16[2,512,128]{2,1,0:T(8,128)(2,1)}, u32[]{:S(2)}) copy-start(bf16[2,512,128]{2,1,0:T(8,128)(2,1)} %get-tuple-element.34.refs_0_) | copy-start | bytes 786436
  8.9 36.5 %all-to-all-start = ((bf16[16,400,128]{2,1,0:T(8,128)(2,1)}), bf16[16,400,128]{2,1,0:T(8,128)(2,1)S(1)}, u32[]{:S(2)}, u32[]{:S(2)}) async-start(bf16[16,400,128]{2,1,0:T(8,128)(2,1)} %get-tuple-element.33), calls=%async_computation | async-start | bytes 3276800 | tf_op jit(solution)/shard_map/all_to_all | solution.py:546
  17.6 36.0 %copy-start.11 = (s32[16]{0:T(128)S(1)}, s32[16]{0:T(128)}, u32[]{:S(2)}) copy-start(s32[16]{0:T(128)} %order.3) | copy-start | bytes 196
  17.6 21.6 %collective-permute-start.6 = (bf16[2,512,128]{2,1,0:T(8,128)(2,1)S(1)}, bf16[2,512,128]{2,1,0:T(8,128)(2,1)S(1)}, u32[]{:S(2)}, u32[]{:S(2)}) collective-permute-start(bf16[2,512,128]{2,1,0:T(8,128)(2,1)S(1)} %copy-done.4), channel_id=1, source_target_pairs={{0,7},{1,6},{2,5},{3,4},{4,3},{5,2},{6,1},{7,0},{8,15},{9,14},{10,... | collective-permute-start | bytes 786440 | tf_op jit(solution)/shard_map/ppermute | solution.py:505
  21.0 23.8 %collective-permute-start.5 = (bf16[2,512,128]{2,1,0:T(8,128)(2,1)S(1)}, bf16[2,512,128]{2,1,0:T(8,128)(2,1)S(1)}, u32[]{:S(2)}, u32[]{:S(2)}) collective-permute-start(bf16[2,512,128]{2,1,0:T(8,128)(2,1)S(1)} %copy-done.4), channel_id=1, source_target_pairs={{0,6},{1,7},{2,4},{3,5},{4,2},{5,3},{6,0},{7,1},{8,14},{9,15},{10,... | collective-permute-start | bytes 786440 | tf_op jit(solution)/shard_map/ppermute | solution.py:505
  21.2 32.3 %collective-permute-start.4 = (bf16[2,512,128]{2,1,0:T(8,128)(2,1)S(1)}, bf16[2,512,128]{2,1,0:T(8,128)(2,1)}, u32[]{:S(2)}, u32[]{:S(2)}) collective-permute-start(bf16[2,512,128]{2,1,0:T(8,128)(2,1)S(1)} %copy-done.4), channel_id=1, source_target_pairs={{0,5},{1,4},{2,7},{3,6},{4,1},{5,0},{6,3},{7,2},{8,13},{9,12},{10,... | collective-permute-start | bytes 786440 | tf_op jit(solution)/shard_map/ppermute | solution.py:505
  22.5 31.1 %collective-permute-start.3 = (bf16[2,512,128]{2,1,0:T(8,128)(2,1)S(1)}, bf16[2,512,128]{2,1,0:T(8,128)(2,1)}, u32[]{:S(2)}, u32[]{:S(2)}) collective-permute-start(bf16[2,512,128]{2,1,0:T(8,128)(2,1)S(1)} %copy-done.4), channel_id=1, source_target_pairs={{0,4},{1,5},{2,6},{3,7},{4,0},{5,1},{6,2},{7,3},{8,12},{9,13},{10,... | collective-permute-start | bytes 786440 | tf_op jit(solution)/shard_map/ppermute | solution.py:505
  24.4 29.2 %collective-permute-start.2 = (bf16[2,512,128]{2,1,0:T(8,128)(2,1)S(1)}, bf16[2,512,128]{2,1,0:T(8,128)(2,1)}, u32[]{:S(2)}, u32[]{:S(2)}) collective-permute-start(bf16[2,512,128]{2,1,0:T(8,128)(2,1)S(1)} %copy-done.4), channel_id=1, source_target_pairs={{0,3},{1,2},{2,1},{3,0},{4,7},{5,6},{6,5},{7,4},{8,11},{9,10},{10,... | collective-permute-start | bytes 786440 | tf_op jit(solution)/shard_map/ppermute | solution.py:505
  39.2 7.4 %copy-start.5 = (bf16[2,512,128]{2,1,0:T(8,128)(2,1)}, bf16[2,512,128]{2,1,0:T(8,128)(2,1)S(1)}, u32[]{:S(2)}) copy-start(bf16[2,512,128]{2,1,0:T(8,128)(2,1)S(1)} %collective-permute-done.6.refs_7_) | copy-start | bytes 786436
  39.2 14.4 %collective-permute-start.1 = (bf16[2,512,128]{2,1,0:T(8,128)(2,1)S(1)}, bf16[2,512,128]{2,1,0:T(8,128)(2,1)}, u32[]{:S(2)}, u32[]{:S(2)}) collective-permute-start(bf16[2,512,128]{2,1,0:T(8,128)(2,1)S(1)} %copy-done.4), channel_id=1, source_target_pairs={{0,2},{1,3},{2,0},{3,1},{4,6},{5,7},{6,4},{7,5},{8,10},{9,11},{10,... | collective-permute-start | bytes 786440 | tf_op jit(solution)/shard_map/ppermute | solution.py:505
  44.9 1.8 %copy-start.8 = (bf16[2,512,128]{2,1,0:T(8,128)(2,1)}, bf16[2,512,128]{2,1,0:T(8,128)(2,1)S(1)}, u32[]{:S(2)}) copy-start(bf16[2,512,128]{2,1,0:T(8,128)(2,1)S(1)} %collective-permute-done.5.refs_6_) | copy-start | bytes 786436
  44.9 8.8 %collective-permute-start = (bf16[2,512,128]{2,1,0:T(8,128)(2,1)S(1)}, bf16[2,512,128]{2,1,0:T(8,128)(2,1)}, u32[]{:S(2)}, u32[]{:S(2)}) collective-permute-start(bf16[2,512,128]{2,1,0:T(8,128)(2,1)S(1)} %copy-done.4), channel_id=1, source_target_pairs={{0,1},{1,0},{2,3},{3,2},{4,5},{5,4},{6,7},{7,6},{8,9},{9,8},{10,11... | collective-permute-start | bytes 786440 | tf_op jit(solution)/shard_map/ppermute | solution.py:505
  46.6 44.6 %all-to-all-start.1 = ((bf16[16,256,128]{2,1,0:T(8,128)(2,1)}), bf16[16,256,128]{2,1,0:T(8,128)(2,1)S(1)}, u32[]{:S(2)}, u32[]{:S(2)}) async-start(bf16[16,256,128]{2,1,0:T(8,128)(2,1)} %scan.1), calls=%async_computation.1 | async-start | bytes 2097152 | tf_op jit(solution)/shard_map/all_to_all | solution.py:549
  53.6 1.0 copy-start.6
  54.6 0.9 copy-start.9
  55.5 46.0 %copy-start.2 = (f32[512,1,128]{2,1,0:T(1,128)S(1)}, f32[512,1,128]{2,1,0:T(1,128)}, u32[]{:S(2)}) copy-start(f32[512,1,128]{2,1,0:T(1,128)} %param.12) | copy-start | bytes 786436
  55.5 46.0 %copy-start.3 = (f32[512,1,128]{2,1,0:T(1,128)S(1)}, f32[512,1,128]{2,1,0:T(1,128)}, u32[]{:S(2)}) copy-start(f32[512,1,128]{2,1,0:T(1,128)} %param.13) | copy-start | bytes 786436
  61.6 1.5 %copy-start.1 = (f32[3,8,512]{2,1,0:T(8,128)}, f32[3,8,512]{2,1,0:T(8,128)S(1)}, u32[]{:S(2)}) copy-start(f32[3,8,512]{2,1,0:T(8,128)S(1)} %attn_stat.1.a) | copy-start | bytes 147460
  61.6 1.4 %collective-permute-start.7 = (f32[3,8,512]{2,1,0:T(8,128)S(1)}, f32[3,8,512]{2,1,0:T(8,128)}, u32[]{:S(2)}, u32[]{:S(2)}) collective-permute-start(f32[3,8,512]{2,1,0:T(8,128)S(1)} %attn_stat.1.a), channel_id=1, source_target_pairs={{0,1},{1,0},{2,3},{3,2},{4,5},{5,4},{6,7},{7,6},{8,9},{9,8},{10,11... | collective-permute-start | bytes 147464 | tf_op jit(solution)/shard_map/ppermute | solution.py:505
  64.5 4.7 %collective-permute-start.10 = (f32[3,8,512]{2,1,0:T(8,128)}, f32[3,8,512]{2,1,0:T(8,128)S(1)}, u32[]{:S(2)}, u32[]{:S(2)}) collective-permute-start(f32[3,8,512]{2,1,0:T(8,128)} %join.1.refs_8_), channel_id=1, source_target_pairs={{0,4},{1,5},{2,6},{3,7},{4,0},{5,1},{6,2},{7,3},{8,12},{9,13},{10,... | collective-permute-start | bytes 147464 | tf_op jit(solution)/shard_map/ppermute | solution.py:505
  65.7 5.1 %collective-permute-start.9 = (f32[3,8,512]{2,1,0:T(8,128)}, f32[3,8,512]{2,1,0:T(8,128)S(1)}, u32[]{:S(2)}, u32[]{:S(2)}) collective-permute-start(f32[3,8,512]{2,1,0:T(8,128)} %join.1.refs_8_), channel_id=1, source_target_pairs={{0,6},{1,7},{2,4},{3,5},{4,2},{5,3},{6,0},{7,1},{8,14},{9,15},{10,... | collective-permute-start | bytes 147464 | tf_op jit(solution)/shard_map/ppermute | solution.py:505
  67.0 3.7 %collective-permute-start.8 = (f32[3,8,512]{2,1,0:T(8,128)}, f32[3,8,512]{2,1,0:T(8,128)S(1)}, u32[]{:S(2)}, u32[]{:S(2)}) collective-permute-start(f32[3,8,512]{2,1,0:T(8,128)} %join.1.refs_8_), channel_id=1, source_target_pairs={{0,2},{1,3},{2,0},{3,1},{4,6},{5,7},{6,4},{7,5},{8,10},{9,11},{10,... | collective-permute-start | bytes 147464 | tf_op jit(solution)/shard_map/ppermute | solution.py:505
  70.8 0.8 copy-start
  71.6 0.9 copy-start.7
  72.5 0.9 copy-start.10
  84.7 13.5 %collective-permute-start.11 = (bf16[128,512]{1,0:T(8,128)(2,1)}, bf16[128,512]{1,0:T(8,128)(2,1)S(1)}, u32[]{:S(2)}, u32[]{:S(2)}) collective-permute-start(bf16[128,512]{1,0:T(8,128)(2,1)} %get-tuple-element.46), channel_id=1, source_target_pairs={{0,1},{1,0},{2,3},{3,2},{4,5},{5,4},{6,7},{7,6},{8,9},{9,8},{10,11... | collective-permute-start | bytes 393224 | tf_op jit(solution)/shard_map/ppermute | solution.py:505
  86.2 13.4 %collective-permute-start.12 = (bf16[128,512]{1,0:T(8,128)(2,1)}, bf16[128,512]{1,0:T(8,128)(2,1)S(1)}, u32[]{:S(2)}, u32[]{:S(2)}) collective-permute-start(bf16[128,512]{1,0:T(8,128)(2,1)} %get-tuple-element.47), channel_id=1, source_target_pairs={{0,2},{1,3},{2,0},{3,1},{4,6},{5,7},{6,4},{7,5},{8,10},{9,11},{10,... | collective-permute-start | bytes 393224 | tf_op jit(solution)/shard_map/ppermute | solution.py:505
  86.3 31.9 %collective-permute-start.13 = (bf16[128,512]{1,0:T(8,128)(2,1)}, bf16[128,512]{1,0:T(8,128)(2,1)S(1)}, u32[]{:S(2)}, u32[]{:S(2)}) collective-permute-start(bf16[128,512]{1,0:T(8,128)(2,1)} %get-tuple-element.48), channel_id=1, source_target_pairs={{0,3},{1,2},{2,1},{3,0},{4,7},{5,6},{6,5},{7,4},{8,11},{9,10},{10,... | collective-permute-start | bytes 393224 | tf_op jit(solution)/shard_map/ppermute | solution.py:505
  88.0 31.5 %collective-permute-start.14 = (bf16[128,512]{1,0:T(8,128)(2,1)}, bf16[128,512]{1,0:T(8,128)(2,1)S(1)}, u32[]{:S(2)}, u32[]{:S(2)}) collective-permute-start(bf16[128,512]{1,0:T(8,128)(2,1)} %get-tuple-element.49), channel_id=1, source_target_pairs={{0,4},{1,5},{2,6},{3,7},{4,0},{5,1},{6,2},{7,3},{8,12},{9,13},{10,... | collective-permute-start | bytes 393224 | tf_op jit(solution)/shard_map/ppermute | solution.py:505
  89.5 31.3 %collective-permute-start.15 = (bf16[128,512]{1,0:T(8,128)(2,1)}, bf16[128,512]{1,0:T(8,128)(2,1)S(1)}, u32[]{:S(2)}, u32[]{:S(2)}) collective-permute-start(bf16[128,512]{1,0:T(8,128)(2,1)} %get-tuple-element.50), channel_id=1, source_target_pairs={{0,5},{1,4},{2,7},{3,6},{4,1},{5,0},{6,3},{7,2},{8,13},{9,12},{10,... | collective-permute-start | bytes 393224 | tf_op jit(solution)/shard_map/ppermute | solution.py:505
  91.3 26.9 %all-to-all-start.2 = ((bf16[16,128,128]{2,1,0:T(8,128)(2,1)}), bf16[16,128,128]{2,1,0:T(8,128)(2,1)S(1)}, u32[]{:S(2)}, u32[]{:S(2)}) async-start(bf16[16,128,128]{2,1,0:T(8,128)(2,1)} %get-tuple-element.37), calls=%async_computation.2 | async-start | bytes 1048576 | tf_op jit(solution)/shard_map/all_to_all | solution.py:555
  98.2 19.9 %copy-start.15 = (bf16[128,512]{1,0:T(8,128)(2,1)}, bf16[128,512]{1,0:T(8,128)(2,1)S(1)}, u32[]{:S(2)}) copy-start(bf16[128,512]{1,0:T(8,128)(2,1)S(1)} %collective-permute-done.11.refs_1_) | copy-start | bytes 393220
  98.2 22.6 %collective-permute-start.16 = (bf16[128,512]{1,0:T(8,128)(2,1)}, bf16[128,512]{1,0:T(8,128)(2,1)S(1)}, u32[]{:S(2)}, u32[]{:S(2)}) collective-permute-start(bf16[128,512]{1,0:T(8,128)(2,1)} %get-tuple-element.51), channel_id=1, source_target_pairs={{0,6},{1,7},{2,4},{3,5},{4,2},{5,3},{6,0},{7,1},{8,14},{9,15},{10,... | collective-permute-start | bytes 393224 | tf_op jit(solution)/shard_map/ppermute | solution.py:505
  99.6 18.5 %copy-start.16 = (bf16[128,512]{1,0:T(8,128)(2,1)}, bf16[128,512]{1,0:T(8,128)(2,1)S(1)}, u32[]{:S(2)}) copy-start(bf16[128,512]{1,0:T(8,128)(2,1)S(1)} %collective-permute-done.12.refs_2_) | copy-start | bytes 393220
  99.6 24.9 %collective-permute-start.17 = (bf16[128,512]{1,0:T(8,128)(2,1)}, bf16[128,512]{1,0:T(8,128)(2,1)S(1)}, u32[]{:S(2)}, u32[]{:S(2)}) collective-permute-start(bf16[128,512]{1,0:T(8,128)(2,1)} %get-tuple-element.52), channel_id=1, source_target_pairs={{0,7},{1,6},{2,5},{3,4},{4,3},{5,2},{6,1},{7,0},{8,15},{9,14},{10,... | collective-permute-start | bytes 393224 | tf_op jit(solution)/shard_map/ppermute | solution.py:505
  101.5 1.6 %copy-start.12 = (bf16[16,512,128]{2,1,0:T(8,128)(2,1)S(1)}, bf16[16,512,128]{2,1,0:T(8,128)(2,1)}, u32[]{:S(2)}) copy-start(bf16[16,512,128]{2,1,0:T(8,128)(2,1)} %get-tuple-element.38.xh) | copy-start | bytes 6291460
  103.1 1.6 %copy-start.13 = (bf16[16,512,128]{2,1,0:T(8,128)(2,1)S(1)}, bf16[16,512,128]{2,1,0:T(8,128)(2,1)}, u32[]{:S(2)}) copy-start(bf16[16,512,128]{2,1,0:T(8,128)(2,1)} %get-tuple-element.39.yh) | copy-start | bytes 6291460
  104.7 0.8 copy-start.14
  118.2 9.7 %copy-start.22 = (bf16[128,128]{1,0:T(8,128)(2,1)}, bf16[128,128]{1,0:T(8,128)(2,1)S(1)}, u32[]{:S(2)}) copy-start(bf16[128,128]{1,0:T(8,128)(2,1)S(1)} %reduce_sum.12.refs_8_) | copy-start | bytes 98308
  118.2 9.7 %copy-start.17 = (bf16[128,512]{1,0:T(8,128)(2,1)}, bf16[128,512]{1,0:T(8,128)(2,1)S(1)}, u32[]{:S(2)}) copy-start(bf16[128,512]{1,0:T(8,128)(2,1)S(1)} %collective-permute-done.13.refs_3_) | copy-start | bytes 393220
  118.3 6.3 %collective-permute-start.24 = (bf16[128,128]{1,0:T(8,128)(2,1)S(1)}, bf16[128,128]{1,0:T(8,128)(2,1)S(1)}, u32[]{:S(2)}, u32[]{:S(2)}) collective-permute-start(bf16[128,128]{1,0:T(8,128)(2,1)S(1)} %reduce_sum.12.refs_8_), channel_id=1, source_target_pairs={{0,7},{1,6},{2,5},{3,4},{4,3},{5,2},{6,1},{7,0},{8,15},{9,14},{10,... | collective-permute-start | bytes 98312 | tf_op jit(solution)/shard_map/ppermute | solution.py:505
  119.4 8.5 %copy-start.18 = (bf16[128,512]{1,0:T(8,128)(2,1)}, bf16[128,512]{1,0:T(8,128)(2,1)S(1)}, u32[]{:S(2)}) copy-start(bf16[128,512]{1,0:T(8,128)(2,1)S(1)} %collective-permute-done.14.refs_4_) | copy-start | bytes 393220
  119.4 6.4 %collective-permute-start.23 = (bf16[128,128]{1,0:T(8,128)(2,1)S(1)}, bf16[128,128]{1,0:T(8,128)(2,1)S(1)}, u32[]{:S(2)}, u32[]{:S(2)}) collective-permute-start(bf16[128,128]{1,0:T(8,128)(2,1)S(1)} %reduce_sum.12.refs_8_), channel_id=1, source_target_pairs={{0,6},{1,7},{2,4},{3,5},{4,2},{5,3},{6,0},{7,1},{8,14},{9,15},{10,... | collective-permute-start | bytes 98312 | tf_op jit(solution)/shard_map/ppermute | solution.py:505
  120.8 7.2 %copy-start.19 = (bf16[128,512]{1,0:T(8,128)(2,1)}, bf16[128,512]{1,0:T(8,128)(2,1)S(1)}, u32[]{:S(2)}) copy-start(bf16[128,512]{1,0:T(8,128)(2,1)S(1)} %collective-permute-done.15.refs_5_) | copy-start | bytes 393220
  120.8 5.9 %collective-permute-start.22 = (bf16[128,128]{1,0:T(8,128)(2,1)S(1)}, bf16[128,128]{1,0:T(8,128)(2,1)S(1)}, u32[]{:S(2)}, u32[]{:S(2)}) collective-permute-start(bf16[128,128]{1,0:T(8,128)(2,1)S(1)} %reduce_sum.12.refs_8_), channel_id=1, source_target_pairs={{0,5},{1,4},{2,7},{3,6},{4,1},{5,0},{6,3},{7,2},{8,13},{9,12},{10,... | collective-permute-start | bytes 98312 | tf_op jit(solution)/shard_map/ppermute | solution.py:505
  120.8 7.2 %copy-start.20 = (bf16[128,512]{1,0:T(8,128)(2,1)}, bf16[128,512]{1,0:T(8,128)(2,1)S(1)}, u32[]{:S(2)}) copy-start(bf16[128,512]{1,0:T(8,128)(2,1)S(1)} %collective-permute-done.16.refs_6_) | copy-start | bytes 393220
  120.8 6.0 %collective-permute-start.21 = (bf16[128,128]{1,0:T(8,128)(2,1)S(1)}, bf16[128,128]{1,0:T(8,128)(2,1)S(1)}, u32[]{:S(2)}, u32[]{:S(2)}) collective-permute-start(bf16[128,128]{1,0:T(8,128)(2,1)S(1)} %reduce_sum.12.refs_8_), channel_id=1, source_target_pairs={{0,4},{1,5},{2,6},{3,7},{4,0},{5,1},{6,2},{7,3},{8,12},{9,13},{10,... | collective-permute-start | bytes 98312 | tf_op jit(solution)/shard_map/ppermute | solution.py:505
  124.6 3.4 %copy-start.21 = (bf16[128,512]{1,0:T(8,128)(2,1)}, bf16[128,512]{1,0:T(8,128)(2,1)S(1)}, u32[]{:S(2)}) copy-start(bf16[128,512]{1,0:T(8,128)(2,1)S(1)} %collective-permute-done.17.refs_7_) | copy-start | bytes 393220
  124.6 3.3 %collective-permute-start.20 = (bf16[128,128]{1,0:T(8,128)(2,1)S(1)}, bf16[128,128]{1,0:T(8,128)(2,1)S(1)}, u32[]{:S(2)}, u32[]{:S(2)}) collective-permute-start(bf16[128,128]{1,0:T(8,128)(2,1)S(1)} %reduce_sum.12.refs_8_), channel_id=1, source_target_pairs={{0,3},{1,2},{2,1},{3,0},{4,7},{5,6},{6,5},{7,4},{8,11},{9,10},{10,... | collective-permute-start | bytes 98312 | tf_op jit(solution)/shard_map/ppermute | solution.py:505
  124.6 3.4 %copy-start.23 = (bf16[128,128]{1,0:T(8,128)(2,1)}, bf16[128,128]{1,0:T(8,128)(2,1)S(1)}, u32[]{:S(2)}) copy-start(bf16[128,128]{1,0:T(8,128)(2,1)S(1)} %collective-permute-done.24.refs_15_) | copy-start | bytes 98308
  124.6 3.3 %collective-permute-start.19 = (bf16[128,128]{1,0:T(8,128)(2,1)S(1)}, bf16[128,128]{1,0:T(8,128)(2,1)S(1)}, u32[]{:S(2)}, u32[]{:S(2)}) collective-permute-start(bf16[128,128]{1,0:T(8,128)(2,1)S(1)} %reduce_sum.12.refs_8_), channel_id=1, source_target_pairs={{0,2},{1,3},{2,0},{3,1},{4,6},{5,7},{6,4},{7,5},{8,10},{9,11},{10,... | collective-permute-start | bytes 98312 | tf_op jit(solution)/shard_map/ppermute | solution.py:505
  125.8 2.2 %copy-start.24 = (bf16[128,128]{1,0:T(8,128)(2,1)}, bf16[128,128]{1,0:T(8,128)(2,1)S(1)}, u32[]{:S(2)}) copy-start(bf16[128,128]{1,0:T(8,128)(2,1)S(1)} %collective-permute-done.23.refs_14_) | copy-start | bytes 98308
  125.8 2.1 %collective-permute-start.18 = (bf16[128,128]{1,0:T(8,128)(2,1)S(1)}, bf16[128,128]{1,0:T(8,128)(2,1)S(1)}, u32[]{:S(2)}, u32[]{:S(2)}) collective-permute-start(bf16[128,128]{1,0:T(8,128)(2,1)S(1)} %reduce_sum.12.refs_8_), channel_id=1, source_target_pairs={{0,1},{1,0},{2,3},{3,2},{4,5},{5,4},{6,7},{7,6},{8,9},{9,8},{10,11... | collective-permute-start | bytes 98312 | tf_op jit(solution)/shard_map/ppermute | solution.py:505
  126.7 1.3 copy-start.25
  126.8 1.2 copy-start.26
  127.9 0.6 copy-start.27
  127.9 0.6 copy-start.28
  127.9 0.6 copy-start.29

commit v5 on v4

--- a/solution.py
+++ b/solution.py
@@ -195,7 +195,7 @@
 
 
 def attn_stat_kernel(order, recv, *refs):
-    qd, (stat, ks, vs, inverse) = refs[:8], refs[8:]
+    qd, (stat, mate, ks, vs, inverse) = refs[:8], refs[8:]
     heads = len(qd)
     scale = LOG2E * 128**-0.5
     sort_keys(order, inverse, recv, ks, vs)
@@ -220,6 +220,8 @@
         return carry
 
     lax.fori_loop(0, 5, item, 0)
+    for i in range(3):
+        mate[i] = turn_rows(stat[i], 1)
 
 
 def attn_stat(order, recv, qd):
@@ -227,8 +229,8 @@
     return pl.pallas_call(
         attn_stat_kernel,
         in_specs=[SM] + [VM] * 9,
-        out_specs=VM,
-        out_shape=jax.ShapeDtypeStruct((3, heads, 512), F32),
+        out_specs=[VM, VM],
+        out_shape=[jax.ShapeDtypeStruct((3, heads, 512), F32)] * 2,
         scratch_shapes=[
             pltpu.VMEM((1024, 128), BF),
             pltpu.VMEM((1024, 128), BF),
@@ -469,7 +471,7 @@
             pltpu.VMEM((heads, tok), F32),
             pltpu.VMEM((tok * heads, width), F32),
         ],
-        compiler_params=pltpu.CompilerParams(vmem_limit_bytes=48 << 20),
+        compiler_params=pltpu.CompilerParams(vmem_limit_bytes=60 << 20),
         cost_estimate=pl.CostEstimate(
             flops=6 * 10**9, bytes_accessed=10**7, transcendentals=10**6
         ),
@@ -478,7 +480,7 @@
 
 
 def finish_kernel(*refs):
-    dqt, parts, (dq, dk, dv) = refs[:8], refs[8:16], refs[16:]
+    dqt, parts, (dq, dk, dv) = refs[:4], refs[4:12], refs[12:]
     total = functools.reduce(jnp.add, [r[...].astype(F32) for r in dqt])
     dq[...] = total.T.astype(BF)
     place = lax.axis_index("head")
@@ -494,9 +496,10 @@
     out = jax.ShapeDtypeStruct((512, 128), BF)
     return pl.pallas_call(
         finish_kernel,
-        in_specs=[VM] * 16,
+        in_specs=[VM] * 12,
         out_specs=[VM, VM, VM],
         out_shape=[out, out, out],
+        compiler_params=pltpu.CompilerParams(vmem_limit_bytes=16 << 20),
         name="finish",
     )(*dqt, *parts)
 
@@ -509,23 +512,26 @@
     return jnp.concatenate([v[j ^ m : (j ^ m) + 1] for j in range(v.shape[0])], axis=0)
 
 
-def join_kernel(a, b, o):
-    other = [turn_rows(b[i], 1) for i in range(3)]
-    top = jnp.maximum(a[0], other[0])
-    f, g = jnp.exp2(a[0] - top), jnp.exp2(other[0] - top)
-    o[0] = top
-    o[1] = f * a[1] + g * other[1]
-    o[2] = f * a[2] + g * other[2]
-
-
 def join(a, b):
-    return pl.pallas_call(
-        join_kernel,
-        in_specs=[VM, VM],
-        out_specs=VM,
-        out_shape=jax.ShapeDtypeStruct(a.shape, F32),
-        name="join",
-    )(a, b)
+    top = jnp.maximum(a[0], b[0])
+    f, g = jnp.exp2(a[0] - top), jnp.exp2(b[0] - top)
+    return jnp.stack([top, f * a[1] + g * b[1], f * a[2] + g * b[2]])
+
+
+def gather_heads(v):
+    out = [v] + [None] * 7
+    for m in (2, 6, 4):
+        out[m] = swap(v, m)
+    for m in (0, 2, 6, 4):
+        out[m + 1] = swap(out[m], 1)
+    return out
+
+
+def pair_sums(parts):
+    return [
+        (parts[m].astype(F32) + swap(parts[m + 1], 1).astype(F32)).astype(BF)
+        for m in (0, 2, 4, 6)
+    ]
 
 
 def after(value, other):
@@ -544,18 +550,19 @@
         queries.reshape(tok, 128), attn_cotangent.reshape(tok, 128),
     )
     recv = lax.all_to_all(send, "seq", 0, 0)
-    qds = [qd] + [swap(qd, m) for m in range(1, 8)]
+    qds = gather_heads(qd)
     turned = scan(recv)
     states = lax.all_to_all(turned, "seq", 0, 0)
-    first = attn_stat(pair_order, after(recv, turned), qds)
-    stat = join(first, swap(first, 1))
-    back, *dqt = attn_grad(pair_order, recv, qds, stat, *[swap(stat, m) for m in (2, 6, 4)])
-    back = after(back, states)
-    dx, da, db, dc = ssd_grad(after(xh, back), yh, states, cum, b, c)
+    first, mate = attn_stat(pair_order, after(recv, turned), qds)
+    stat = join(first, swap(mate, 1))
+    rest = [swap(stat, m) for m in (2, 6, 4)]
+    back, *dqt = attn_grad(pair_order, after(recv, states), qds, stat, *rest)
+    pair = pair_sums(dqt)
+    dx, da, db, dc = ssd_grad(after(xh, (back, *pair)), yh, states, cum, b, c)
     back = lax.all_to_all(back, "seq", 0, 0)
-    dqt = [dqt[0]] + [swap(dqt[m], m) for m in range(1, 8)]
+    dqt = [pair[0]] + [swap(pair[i], m) for i, m in ((1, 2), (3, 6), (2, 4))]
     dkv = jnp.sum(after(back, da).astype(F32), axis=0).astype(BF)
-    parts = [dkv] + [swap(dkv, m) for m in range(1, 8)]
+    parts = gather_heads(dkv)
     dq, dk, dv = finish(dqt, parts)
     return (
         dx,

time: 132 us -> 117 us (0.89)
  local copies, waits for them, and re-layouts: 9.14 us -> 0.02 us
  waiting for transfers between devices: 25.7 us -> 21.6 us
  other arithmetic: 0.08 us -> 2.97 us
  starting transfers between devices: 51.7 us -> 49.4 us
    ppermute x25, waiting for transfers between devices: 25.7 us -> 11.8 us  [swap(): return lax.ppermute(v, 'head', [(i, i ^ m) for i in range(8)])]
    unnamed x60 -> x6, local copies, waits for them, and re-layouts: 9.14 us -> 0.02 us
    all_to_all x1, waiting for transfers between devices: 0.01 us -> 7.52 us  [per_device(): recv = lax.all_to_all(send, 'seq', 0, 0)]
    pallas_call x3 -> x2, Pallas kernels: 9.76 us -> 6.62 us  [the longest x1 5.81 us: attn_stat(): pl.pallas_call(attn_stat_kernel, in_specs=[SM] + [VM] * 9, out_specs=[VM,...]
    convert_element_type x0 -> x4, other arithmetic: none -> 2.85 us  [pair_sums(): (parts[m].astype(F32) + swap(parts[m + 1], 1).astype(F32)).astype(BF)]
    all_to_all x1, starting transfers between devices: 6.94 us -> 4.62 us  [per_device(): states = lax.all_to_all(turned, 'seq', 0, 0)]
    all_to_all x1, waiting for transfers between devices: 0.01 us -> 2.25 us  [per_device(): states = lax.all_to_all(turned, 'seq', 0, 0)]
    pallas_call x1, Pallas kernels: 12.7 us -> 14.9 us  [ssd_grad(): pl.pallas_call(ssd_grad_kernel, grid=(heads // 8,), in_specs=[per, per, p...]
  transfers between devices with their start and end apart: 28 -> 28, of which waited for: 7 -> 7; matrix products, arithmetic and copies ran while one was open for 0% -> 3% of each run, Pallas kernels for 25% -> 19%
where the time goes in v5:
time: 117 us
  starting transfers between devices  49.4 us (42%)
  Pallas kernels  42 us (36%)
  waiting for transfers between devices  21.6 us (18%)
  other arithmetic  2.97 us (3%)
    ppermute x25, starting transfers between devices, swap(): return lax.ppermute(v, 'head', [(i, i ^ m) for i in range(8)])  29.8 us
    pallas_call x1, Pallas kernels, ssd_grad(): pl.pallas_call(ssd_grad_kernel, grid=(heads // 8,), in_specs=[per, per, p...  14.9 us
    ppermute x25, waiting for transfers between devices, swap(): return lax.ppermute(v, 'head', [(i, i ^ m) for i in range(8)])  11.8 us
    pallas_call x1, Pallas kernels, attn_grad(): pl.pallas_call(attn_grad_kernel, in_specs=[SM] + [VM] * 13, out_specs=[HB...  11 us
    all_to_all x1, starting transfers between devices, per_device(): recv = lax.all_to_all(send, 'seq', 0, 0)  8.74 us
    pallas_call x1, Pallas kernels, ssd_send(): pl.pallas_call(ssd_send_kernel, grid_spec=pltpu.PrefetchScalarGridSpec(nu...  8.22 us
    all_to_all x1, waiting for transfers between devices, per_device(): recv = lax.all_to_all(send, 'seq', 0, 0)  7.52 us
    all_to_all x1, starting transfers between devices, per_device(): back = lax.all_to_all(back, 'seq', 0, 0)  6.22 us
  transfers between devices with their start and end apart: 28, of which 7 were waited for; matrix products, arithmetic and copies ran while one was open for 3% of the time, Pallas kernels for 19%

profile of v5, /device:TPU:1, one launch (start us, length us, event | category | flops | bytes accessed | tf_op | source)
XLA Modules:
  0.0 116.7 jit_solution(3719929708388860301)
XLA Ops:
  0.6 8.2 %ssd_send.1 = (bf16[16,400,128]{2,1,0:T(8,128)(2,1)}, bf16[16,512,128]{2,1,0:T(8,128)(2,1)}, bf16[16,512,128]{2,1,0:T(8,128)(2,1)}, f32[16,512]{1,0:T(8,128)}, bf16[2,512,128]{2,1,0:T(8,128)(2,1)}) custom-call(bf16[512,16,128]{2,1,0:T(8,128)(2,1)} %x_ref.1, bf16[512,16,128]{2,1,0:T(8,128)(2,1)} %y_ref.1, f32[16,512]{1,0:T(8,128)} %bitcast.20, ...), custom_call_target="tpu_custom_call" | custom-call | flops 3000000000 | bytes 10000000 | tf_op jit(solution)/shard_map/ssd_send/pallas_call | solution.py:105
  8.9 0.0 copy-start
  8.9 8.7 %all-to-all-start = ((bf16[16,400,128]{2,1,0:T(8,128)(2,1)}), bf16[16,400,128]{2,1,0:T(8,128)(2,1)S(1)}, u32[]{:S(2)}, u32[]{:S(2)}) async-start(bf16[16,400,128]{2,1,0:T(8,128)(2,1)} %get-tuple-element.35), calls=%async_computation | async-start | bytes 3276800 | tf_op jit(solution)/shard_map/all_to_all | solution.py:552
  17.6 0.0 copy-start.1
  17.6 2.6 %collective-permute-start.5 = (bf16[2,512,128]{2,1,0:T(8,128)(2,1)S(1)}, bf16[2,512,128]{2,1,0:T(8,128)(2,1)S(1)}, u32[]{:S(2)}, u32[]{:S(2)}) collective-permute-start(bf16[2,512,128]{2,1,0:T(8,128)(2,1)S(1)} %copy-done), channel_id=1, source_target_pairs={{0,6},{1,7},{2,4},{3,5},{4,2},{5,3},{6,0},{7,1},{8,14},{9,15},{10,... | collective-permute-start | bytes 786440 | tf_op jit(solution)/shard_map/ppermute | solution.py:508
  20.2 0.5 collective-permute-start.3
  20.7 0.3 collective-permute-start.1
  21.0 1.8 %collective-permute-start = (bf16[2,512,128]{2,1,0:T(8,128)(2,1)S(1)}, bf16[2,512,128]{2,1,0:T(8,128)(2,1)S(1)}, u32[]{:S(2)}, u32[]{:S(2)}) collective-permute-start(bf16[2,512,128]{2,1,0:T(8,128)(2,1)S(1)} %copy-done), channel_id=1, source_target_pairs={{0,1},{1,0},{2,3},{3,2},{4,5},{5,4},{6,7},{7,6},{8,9},{9,8},{10,11... | collective-permute-start | bytes 786440 | tf_op jit(solution)/shard_map/ppermute | solution.py:508
  22.8 8.5 %collective-permute-done.5.refs_6_ = bf16[2,512,128]{2,1,0:T(8,128)(2,1)S(1)} collective-permute-done((bf16[2,512,128]{2,1,0:T(8,128)(2,1)S(1)}, bf16[2,512,128]{2,1,0:T(8,128)(2,1)S(1)}, u32[]{:S(2)}, u32[]{:S(2)}) %collective-permute-start.5) | collective-permute-done | bytes 262176 | tf_op jit(solution)/shard_map/ppermute | solution.py:508
  31.3 2.0 %collective-permute-start.6 = (bf16[2,512,128]{2,1,0:T(8,128)(2,1)S(1)}, bf16[2,512,128]{2,1,0:T(8,128)(2,1)S(1)}, u32[]{:S(2)}, u32[]{:S(2)}) collective-permute-start(bf16[2,512,128]{2,1,0:T(8,128)(2,1)S(1)} %collective-permute-done.5.refs_6_), channel_id=1, source_target_pairs={{0,1},{1,0},{2,3},{3,2},{4,5},{5,4},{6,7},{7,6},{8,9},{9,8},{10,11... | collective-permute-start | bytes 786440 | tf_op jit(solution)/shard_map/ppermute | solution.py:508
  33.3 0.0 collective-permute-done.3.refs_4_
  33.3 0.0 collective-permute-start.4
  33.3 0.0 collective-permute-done.1.refs_2_
  33.3 0.6 collective-permute-start.2
  33.9 7.5 %all-to-all-done.recv = bf16[16,400,128]{2,1,0:T(8,128)(2,1)S(1)} async-done(((bf16[16,400,128]{2,1,0:T(8,128)(2,1)}), bf16[16,400,128]{2,1,0:T(8,128)(2,1)S(1)}, u32[]{:S(2)}, u32[]{:S(2)}) %all-to-all-start) | async-done | bytes 1638432 | tf_op jit(solution)/shard_map/all_to_all | solution.py:552
  41.4 1.3 %scan.1 = bf16[16,256,128]{2,1,0:T(8,128)(2,1)} custom-call(bf16[16,400,128]{2,1,0:T(8,128)(2,1)S(1)} %all-to-all-done.recv), custom_call_target="tpu_custom_call" | custom-call | tf_op jit(solution)/shard_map/scan/pallas_call | solution.py:164
  42.7 4.6 %all-to-all-start.1 = ((bf16[16,256,128]{2,1,0:T(8,128)(2,1)}), bf16[16,256,128]{2,1,0:T(8,128)(2,1)}, u32[]{:S(2)}, u32[]{:S(2)}) async-start(bf16[16,256,128]{2,1,0:T(8,128)(2,1)} %scan.1), calls=%async_computation.1 | async-start | bytes 2097152 | tf_op jit(solution)/shard_map/all_to_all | solution.py:555
  47.3 0.0 collective-permute-done.refs_1_
  47.3 0.0 collective-permute-done.6.refs_7_
  47.3 0.0 collective-permute-done.4.refs_5_
  47.3 0.0 collective-permute-done.2.refs_3_
  47.4 5.8 %attn_stat.1 = (f32[3,8,512]{2,1,0:T(8,128)S(1)}, f32[3,8,512]{2,1,0:T(8,128)S(1)}) custom-call(s32[16]{0:T(128)S(1)} %copy-done.1, bf16[16,400,128]{2,1,0:T(8,128)(2,1)S(1)} %all-to-all-done.recv, bf16[2,512,128]{2,1,0:T(8,128)(2,1)S(1)} %copy-done, bf16[2,512,128]{2,1,0:T(8,128)(2,1)S(1)} %collective-permute-done.refs_1_, ...), custom_call_target="tpu_custom_call" | custom-call | flops 4000000000 | bytes 5000000 | tf_op jit(solution)/shard_map/attn_stat/pallas_call | solution.py:229
  53.2 2.3 %collective-permute-start.7 = (f32[3,8,512]{2,1,0:T(8,128)S(1)}, f32[3,8,512]{2,1,0:T(8,128)S(1)}, u32[]{:S(2)}, u32[]{:S(2)}) collective-permute-start(f32[3,8,512]{2,1,0:T(8,128)S(1)} %get-tuple-element.40), channel_id=1, source_target_pairs={{0,1},{1,0},{2,3},{3,2},{4,5},{5,4},{6,7},{7,6},{8,9},{9,8},{10,11... | collective-permute-start | bytes 147464 | tf_op jit(solution)/shard_map/ppermute | solution.py:508
  55.4 0.9 collective-permute-done.7
  56.4 2.8 %collective-permute-start.10 = (f32[3,8,512]{2,1,0:T(8,128)S(1)}, f32[3,8,512]{2,1,0:T(8,128)}, u32[]{:S(2)}, u32[]{:S(2)}) collective-permute-start(f32[3,8,512]{2,1,0:T(8,128)S(1)} %pad_maximum_fusion.refs_8_), channel_id=1, source_target_pairs={{0,4},{1,5},{2,6},{3,7},{4,0},{5,1},{6,2},{7,3},{8,12},{9,13},{10,... | collective-permute-start | bytes 147464 | tf_op jit(solution)/shard_map/ppermute | solution.py:508
  59.2 0.9 collective-permute-start.9
  60.1 0.0 collective-permute-start.8
  60.1 2.3 %all-to-all-done.1.states = bf16[16,256,128]{2,1,0:T(8,128)(2,1)} async-done(((bf16[16,256,128]{2,1,0:T(8,128)(2,1)}), bf16[16,256,128]{2,1,0:T(8,128)(2,1)}, u32[]{:S(2)}, u32[]{:S(2)}) %all-to-all-start.1) | async-done | bytes 1048608 | tf_op jit(solution)/shard_map/all_to_all | solution.py:555
  62.3 0.0 collective-permute-done.10.refs_11_
  62.3 1.1 collective-permute-done.9.refs_10_
  63.5 0.0 collective-permute-done.8.refs_9_
  63.5 11.0 %attn_grad.1 = (bf16[16,128,128]{2,1,0:T(8,128)(2,1)}, bf16[128,512]{1,0:T(8,128)(2,1)}, bf16[128,512]{1,0:T(8,128)(2,1)}, bf16[128,512]{1,0:T(8,128)(2,1)}, bf1...) custom-call(s32[16]{0:T(128)S(1)} %copy-done.1, ...), custom_call_target="tpu_custom_call" | custom-call | flops 8000000000 | bytes 6000000 | tf_op jit(solution)/shard_map/attn_grad/pallas_call | solution.py:311
  74.5 0.0 copy-start.2
  74.5 2.4 %collective-permute-start.12 = (bf16[128,512]{1,0:T(8,128)(2,1)}, bf16[128,512]{1,0:T(8,128)(2,1)S(1)}, u32[]{:S(2)}, u32[]{:S(2)}) collective-permute-start(bf16[128,512]{1,0:T(8,128)(2,1)} %get-tuple-element.45), channel_id=1, source_target_pairs={{0,1},{1,0},{2,3},{3,2},{4,5},{5,4},{6,7},{7,6},{8,9},{9,8},{10,11... | collective-permute-start | bytes 393224 | tf_op jit(solution)/shard_map/ppermute | solution.py:508
  76.9 6.2 %all-to-all-start.2 = ((bf16[16,128,128]{2,1,0:T(8,128)(2,1)}), bf16[16,128,128]{2,1,0:T(8,128)(2,1)S(1)}, u32[]{:S(2)}, u32[]{:S(2)}) async-start(bf16[16,128,128]{2,1,0:T(8,128)(2,1)} %get-tuple-element.41), calls=%async_computation.2 | async-start | bytes 1048576 | tf_op jit(solution)/shard_map/all_to_all | solution.py:562
  83.2 0.4 collective-permute-start.11
  83.5 0.2 collective-permute-start.13
  83.7 0.3 collective-permute-start.14
  84.1 0.9 add_convert_fusion.2
  85.0 0.1 collective-permute-start.15
  85.1 0.0 collective-permute-done.13
  85.1 0.9 add_convert_fusion.1
  86.0 3.0 %collective-permute-start.17 = (bf16[128,512]{1,0:T(8,128)(2,1)S(1)}, bf16[128,512]{1,0:T(8,128)(2,1)S(1)}, u32[]{:S(2)}, u32[]{:S(2)}) collective-permute-start(bf16[128,512]{1,0:T(8,128)(2,1)S(1)} %add_convert_fusion.1), channel_id=1, source_target_pairs={{0,4},{1,5},{2,6},{3,7},{4,0},{5,1},{6,2},{7,3},{8,12},{9,13},{10,... | collective-permute-start | bytes 393224 | tf_op jit(solution)/shard_map/ppermute | solution.py:508
  89.0 0.0 collective-permute-done.14
  89.0 0.9 add_convert_fusion
  90.0 1.2 %collective-permute-start.16 = (bf16[128,512]{1,0:T(8,128)(2,1)S(1)}, bf16[128,512]{1,0:T(8,128)(2,1)S(1)}, u32[]{:S(2)}, u32[]{:S(2)}) collective-permute-start(bf16[128,512]{1,0:T(8,128)(2,1)S(1)} %add_convert_fusion), channel_id=1, source_target_pairs={{0,6},{1,7},{2,4},{3,5},{4,2},{5,3},{6,0},{7,1},{8,14},{9,15},{10,... | collective-permute-start | bytes 393224 | tf_op jit(solution)/shard_map/ppermute | solution.py:508
  91.2 14.9 %ssd_grad.1 = (bf16[512,16,128]{2,1,0:T(8,128)(2,1)}, f32[16,512]{1,0:T(8,128)}, f32[512,128]{1,0:T(8,128)}, f32[512,128]{1,0:T(8,128)}) custom-call(bf16[16,512,128]{2,1,0:T(8,128)(2,1)} %get-tuple-element.50.xh, bf16[16,512,128]{2,1,0:T(8,128)(2,1)} %get-tuple-element.51.yh, bf16[16,256,128]{2,1,0:T(8,128)(2,1)} %all-to-all-done.1.states, ...), custom_call_target="tpu_custom_call" | custom-call | flops 6000000000 | bytes 10000000 | tf_op jit(solution)/shard_map/ssd_grad/pallas_call | solution.py:444
  106.1 0.0 all-to-all-done.2
  106.1 0.1 reduce_sum.12.refs_4_
  106.2 1.8 %collective-permute-start.23 = (bf16[128,128]{1,0:T(8,128)(2,1)S(1)}, bf16[128,128]{1,0:T(8,128)(2,1)S(1)}, u32[]{:S(2)}, u32[]{:S(2)}) collective-permute-start(bf16[128,128]{1,0:T(8,128)(2,1)S(1)} %reduce_sum.12.refs_4_), channel_id=1, source_target_pairs={{0,6},{1,7},{2,4},{3,5},{4,2},{5,3},{6,0},{7,1},{8,14},{9,15},{10,... | collective-permute-start | bytes 98312 | tf_op jit(solution)/shard_map/ppermute | solution.py:508
  108.0 0.0 collective-permute-start.21
  108.0 1.5 %collective-permute-start.19 = (bf16[128,128]{1,0:T(8,128)(2,1)S(1)}, bf16[128,128]{1,0:T(8,128)(2,1)S(1)}, u32[]{:S(2)}, u32[]{:S(2)}) collective-permute-start(bf16[128,128]{1,0:T(8,128)(2,1)S(1)} %reduce_sum.12.refs_4_), channel_id=1, source_target_pairs={{0,2},{1,3},{2,0},{3,1},{4,6},{5,7},{6,4},{7,5},{8,10},{9,11},{10,... | collective-permute-start | bytes 98312 | tf_op jit(solution)/shard_map/ppermute | solution.py:508
  109.5 0.0 collective-permute-done.17.refs_3_
  109.5 1.9 %collective-permute-start.18 = (bf16[128,128]{1,0:T(8,128)(2,1)S(1)}, bf16[128,128]{1,0:T(8,128)(2,1)S(1)}, u32[]{:S(2)}, u32[]{:S(2)}) collective-permute-start(bf16[128,128]{1,0:T(8,128)(2,1)S(1)} %reduce_sum.12.refs_4_), channel_id=1, source_target_pairs={{0,1},{1,0},{2,3},{3,2},{4,5},{5,4},{6,7},{7,6},{8,9},{9,8},{10,11... | collective-permute-start | bytes 98312 | tf_op jit(solution)/shard_map/ppermute | solution.py:508
  111.4 0.0 collective-permute-done.23.refs_10_
  111.4 1.0 collective-permute-start.24
  112.4 2.3 %collective-permute-start.22 = (bf16[128,128]{1,0:T(8,128)(2,1)S(1)}, bf16[128,128]{1,0:T(8,128)(2,1)S(1)}, u32[]{:S(2)}, u32[]{:S(2)}) collective-permute-start(bf16[128,128]{1,0:T(8,128)(2,1)S(1)} %collective-permute-done.21.refs_8_), channel_id=1, source_target_pairs={{0,1},{1,0},{2,3},{3,2},{4,5},{5,4},{6,7},{7,6},{8,9},{9,8},{10,11... | collective-permute-start | bytes 98312 | tf_op jit(solution)/shard_map/ppermute | solution.py:508
  114.7 0.0 collective-permute-done.19.refs_6_
  114.7 0.0 collective-permute-start.20
  114.7 0.0 collective-permute-done.16.refs_2_
  114.7 0.0 collective-permute-done.24.refs_11_
  114.7 0.8 collective-permute-done.22.refs_9_
  115.6 0.4 collective-permute-done.20.refs_7_
  115.9 0.8 finish.1
  (12 shorter events, 0.1 us)
Async XLA Ops:
  8.9 8.8 %copy-start = (bf16[2,512,128]{2,1,0:T(8,128)(2,1)S(1)}, bf16[2,512,128]{2,1,0:T(8,128)(2,1)}, u32[]{:S(2)}) copy-start(bf16[2,512,128]{2,1,0:T(8,128)(2,1)} %get-tuple-element.37.refs_0_) | copy-start | bytes 786436
  8.9 32.5 %all-to-all-start = ((bf16[16,400,128]{2,1,0:T(8,128)(2,1)}), bf16[16,400,128]{2,1,0:T(8,128)(2,1)S(1)}, u32[]{:S(2)}, u32[]{:S(2)}) async-start(bf16[16,400,128]{2,1,0:T(8,128)(2,1)} %get-tuple-element.35), calls=%async_computation | async-start | bytes 3276800 | tf_op jit(solution)/shard_map/all_to_all | solution.py:552
  17.6 29.7 %copy-start.1 = (s32[16]{0:T(128)S(1)}, s32[16]{0:T(128)}, u32[]{:S(2)}) copy-start(s32[16]{0:T(128)} %order.3) | copy-start | bytes 196
  17.6 13.7 %collective-permute-start.5 = (bf16[2,512,128]{2,1,0:T(8,128)(2,1)S(1)}, bf16[2,512,128]{2,1,0:T(8,128)(2,1)S(1)}, u32[]{:S(2)}, u32[]{:S(2)}) collective-permute-start(bf16[2,512,128]{2,1,0:T(8,128)(2,1)S(1)} %copy-done), channel_id=1, source_target_pairs={{0,6},{1,7},{2,4},{3,5},{4,2},{5,3},{6,0},{7,1},{8,14},{9,15},{10,... | collective-permute-start | bytes 786440 | tf_op jit(solution)/shard_map/ppermute | solution.py:508
  20.2 13.1 %collective-permute-start.3 = (bf16[2,512,128]{2,1,0:T(8,128)(2,1)S(1)}, bf16[2,512,128]{2,1,0:T(8,128)(2,1)S(1)}, u32[]{:S(2)}, u32[]{:S(2)}) collective-permute-start(bf16[2,512,128]{2,1,0:T(8,128)(2,1)S(1)} %copy-done), channel_id=1, source_target_pairs={{0,4},{1,5},{2,6},{3,7},{4,0},{5,1},{6,2},{7,3},{8,12},{9,13},{10,... | collective-permute-start | bytes 786440 | tf_op jit(solution)/shard_map/ppermute | solution.py:508
  20.7 12.6 %collective-permute-start.1 = (bf16[2,512,128]{2,1,0:T(8,128)(2,1)S(1)}, bf16[2,512,128]{2,1,0:T(8,128)(2,1)S(1)}, u32[]{:S(2)}, u32[]{:S(2)}) collective-permute-start(bf16[2,512,128]{2,1,0:T(8,128)(2,1)S(1)} %copy-done), channel_id=1, source_target_pairs={{0,2},{1,3},{2,0},{3,1},{4,6},{5,7},{6,4},{7,5},{8,10},{9,11},{10,... | collective-permute-start | bytes 786440 | tf_op jit(solution)/shard_map/ppermute | solution.py:508
  21.0 26.3 %collective-permute-start = (bf16[2,512,128]{2,1,0:T(8,128)(2,1)S(1)}, bf16[2,512,128]{2,1,0:T(8,128)(2,1)S(1)}, u32[]{:S(2)}, u32[]{:S(2)}) collective-permute-start(bf16[2,512,128]{2,1,0:T(8,128)(2,1)S(1)} %copy-done), channel_id=1, source_target_pairs={{0,1},{1,0},{2,3},{3,2},{4,5},{5,4},{6,7},{7,6},{8,9},{9,8},{10,11... | collective-permute-start | bytes 786440 | tf_op jit(solution)/shard_map/ppermute | solution.py:508
  31.3 16.0 %collective-permute-start.6 = (bf16[2,512,128]{2,1,0:T(8,128)(2,1)S(1)}, bf16[2,512,128]{2,1,0:T(8,128)(2,1)S(1)}, u32[]{:S(2)}, u32[]{:S(2)}) collective-permute-start(bf16[2,512,128]{2,1,0:T(8,128)(2,1)S(1)} %collective-permute-done.5.refs_6_), channel_id=1, source_target_pairs={{0,1},{1,0},{2,3},{3,2},{4,5},{5,4},{6,7},{7,6},{8,9},{9,8},{10,11... | collective-permute-start | bytes 786440 | tf_op jit(solution)/shard_map/ppermute | solution.py:508
  33.3 14.1 %collective-permute-start.4 = (bf16[2,512,128]{2,1,0:T(8,128)(2,1)S(1)}, bf16[2,512,128]{2,1,0:T(8,128)(2,1)S(1)}, u32[]{:S(2)}, u32[]{:S(2)}) collective-permute-start(bf16[2,512,128]{2,1,0:T(8,128)(2,1)S(1)} %collective-permute-done.3.refs_4_), channel_id=1, source_target_pairs={{0,1},{1,0},{2,3},{3,2},{4,5},{5,4},{6,7},{7,6},{8,9},{9,8},{10,11... | collective-permute-start | bytes 786440 | tf_op jit(solution)/shard_map/ppermute | solution.py:508
  33.3 14.1 %collective-permute-start.2 = (bf16[2,512,128]{2,1,0:T(8,128)(2,1)S(1)}, bf16[2,512,128]{2,1,0:T(8,128)(2,1)}, u32[]{:S(2)}, u32[]{:S(2)}) collective-permute-start(bf16[2,512,128]{2,1,0:T(8,128)(2,1)S(1)} %collective-permute-done.1.refs_2_), channel_id=1, source_target_pairs={{0,1},{1,0},{2,3},{3,2},{4,5},{5,4},{6,7},{7,6},{8,9},{9,8},{10,11... | collective-permute-start | bytes 786440 | tf_op jit(solution)/shard_map/ppermute | solution.py:508
  42.7 19.6 %all-to-all-start.1 = ((bf16[16,256,128]{2,1,0:T(8,128)(2,1)}), bf16[16,256,128]{2,1,0:T(8,128)(2,1)}, u32[]{:S(2)}, u32[]{:S(2)}) async-start(bf16[16,256,128]{2,1,0:T(8,128)(2,1)} %scan.1), calls=%async_computation.1 | async-start | bytes 2097152 | tf_op jit(solution)/shard_map/all_to_all | solution.py:555
  53.2 3.1 %collective-permute-start.7 = (f32[3,8,512]{2,1,0:T(8,128)S(1)}, f32[3,8,512]{2,1,0:T(8,128)S(1)}, u32[]{:S(2)}, u32[]{:S(2)}) collective-permute-start(f32[3,8,512]{2,1,0:T(8,128)S(1)} %get-tuple-element.40), channel_id=1, source_target_pairs={{0,1},{1,0},{2,3},{3,2},{4,5},{5,4},{6,7},{7,6},{8,9},{9,8},{10,11... | collective-permute-start | bytes 147464 | tf_op jit(solution)/shard_map/ppermute | solution.py:508
  56.4 5.9 %collective-permute-start.10 = (f32[3,8,512]{2,1,0:T(8,128)S(1)}, f32[3,8,512]{2,1,0:T(8,128)}, u32[]{:S(2)}, u32[]{:S(2)}) collective-permute-start(f32[3,8,512]{2,1,0:T(8,128)S(1)} %pad_maximum_fusion.refs_8_), channel_id=1, source_target_pairs={{0,4},{1,5},{2,6},{3,7},{4,0},{5,1},{6,2},{7,3},{8,12},{9,13},{10,... | collective-permute-start | bytes 147464 | tf_op jit(solution)/shard_map/ppermute | solution.py:508
  59.2 4.3 %collective-permute-start.9 = (f32[3,8,512]{2,1,0:T(8,128)S(1)}, f32[3,8,512]{2,1,0:T(8,128)}, u32[]{:S(2)}, u32[]{:S(2)}) collective-permute-start(f32[3,8,512]{2,1,0:T(8,128)S(1)} %pad_maximum_fusion.refs_8_), channel_id=1, source_target_pairs={{0,6},{1,7},{2,4},{3,5},{4,2},{5,3},{6,0},{7,1},{8,14},{9,15},{10,... | collective-permute-start | bytes 147464 | tf_op jit(solution)/shard_map/ppermute | solution.py:508
  60.1 3.4 %collective-permute-start.8 = (f32[3,8,512]{2,1,0:T(8,128)S(1)}, f32[3,8,512]{2,1,0:T(8,128)}, u32[]{:S(2)}, u32[]{:S(2)}) collective-permute-start(f32[3,8,512]{2,1,0:T(8,128)S(1)} %pad_maximum_fusion.refs_8_), channel_id=1, source_target_pairs={{0,2},{1,3},{2,0},{3,1},{4,6},{5,7},{6,4},{7,5},{8,10},{9,11},{10,... | collective-permute-start | bytes 147464 | tf_op jit(solution)/shard_map/ppermute | solution.py:508
  74.5 16.7 %copy-start.2 = (bf16[128,512]{1,0:T(8,128)(2,1)S(1)}, bf16[128,512]{1,0:T(8,128)(2,1)}, u32[]{:S(2)}) copy-start(bf16[128,512]{1,0:T(8,128)(2,1)} %get-tuple-element.42) | copy-start | bytes 393220
  74.5 9.6 %collective-permute-start.12 = (bf16[128,512]{1,0:T(8,128)(2,1)}, bf16[128,512]{1,0:T(8,128)(2,1)S(1)}, u32[]{:S(2)}, u32[]{:S(2)}) collective-permute-start(bf16[128,512]{1,0:T(8,128)(2,1)} %get-tuple-element.45), channel_id=1, source_target_pairs={{0,1},{1,0},{2,3},{3,2},{4,5},{5,4},{6,7},{7,6},{8,9},{9,8},{10,11... | collective-permute-start | bytes 393224 | tf_op jit(solution)/shard_map/ppermute | solution.py:508
  76.9 29.1 %all-to-all-start.2 = ((bf16[16,128,128]{2,1,0:T(8,128)(2,1)}), bf16[16,128,128]{2,1,0:T(8,128)(2,1)S(1)}, u32[]{:S(2)}, u32[]{:S(2)}) async-start(bf16[16,128,128]{2,1,0:T(8,128)(2,1)} %get-tuple-element.41), calls=%async_computation.2 | async-start | bytes 1048576 | tf_op jit(solution)/shard_map/all_to_all | solution.py:562
  83.2 8.0 %collective-permute-start.11 = (bf16[128,512]{1,0:T(8,128)(2,1)}, bf16[128,512]{1,0:T(8,128)(2,1)S(1)}, u32[]{:S(2)}, u32[]{:S(2)}) collective-permute-start(bf16[128,512]{1,0:T(8,128)(2,1)} %get-tuple-element.43), channel_id=1, source_target_pairs={{0,1},{1,0},{2,3},{3,2},{4,5},{5,4},{6,7},{7,6},{8,9},{9,8},{10,11... | collective-permute-start | bytes 393224 | tf_op jit(solution)/shard_map/ppermute | solution.py:508
  83.5 1.6 %collective-permute-start.13 = (bf16[128,512]{1,0:T(8,128)(2,1)}, bf16[128,512]{1,0:T(8,128)(2,1)S(1)}, u32[]{:S(2)}, u32[]{:S(2)}) collective-permute-start(bf16[128,512]{1,0:T(8,128)(2,1)} %get-tuple-element.47), channel_id=1, source_target_pairs={{0,1},{1,0},{2,3},{3,2},{4,5},{5,4},{6,7},{7,6},{8,9},{9,8},{10,11... | collective-permute-start | bytes 393224 | tf_op jit(solution)/shard_map/ppermute | solution.py:508
  83.7 5.3 %collective-permute-start.14 = (bf16[128,512]{1,0:T(8,128)(2,1)}, bf16[128,512]{1,0:T(8,128)(2,1)S(1)}, u32[]{:S(2)}, u32[]{:S(2)}) collective-permute-start(bf16[128,512]{1,0:T(8,128)(2,1)} %get-tuple-element.49), channel_id=1, source_target_pairs={{0,1},{1,0},{2,3},{3,2},{4,5},{5,4},{6,7},{7,6},{8,9},{9,8},{10,11... | collective-permute-start | bytes 393224 | tf_op jit(solution)/shard_map/ppermute | solution.py:508
  85.0 23.0 %collective-permute-start.15 = (bf16[128,512]{1,0:T(8,128)(2,1)S(1)}, bf16[128,512]{1,0:T(8,128)(2,1)S(1)}, u32[]{:S(2)}, u32[]{:S(2)}) collective-permute-start(bf16[128,512]{1,0:T(8,128)(2,1)S(1)} %add_convert_fusion.2), channel_id=1, source_target_pairs={{0,2},{1,3},{2,0},{3,1},{4,6},{5,7},{6,4},{7,5},{8,10},{9,11},{10,... | collective-permute-start | bytes 393224 | tf_op jit(solution)/shard_map/ppermute | solution.py:508
  86.0 23.5 %collective-permute-start.17 = (bf16[128,512]{1,0:T(8,128)(2,1)S(1)}, bf16[128,512]{1,0:T(8,128)(2,1)S(1)}, u32[]{:S(2)}, u32[]{:S(2)}) collective-permute-start(bf16[128,512]{1,0:T(8,128)(2,1)S(1)} %add_convert_fusion.1), channel_id=1, source_target_pairs={{0,4},{1,5},{2,6},{3,7},{4,0},{5,1},{6,2},{7,3},{8,12},{9,13},{10,... | collective-permute-start | bytes 393224 | tf_op jit(solution)/shard_map/ppermute | solution.py:508
  90.0 24.8 %collective-permute-start.16 = (bf16[128,512]{1,0:T(8,128)(2,1)S(1)}, bf16[128,512]{1,0:T(8,128)(2,1)S(1)}, u32[]{:S(2)}, u32[]{:S(2)}) collective-permute-start(bf16[128,512]{1,0:T(8,128)(2,1)S(1)} %add_convert_fusion), channel_id=1, source_target_pairs={{0,6},{1,7},{2,4},{3,5},{4,2},{5,3},{6,0},{7,1},{8,14},{9,15},{10,... | collective-permute-start | bytes 393224 | tf_op jit(solution)/shard_map/ppermute | solution.py:508
  106.2 5.2 %collective-permute-start.23 = (bf16[128,128]{1,0:T(8,128)(2,1)S(1)}, bf16[128,128]{1,0:T(8,128)(2,1)S(1)}, u32[]{:S(2)}, u32[]{:S(2)}) collective-permute-start(bf16[128,128]{1,0:T(8,128)(2,1)S(1)} %reduce_sum.12.refs_4_), channel_id=1, source_target_pairs={{0,6},{1,7},{2,4},{3,5},{4,2},{5,3},{6,0},{7,1},{8,14},{9,15},{10,... | collective-permute-start | bytes 98312 | tf_op jit(solution)/shard_map/ppermute | solution.py:508
  108.0 4.4 %collective-permute-start.21 = (bf16[128,128]{1,0:T(8,128)(2,1)S(1)}, bf16[128,128]{1,0:T(8,128)(2,1)S(1)}, u32[]{:S(2)}, u32[]{:S(2)}) collective-permute-start(bf16[128,128]{1,0:T(8,128)(2,1)S(1)} %reduce_sum.12.refs_4_), channel_id=1, source_target_pairs={{0,4},{1,5},{2,6},{3,7},{4,0},{5,1},{6,2},{7,3},{8,12},{9,13},{10,... | collective-permute-start | bytes 98312 | tf_op jit(solution)/shard_map/ppermute | solution.py:508
  108.0 6.7 %collective-permute-start.19 = (bf16[128,128]{1,0:T(8,128)(2,1)S(1)}, bf16[128,128]{1,0:T(8,128)(2,1)S(1)}, u32[]{:S(2)}, u32[]{:S(2)}) collective-permute-start(bf16[128,128]{1,0:T(8,128)(2,1)S(1)} %reduce_sum.12.refs_4_), channel_id=1, source_target_pairs={{0,2},{1,3},{2,0},{3,1},{4,6},{5,7},{6,4},{7,5},{8,10},{9,11},{10,... | collective-permute-start | bytes 98312 | tf_op jit(solution)/shard_map/ppermute | solution.py:508
  109.5 5.2 %collective-permute-start.18 = (bf16[128,128]{1,0:T(8,128)(2,1)S(1)}, bf16[128,128]{1,0:T(8,128)(2,1)S(1)}, u32[]{:S(2)}, u32[]{:S(2)}) collective-permute-start(bf16[128,128]{1,0:T(8,128)(2,1)S(1)} %reduce_sum.12.refs_4_), channel_id=1, source_target_pairs={{0,1},{1,0},{2,3},{3,2},{4,5},{5,4},{6,7},{7,6},{8,9},{9,8},{10,11... | collective-permute-start | bytes 98312 | tf_op jit(solution)/shard_map/ppermute | solution.py:508
  111.4 3.4 %collective-permute-start.24 = (bf16[128,128]{1,0:T(8,128)(2,1)S(1)}, bf16[128,128]{1,0:T(8,128)(2,1)S(1)}, u32[]{:S(2)}, u32[]{:S(2)}) collective-permute-start(bf16[128,128]{1,0:T(8,128)(2,1)S(1)} %collective-permute-done.23.refs_10_), channel_id=1, source_target_pairs={{0,1},{1,0},{2,3},{3,2},{4,5},{5,4},{6,7},{7,6},{8,9},{9,8},{10,11... | collective-permute-start | bytes 98312 | tf_op jit(solution)/shard_map/ppermute | solution.py:508
  112.4 3.2 %collective-permute-start.22 = (bf16[128,128]{1,0:T(8,128)(2,1)S(1)}, bf16[128,128]{1,0:T(8,128)(2,1)S(1)}, u32[]{:S(2)}, u32[]{:S(2)}) collective-permute-start(bf16[128,128]{1,0:T(8,128)(2,1)S(1)} %collective-permute-done.21.refs_8_), channel_id=1, source_target_pairs={{0,1},{1,0},{2,3},{3,2},{4,5},{5,4},{6,7},{7,6},{8,9},{9,8},{10,11... | collective-permute-start | bytes 98312 | tf_op jit(solution)/shard_map/ppermute | solution.py:508
  114.7 1.2 %collective-permute-start.20 = (bf16[128,128]{1,0:T(8,128)(2,1)S(1)}, bf16[128,128]{1,0:T(8,128)(2,1)S(1)}, u32[]{:S(2)}, u32[]{:S(2)}) collective-permute-start(bf16[128,128]{1,0:T(8,128)(2,1)S(1)} %collective-permute-done.19.refs_6_), channel_id=1, source_target_pairs={{0,1},{1,0},{2,3},{3,2},{4,5},{5,4},{6,7},{7,6},{8,9},{9,8},{10,11... | collective-permute-start | bytes 98312 | tf_op jit(solution)/shard_map/ppermute | solution.py:508

commit v6 on v5

--- a/solution.py
+++ b/solution.py
@@ -334,13 +334,33 @@
     )(order, recv, *qd, *stats)
 
 
-def ssd_grad_kernel(
-    xh, yh, states, cum, b_ref, c_ref,
-    dx_ref, da_ref, db_ref, dc_ref,
-    g_s, dg_s, dct, dbt, bt_s, ct_s, colp, dcol, drow, dxs,
+STEP_HEADS = 4
+
+
+def turned_columns(cum, k, table):
+    cm = cum[:, k * BLOCK : (k + 1) * BLOCK]
+    tl = jnp.exp(cm[:, BLOCK - 1 :] - cm)
+    gap = jnp.zeros((BLOCK // 2 - cm.shape[0], BLOCK), F32)
+    table[k] = jnp.concatenate([cm, gap, tl, gap], axis=0).T
+
+
+def head_vectors(cum, h, nb):
+    row = cum[pl.ds(h, 1), :]
+    c = [row[:, k * BLOCK : (k + 1) * BLOCK] for k in range(nb)]
+    total = [v[:, BLOCK - 1 :] for v in c]
+    keep = [jnp.exp(t) for t in total]
+    tail = [jnp.exp(t - v) for t, v in zip(total, c)]
+    grow = [jnp.exp(v) for v in c]
+    return c, keep, tail, grow
+
+
+def ssd_local_kernel(
+    xh, yh, cum, b_ref, c_ref,
+    dxl, fp, line_ref, db_ref, dc_ref,
+    g_s, dg_s, bt_s, ct_s, colp, dcol, drow,
 ):
-    base = pl.program_id(0) * 8
-    heads = pl.num_programs(0) * 8
+    base = pl.program_id(0) * STEP_HEADS
+    nh = cum.shape[0]
     nb = xh.shape[1] // BLOCK
     rows = iota((BLOCK, BLOCK), 0)
     lanes = iota((BLOCK, BLOCK), 1)
@@ -348,8 +368,6 @@
     @pl.when(base == 0)
     def _():
         dg_s[...] = jnp.zeros_like(dg_s)
-        dct[...] = jnp.zeros_like(dct)
-        dbt[...] = jnp.zeros_like(dbt)
         dcol[...] = jnp.zeros_like(dcol)
         drow[...] = jnp.zeros_like(drow)
         for k in range(nb):
@@ -359,70 +377,137 @@
             g_s[k] = jnp.where(rows <= lanes, dot(b, c, 1, 1, HIGHEST), 0.0)
             bt_s[k] = b.T
             ct_s[k] = c.T
-            cm = cum[:, sl]
-            tl = jnp.exp(cm[:, BLOCK - 1 :] - cm)
-            gap = jnp.zeros((BLOCK // 2 - heads_of(cum), BLOCK), F32)
-            colp[k] = jnp.concatenate([cm, gap, tl, gap], axis=0).T
-
-    nh = heads_of(cum)
+            turned_columns(cum, k, colp)
+
     turned = [pltpu.roll(colp[k], lax.rem(BLOCK - base, BLOCK), 1) for k in range(nb)]
-    for hh in range(8):
+    for hh in range(STEP_HEADS):
         h = base + hh
-        crow = cum[pl.ds(h, 1), :]
-        x = [xh[hh, k * BLOCK : (k + 1) * BLOCK, :] for k in range(nb)]
-        y = [yh[hh, k * BLOCK : (k + 1) * BLOCK, :] for k in range(nb)]
-        c = [crow[:, k * BLOCK : (k + 1) * BLOCK] for k in range(nb)]
-        total = [v[:, BLOCK - 1 :] for v in c]
-        keep = [jnp.exp(t) for t in total]
-        tail = [jnp.exp(t - v) for t, v in zip(total, c)]
-        grow = [jnp.exp(v) for v in c]
+        c, keep, tail, grow = head_vectors(cum, h, nb)
+        for k in range(nb):
+            at = slice(k * BLOCK, (k + 1) * BLOCK)
+            x = xh[hh, at, :]
+            y = yh[hh, at, :]
+            decay = jnp.exp(jnp.minimum(c[k] - turned[k][:, hh : hh + 1], 0.0))
+            w = g_s[k] * decay
+            t = dot(x, y, 1, 1) * decay
+            dg_s[k] += t
+            z = t * g_s[k]
+            cs = (ct_s[k] * grow[k]).astype(BF)
+            wy = dot(jnp.concatenate([w.astype(BF), cs], axis=0), y, 1, 0)
+            dxl[hh, at, :] = wy[:BLOCK].astype(BF)
+            if k > 0:
+                fp[hh, nb - 2 + k] = wy[BLOCK:].astype(BF)
+            if k < nb - 1:
+                fp[hh, k] = dot((bt_s[k] * tail[k]).astype(BF), x, 1, 0).astype(BF)
+            line = jnp.sum(z, axis=0, keepdims=True)
+            drow[:, at] = jnp.where(iota((nh, BLOCK), 0) == h, line, drow[:, at])
+            dcol[k] = jnp.where(lanes == h, jnp.sum(z, axis=1, keepdims=True), dcol[k])
+
+    @pl.when(base == nh - STEP_HEADS)
+    def _():
+        for k in range(nb):
+            sl = slice(k * BLOCK, (k + 1) * BLOCK)
+            dg = jnp.where(rows <= lanes, dg_s[k], 0.0)
+            db_ref[sl, :] = dot(dg, c_ref[sl, :], 1, 0, HIGHEST)
+            dc_ref[sl, :] = dot(dg.T, b_ref[sl, :], 1, 0, HIGHEST)
+            line_ref[:, sl] = drow[:, sl] - dcol[k].T[:nh]
+
+
+def whole(*shape):
+    return pl.BlockSpec(shape, lambda h: (0,) * len(shape))
+
+
+def ssd_local(xh, yh, cum, b, c):
+    heads, tok, width = xh.shape
+    nb = tok // BLOCK
+    per = pl.BlockSpec((STEP_HEADS, tok, width), lambda h: (h, 0, 0))
+    sq = pltpu.VMEM((nb, 128, 128), F32)
+    return pl.pallas_call(
+        ssd_local_kernel,
+        grid=(heads // STEP_HEADS,),
+        in_specs=[per, per, whole(heads, tok), whole(tok, 128), whole(tok, 128)],
+        out_specs=[
+            per,
+            pl.BlockSpec((STEP_HEADS, 2 * nb - 2, 128, 128), lambda h: (h, 0, 0, 0)),
+            whole(heads, tok),
+            whole(tok, 128),
+            whole(tok, 128),
+        ],
+        out_shape=[
+            jax.ShapeDtypeStruct((heads, tok, width), BF),
+            jax.ShapeDtypeStruct((heads, 2 * nb - 2, 128, 128), BF),
+            jax.ShapeDtypeStruct((heads, tok), F32),
+            jax.ShapeDtypeStruct((tok, 128), F32),
+            jax.ShapeDtypeStruct((tok, 128), F32),
+        ],
+        scratch_shapes=[sq] * 6 + [pltpu.VMEM((heads, tok), F32)],
+        compiler_params=pltpu.CompilerParams(vmem_limit_bytes=60 << 20),
+        cost_estimate=pl.CostEstimate(
+            flops=4 * 10**9, bytes_accessed=10**7, transcendentals=10**6
+        ),
+        name="ssd_local",
+    )(xh, yh, cum, b, c)
+
+
+def ssd_grad_kernel(
+    xh, yh, states, cum, b_ref, c_ref, dxl, fp, line_ref, dbl, dcl,
+    dx_ref, da_ref, db_ref, dc_ref,
+    dct, dbt, bt_s, ct_s, colp, drow, dxs,
+):
+    base = pl.program_id(0) * STEP_HEADS
+    nh = cum.shape[0]
+    nb = xh.shape[1] // BLOCK
+
+    @pl.when(base == 0)
+    def _():
+        dct[...] = jnp.zeros_like(dct)
+        dbt[...] = jnp.zeros_like(dbt)
+        drow[...] = line_ref[...]
+        for k in range(nb):
+            sl = slice(k * BLOCK, (k + 1) * BLOCK)
+            bt_s[k] = b_ref[sl, :].T
+            ct_s[k] = c_ref[sl, :].T
+            turned_columns(cum, k, colp)
+
+    turned = [pltpu.roll(colp[k], lax.rem(BLOCK - base, BLOCK), 1) for k in range(nb)]
+    for hh in range(STEP_HEADS):
+        h = base + hh
+        c, keep, tail, grow = head_vectors(cum, h, nb)
         state = [states[hh, 0:128, :].astype(F32)]
         for k in range(nb - 1):
-            bs = (bt_s[k] * tail[k]).astype(BF)
-            state.append(keep[k] * state[k] + dot(bs, x[k], 1, 0))
+            state.append(keep[k] * state[k] + fp[hh, k].astype(F32))
         pull = states[hh, 128:256, :].astype(F32)
         for k in reversed(range(nb)):
-            decay = jnp.exp(jnp.minimum(c[k] - turned[k][:, hh : hh + 1], 0.0))
-            w = g_s[k] * decay
+            at = slice(k * BLOCK, (k + 1) * BLOCK)
+            x = xh[hh, at, :]
+            y = yh[hh, at, :]
             sb = state[k].astype(BF)
-            xy = dot(jnp.concatenate([x[k], sb], axis=0), y[k], 1, 1)
-            dw = xy[:BLOCK]
-            t = dw * decay
-            dg_s[k] += t
-            z = t * g_s[k]
             pb = pull.astype(BF)
-            bs = (b_ref[k * BLOCK : (k + 1) * BLOCK, :] * turned[k][:, 64 + hh : 65 + hh]).astype(BF)
-            cs = (ct_s[k] * grow[k]).astype(BF)
-            wy = dot(jnp.concatenate([w.astype(BF), cs], axis=0), y[k], 1, 0)
-            dx = wy[:BLOCK] + dot(bs, pb, 1, 0)
-            dxs[pl.ds(k * BLOCK * heads + h, BLOCK, stride=nh), :] = dx
-            dcs = xy[BLOCK:] * grow[k]
+            bs = (b_ref[at, :] * turned[k][:, 64 + hh : 65 + hh]).astype(BF)
+            dx = dxl[hh, at, :].astype(F32) + dot(bs, pb, 1, 0)
+            dxs[pl.ds(k * BLOCK * nh + h, BLOCK, stride=nh), :] = dx
+            dcs = dot(sb, y, 1, 1) * grow[k]
             dct[k] += dcs
-            q = dcs * ct_s[k]
-            dbs = dot(pb, x[k], 1, 1) * tail[k]
+            dbs = dot(pb, x, 1, 1) * tail[k]
             dbt[k] += dbs
-            v = dbs * bt_s[k]
-            vs = jnp.sum(v, axis=0, keepdims=True)
-            line = jnp.sum(z + q, axis=0, keepdims=True) - vs
+            vs = jnp.sum(dbs * bt_s[k], axis=0, keepdims=True)
+            line = jnp.sum(dcs * ct_s[k], axis=0, keepdims=True) - vs
             cross = keep[k] * jnp.sum(state[k] * pull, axis=0, keepdims=True)
             last = jnp.sum(vs + cross, axis=1, keepdims=True)
             line = jnp.where(iota((1, BLOCK), 1) == BLOCK - 1, line + last, line)
-            at = slice(k * BLOCK, (k + 1) * BLOCK)
-            drow[:, at] = jnp.where(iota((nh, BLOCK), 0) == h, line, drow[:, at])
-            zc = jnp.sum(z, axis=1, keepdims=True)
-            dcol[k] = jnp.where(lanes == h, zc, dcol[k])
+            old = drow[:, at]
+            drow[:, at] = jnp.where(iota((nh, BLOCK), 0) == h, old + line, old)
             if k > 0:
-                pull = keep[k] * pull + wy[BLOCK:].astype(BF).astype(F32)
-
-    @pl.when(base == heads - 8)
+                pull = keep[k] * pull + fp[hh, nb - 2 + k].astype(F32)
+
+    @pl.when(base == nh - STEP_HEADS)
     def _():
-        late = (rows >= lanes).astype(F32)
+        late = (iota((BLOCK, BLOCK), 0) >= iota((BLOCK, BLOCK), 1)).astype(F32)
         for k in range(nb):
             sl = slice(k * BLOCK, (k + 1) * BLOCK)
-            dg = jnp.where(rows <= lanes, dg_s[k], 0.0)
-            db_ref[sl, :] = dbt[k].T + dot(dg, c_ref[sl, :], 1, 0, HIGHEST)
-            dc_ref[sl, :] = dct[k].T + dot(dg.T, b_ref[sl, :], 1, 0, HIGHEST)
-            da_ref[:, sl] = dot(drow[:, sl] - dcol[k].T[:nh], late, 1, 0, HIGHEST)
+            db_ref[sl, :] = dbl[sl, :] + dbt[k].T
+            dc_ref[sl, :] = dcl[sl, :] + dct[k].T
+            da_ref[:, sl] = dot(drow[:, sl], late, 1, 0, HIGHEST)
             dx_ref[sl] = (
                 dxs[k * BLOCK * nh : (k + 1) * BLOCK * nh, :]
                 .reshape(BLOCK, nh, 128)
@@ -430,24 +515,24 @@
             )
 
 
-def heads_of(cum):
-    return cum.shape[0]
-
-
-def ssd_grad(xh, yh, states, cum, b, c):
+def ssd_grad(xh, yh, states, cum, b, c, local):
     heads, tok, width = xh.shape
     nb = tok // BLOCK
     rows = states.shape[1]
-    per = pl.BlockSpec((8, tok, width), lambda h: (h, 0, 0))
-    whole = lambda *s: pl.BlockSpec(s, lambda h: (0,) * len(s))
+    per = pl.BlockSpec((STEP_HEADS, tok, width), lambda h: (h, 0, 0))
     sq = pltpu.VMEM((nb, 128, 128), F32)
     return pl.pallas_call(
         ssd_grad_kernel,
-        grid=(heads // 8,),
+        grid=(heads // STEP_HEADS,),
         in_specs=[
             per,
             per,
-            pl.BlockSpec((8, rows, 128), lambda h: (h, 0, 0)),
+            pl.BlockSpec((STEP_HEADS, rows, 128), lambda h: (h, 0, 0)),
+            whole(heads, tok),
+            whole(tok, 128),
+            whole(tok, 128),
+            per,
+            pl.BlockSpec((STEP_HEADS, 2 * nb - 2, 128, 128), lambda h: (h, 0, 0, 0)),
             whole(heads, tok),
             whole(tok, 128),
             whole(tok, 128),
@@ -464,23 +549,18 @@
             jax.ShapeDtypeStruct((tok, 128), F32),
             jax.ShapeDtypeStruct((tok, 128), F32),
         ],
-        scratch_shapes=[
-            sq, sq, sq, sq, sq, sq,
-            sq,
-            sq,
-            pltpu.VMEM((heads, tok), F32),
-            pltpu.VMEM((tok * heads, width), F32),
-        ],
+        scratch_shapes=[sq] * 5
+        + [pltpu.VMEM((heads, tok), F32), pltpu.VMEM((tok * heads, width), F32)],
         compiler_params=pltpu.CompilerParams(vmem_limit_bytes=60 << 20),
         cost_estimate=pl.CostEstimate(
             flops=6 * 10**9, bytes_accessed=10**7, transcendentals=10**6
         ),
         name="ssd_grad",
-    )(xh, yh, states, cum, b, c)
+    )(xh, yh, states, cum, b, c, *local)
 
 
 def finish_kernel(*refs):
-    dqt, parts, (dq, dk, dv) = refs[:4], refs[4:12], refs[12:]
+    dqt, parts, (dq, dk, dv) = refs[:5], refs[5:13], refs[13:]
     total = functools.reduce(jnp.add, [r[...].astype(F32) for r in dqt])
     dq[...] = total.T.astype(BF)
     place = lax.axis_index("head")
@@ -496,7 +576,7 @@
     out = jax.ShapeDtypeStruct((512, 128), BF)
     return pl.pallas_call(
         finish_kernel,
-        in_specs=[VM] * 12,
+        in_specs=[VM] * 13,
         out_specs=[VM, VM, VM],
         out_shape=[out, out, out],
         compiler_params=pltpu.CompilerParams(vmem_limit_bytes=16 << 20),
@@ -527,11 +607,23 @@
     return out
 
 
+def pair_sums_kernel(*refs):
+    for a, b, o in zip(refs[:3], refs[3:6], refs[6:]):
+        o[...] = (a[...].astype(F32) + b[...].astype(F32)).astype(BF)
+
+
 def pair_sums(parts):
-    return [
-        (parts[m].astype(F32) + swap(parts[m + 1], 1).astype(F32)).astype(BF)
-        for m in (0, 2, 4, 6)
-    ]
+    mates = [swap(parts[m + 1], 1) for m in (0, 2, 4, 6)]
+    out = jax.ShapeDtypeStruct(parts[0].shape, BF)
+    sums = pl.pallas_call(
+        pair_sums_kernel,
+        in_specs=[VM] * 6,
+        out_specs=[VM] * 3,
+        out_shape=[out] * 3,
+        compiler_params=pltpu.CompilerParams(vmem_limit_bytes=16 << 20),
+        name="pair_sums",
+    )(*parts[2::2], *mates[1:])
+    return [parts[0], mates[0]], sums
 
 
 def after(value, other):
@@ -551,16 +643,17 @@
     )
     recv = lax.all_to_all(send, "seq", 0, 0)
     qds = gather_heads(qd)
-    turned = scan(recv)
+    local = ssd_local(xh, yh, cum, b, c)
+    turned = scan(after(recv, local[2]))
     states = lax.all_to_all(turned, "seq", 0, 0)
     first, mate = attn_stat(pair_order, after(recv, turned), qds)
     stat = join(first, swap(mate, 1))
     rest = [swap(stat, m) for m in (2, 6, 4)]
     back, *dqt = attn_grad(pair_order, after(recv, states), qds, stat, *rest)
-    pair = pair_sums(dqt)
-    dx, da, db, dc = ssd_grad(after(xh, (back, *pair)), yh, states, cum, b, c)
+    kept, sums = pair_sums(dqt)
+    dx, da, db, dc = ssd_grad(after(xh, (back, *sums)), yh, states, cum, b, c, local)
     back = lax.all_to_all(back, "seq", 0, 0)
-    dqt = [pair[0]] + [swap(pair[i], m) for i, m in ((1, 2), (3, 6), (2, 4))]
+    dqt = kept + [swap(sums[i], m) for i, m in ((0, 2), (2, 6), (1, 4))]
     dkv = jnp.sum(after(back, da).astype(F32), axis=0).astype(BF)
     parts = gather_heads(dkv)
     dq, dk, dv = finish(dqt, parts)

time: 117 us -> 119 us (1.017)
  Pallas kernels: 42 us -> 50.9 us
  waiting for transfers between devices: 21.6 us -> 17.3 us
  starting transfers between devices: 49.4 us -> 46.4 us
  other arithmetic: 2.97 us -> 0.12 us
  local copies, waits for them, and re-layouts: 0.02 us -> 2.72 us
    pallas_call x2 -> x4, Pallas kernels: 15.7 us -> 24.6 us  [the longest x1 11.9 us: ssd_local(): pl.pallas_call(ssd_local_kernel, grid=(heads // STEP_HEADS,), in_specs=[p...]
    all_to_all x1, waiting for transfers between devices: 7.52 us -> 0.01 us  [per_device(): recv = lax.all_to_all(send, 'seq', 0, 0)]
    all_to_all x1, waiting for transfers between devices: 2.25 us -> 6.64 us  [per_device(): states = lax.all_to_all(turned, 'seq', 0, 0)]
    convert_element_type x4 -> x0, other arithmetic: 2.85 us -> none  [pair_sums(): (parts[m].astype(F32) + swap(parts[m + 1], 1).astype(F32)).astype(BF)]
    ppermute x25, starting transfers between devices: 29.8 us -> 27 us  [swap(): return lax.ppermute(v, 'head', [(i, i ^ m) for i in range(8)])]
    unnamed x6 -> x12, local copies, waits for them, and re-layouts: 0.02 us -> 2.72 us
    all_to_all x1, starting transfers between devices: 6.22 us -> 3.94 us  [per_device(): back = lax.all_to_all(back, 'seq', 0, 0)]
    all_to_all x1, starting transfers between devices: 4.62 us -> 6.71 us  [per_device(): states = lax.all_to_all(turned, 'seq', 0, 0)]
  transfers between devices with their start and end apart: 28 -> 28, of which waited for: 7 -> 5; matrix products, arithmetic and copies ran while one was open for 3% -> 0% of each run, Pallas kernels for 19% -> 26%
where the time goes in v6:
time: 119 us; the launch traced here: 118 us
  Pallas kernels  50.9 us (43%)
  starting transfers between devices  46.4 us (39%)
  waiting for transfers between devices  17.3 us (15%)
  local copies, waits for them, and re-layouts  2.72 us (2%)
    ppermute x25, starting transfers between devices, swap(): return lax.ppermute(v, 'head', [(i, i ^ m) for i in range(8)])  27 us
    pallas_call x1, Pallas kernels, ssd_local(): pl.pallas_call(ssd_local_kernel, grid=(heads // STEP_HEADS,), in_specs=[p...  11.9 us
    pallas_call x1, Pallas kernels, ssd_grad(): pl.pallas_call(ssd_grad_kernel, grid=(heads // STEP_HEADS,), in_specs=[pe...  11.7 us
    pallas_call x1, Pallas kernels, attn_grad(): pl.pallas_call(attn_grad_kernel, in_specs=[SM] + [VM] * 13, out_specs=[HB...  11 us
    ppermute x25, waiting for transfers between devices, swap(): return lax.ppermute(v, 'head', [(i, i ^ m) for i in range(8)])  10.7 us
    all_to_all x1, starting transfers between devices, per_device(): recv = lax.all_to_all(send, 'seq', 0, 0)  8.74 us
    pallas_call x1, Pallas kernels, ssd_send(): pl.pallas_call(ssd_send_kernel, grid_spec=pltpu.PrefetchScalarGridSpec(nu...  8.22 us
    all_to_all x1, starting transfers between devices, per_device(): states = lax.all_to_all(turned, 'seq', 0, 0)  6.71 us
  transfers between devices with their start and end apart: 28, of which 5 were waited for; matrix products, arithmetic and copies ran while one was open for 0% of the time, Pallas kernels for 26%

profile of v6, /device:TPU:1, one launch (start us, length us, event | category | flops | bytes accessed | tf_op | source)
XLA Modules:
  0.0 118.4 jit_solution(14903832582225266463)
XLA Ops:
  0.6 8.2 %ssd_send.1 = (bf16[16,400,128]{2,1,0:T(8,128)(2,1)}, bf16[16,512,128]{2,1,0:T(8,128)(2,1)}, bf16[16,512,128]{2,1,0:T(8,128)(2,1)}, f32[16,512]{1,0:T(8,128)}, bf16[2,512,128]{2,1,0:T(8,128)(2,1)}) custom-call(bf16[512,16,128]{2,1,0:T(8,128)(2,1)} %x_ref.1, bf16[512,16,128]{2,1,0:T(8,128)(2,1)} %y_ref.1, f32[16,512]{1,0:T(8,128)} %bitcast.22, ...), custom_call_target="tpu_custom_call" | custom-call | flops 3000000000 | bytes 10000000 | tf_op jit(solution)/shard_map/ssd_send/pallas_call | solution.py:105
  8.9 0.0 copy-start.4
  8.9 8.7 %all-to-all-start = ((bf16[16,400,128]{2,1,0:T(8,128)(2,1)}), bf16[16,400,128]{2,1,0:T(8,128)(2,1)S(1)}, u32[]{:S(2)}, u32[]{:S(2)}) async-start(bf16[16,400,128]{2,1,0:T(8,128)(2,1)} %get-tuple-element.44), calls=%async_computation | async-start | bytes 3276800 | tf_op jit(solution)/shard_map/all_to_all | solution.py:644
  17.6 2.6 %collective-permute-start.5 = (bf16[2,512,128]{2,1,0:T(8,128)(2,1)S(1)}, bf16[2,512,128]{2,1,0:T(8,128)(2,1)S(1)}, u32[]{:S(2)}, u32[]{:S(2)}) collective-permute-start(bf16[2,512,128]{2,1,0:T(8,128)(2,1)S(1)} %copy-done.4), channel_id=1, source_target_pairs={{0,6},{1,7},{2,4},{3,5},{4,2},{5,3},{6,0},{7,1},{8,14},{9,15},{10,... | collective-permute-start | bytes 786440 | tf_op jit(solution)/shard_map/ppermute | solution.py:588
  20.2 0.5 collective-permute-start.3
  20.7 0.3 collective-permute-start.1
  21.0 1.8 %collective-permute-start = (bf16[2,512,128]{2,1,0:T(8,128)(2,1)S(1)}, bf16[2,512,128]{2,1,0:T(8,128)(2,1)S(1)}, u32[]{:S(2)}, u32[]{:S(2)}) collective-permute-start(bf16[2,512,128]{2,1,0:T(8,128)(2,1)S(1)} %copy-done.4), channel_id=1, source_target_pairs={{0,1},{1,0},{2,3},{3,2},{4,5},{5,4},{6,7},{7,6},{8,9},{9,8},{10,11... | collective-permute-start | bytes 786440 | tf_op jit(solution)/shard_map/ppermute | solution.py:588
  22.8 8.5 %collective-permute-done.5.refs_6_ = bf16[2,512,128]{2,1,0:T(8,128)(2,1)S(1)} collective-permute-done((bf16[2,512,128]{2,1,0:T(8,128)(2,1)S(1)}, bf16[2,512,128]{2,1,0:T(8,128)(2,1)S(1)}, u32[]{:S(2)}, u32[]{:S(2)}) %collective-permute-start.5) | collective-permute-done | bytes 262176 | tf_op jit(solution)/shard_map/ppermute | solution.py:588
  31.3 2.0 %collective-permute-start.6 = (bf16[2,512,128]{2,1,0:T(8,128)(2,1)S(1)}, bf16[2,512,128]{2,1,0:T(8,128)(2,1)S(1)}, u32[]{:S(2)}, u32[]{:S(2)}) collective-permute-start(bf16[2,512,128]{2,1,0:T(8,128)(2,1)S(1)} %collective-permute-done.5.refs_6_), channel_id=1, source_target_pairs={{0,1},{1,0},{2,3},{3,2},{4,5},{5,4},{6,7},{7,6},{8,9},{9,8},{10,11... | collective-permute-start | bytes 786440 | tf_op jit(solution)/shard_map/ppermute | solution.py:588
  33.3 0.0 collective-permute-done.3.refs_4_
  33.3 0.0 collective-permute-start.4
  33.3 0.0 collective-permute-done.1.refs_2_
  33.3 0.6 collective-permute-start.2
  33.9 11.9 %ssd_local.1 = (bf16[16,512,128]{2,1,0:T(8,128)(2,1)}, bf16[16,6,128,128]{3,2,1,0:T(8,128)(2,1)}, f32[16,512]{1,0:T(8,128)}, f32[512,128]{1,0:T(8,128)}, f32[512,128]{1,0:T(8,128)}) custom-call(bf16[16,512,128]{2,1,0:T(8,128)(2,1)} %get-tuple-element.64.xh, bf16[16,512,128]{2,1,0:T(8,128)(2,1)} %get-tuple-element.45.yh, f32[16,512]{1,0:T(8,128)} %get-tuple-element.46.cum, ...), custom_call_target="tpu_custom_call" | custom-call | flops 4000000000 | bytes 10000000 | tf_op jit(solution)/shard_map/ssd_local/pallas_call | solution.py:425
  45.8 0.0 copy-start.5
  45.8 1.3 %scan.1 = bf16[16,256,128]{2,1,0:T(8,128)(2,1)} custom-call(bf16[16,400,128]{2,1,0:T(8,128)(2,1)S(1)} %all-to-all-done.recv), custom_call_target="tpu_custom_call" | custom-call | tf_op jit(solution)/shard_map/scan/pallas_call | solution.py:164
  47.1 6.7 %all-to-all-start.1 = ((bf16[16,256,128]{2,1,0:T(8,128)(2,1)}), bf16[16,256,128]{2,1,0:T(8,128)(2,1)}, u32[]{:S(2)}, u32[]{:S(2)}) async-start(bf16[16,256,128]{2,1,0:T(8,128)(2,1)} %scan.1), calls=%async_computation.1 | async-start | bytes 2097152 | tf_op jit(solution)/shard_map/all_to_all | solution.py:648
  53.8 0.0 collective-permute-done.6.refs_7_
  53.8 0.0 collective-permute-done.4.refs_5_
  53.8 5.8 %attn_stat.1 = (f32[3,8,512]{2,1,0:T(8,128)S(1)}, f32[3,8,512]{2,1,0:T(8,128)S(1)}) custom-call(s32[16]{0:T(128)S(1)} %copy-done.5, bf16[16,400,128]{2,1,0:T(8,128)(2,1)S(1)} %all-to-all-done.recv, bf16[2,512,128]{2,1,0:T(8,128)(2,1)S(1)} %copy-done.4, bf16[2,512,128]{2,1,0:T(8,128)(2,1)S(1)} %collective-permute-done.refs_1_, ...), custom_call_target="tpu_custom_call" | custom-call | flops 4000000000 | bytes 5000000 | tf_op jit(solution)/shard_map/attn_stat/pallas_call | solution.py:229
  59.7 0.4 collective-permute-start.7
  60.1 0.9 collective-permute-done.7
  61.1 2.8 %collective-permute-start.10 = (f32[3,8,512]{2,1,0:T(8,128)S(1)}, f32[3,8,512]{2,1,0:T(8,128)}, u32[]{:S(2)}, u32[]{:S(2)}) collective-permute-start(f32[3,8,512]{2,1,0:T(8,128)S(1)} %pad_maximum_fusion.refs_8_), channel_id=1, source_target_pairs={{0,4},{1,5},{2,6},{3,7},{4,0},{5,1},{6,2},{7,3},{8,12},{9,13},{10,... | collective-permute-start | bytes 147464 | tf_op jit(solution)/shard_map/ppermute | solution.py:588
  63.9 0.8 collective-permute-start.9
  64.7 0.0 collective-permute-start.8
  64.7 6.6 %all-to-all-done.1.states = bf16[16,256,128]{2,1,0:T(8,128)(2,1)} async-done(((bf16[16,256,128]{2,1,0:T(8,128)(2,1)}), bf16[16,256,128]{2,1,0:T(8,128)(2,1)}, u32[]{:S(2)}, u32[]{:S(2)}) %all-to-all-start.1) | async-done | bytes 1048608 | tf_op jit(solution)/shard_map/all_to_all | solution.py:648
  71.4 0.0 collective-permute-done.10.refs_11_
  71.4 0.0 collective-permute-done.9.refs_10_
  71.4 0.0 collective-permute-done.8.refs_9_
  71.4 11.0 %attn_grad.1 = (bf16[16,128,128]{2,1,0:T(8,128)(2,1)}, bf16[128,512]{1,0:T(8,128)(2,1)}, bf16[128,512]{1,0:T(8,128)(2,1)}, bf16[128,512]{1,0:T(8,128)(2,1)}, bf1...) custom-call(s32[16]{0:T(128)S(1)} %copy-done.5, ...), custom_call_target="tpu_custom_call" | custom-call | flops 8000000000 | bytes 6000000 | tf_op jit(solution)/shard_map/attn_grad/pallas_call | solution.py:311
  82.4 1.5 %collective-permute-start.11 = (bf16[128,512]{1,0:T(8,128)(2,1)}, bf16[128,512]{1,0:T(8,128)(2,1)S(1)}, u32[]{:S(2)}, u32[]{:S(2)}) collective-permute-start(bf16[128,512]{1,0:T(8,128)(2,1)} %get-tuple-element.58), channel_id=1, source_target_pairs={{0,1},{1,0},{2,3},{3,2},{4,5},{5,4},{6,7},{7,6},{8,9},{9,8},{10,11... | collective-permute-start | bytes 393224 | tf_op jit(solution)/shard_map/ppermute | solution.py:588
  83.9 0.1 collective-permute-start.12
  84.0 0.4 collective-permute-start.13
  84.5 3.9 %all-to-all-start.2 = ((bf16[16,128,128]{2,1,0:T(8,128)(2,1)}), bf16[16,128,128]{2,1,0:T(8,128)(2,1)S(1)}, u32[]{:S(2)}, u32[]{:S(2)}) async-start(bf16[16,128,128]{2,1,0:T(8,128)(2,1)} %get-tuple-element.54), calls=%async_computation.2 | async-start | bytes 1048576 | tf_op jit(solution)/shard_map/all_to_all | solution.py:655
  88.4 0.4 collective-permute-start.14
  88.8 0.0 collective-permute-done.11.refs_3_
  88.8 0.0 collective-permute-done.12.refs_4_
  88.8 0.0 collective-permute-done.13.refs_5_
  88.8 0.0 copy-start.1
  88.9 0.9 copy-done.1
  89.8 0.9 copy-done.2
  90.7 0.9 copy-done.3
  91.6 0.1 pair_sums.1
  91.7 0.6 collective-permute-start.15
  92.3 2.5 %collective-permute-start.17 = (bf16[128,512]{1,0:T(8,128)(2,1)S(1)}, bf16[128,512]{1,0:T(8,128)(2,1)S(1)}, u32[]{:S(2)}, u32[]{:S(2)}) collective-permute-start(bf16[128,512]{1,0:T(8,128)(2,1)S(1)} %get-tuple-element.62), channel_id=1, source_target_pairs={{0,4},{1,5},{2,6},{3,7},{4,0},{5,1},{6,2},{7,3},{8,12},{9,13},{10,... | collective-permute-start | bytes 393224 | tf_op jit(solution)/shard_map/ppermute | solution.py:588
  94.8 0.8 collective-permute-start.16
  95.6 11.7 %ssd_grad.1 = (bf16[512,16,128]{2,1,0:T(8,128)(2,1)}, f32[16,512]{1,0:T(8,128)}, f32[512,128]{1,0:T(8,128)}, f32[512,128]{1,0:T(8,128)}) custom-call(bf16[16,512,128]{2,1,0:T(8,128)(2,1)} %get-tuple-element.64.xh, bf16[16,512,128]{2,1,0:T(8,128)(2,1)} %get-tuple-element.45.yh, bf16[16,256,128]{2,1,0:T(8,128)(2,1)} %all-to-all-done.1.states, ...), custom_call_target="tpu_custom_call" | custom-call | flops 6000000000 | bytes 10000000 | tf_op jit(solution)/shard_map/ssd_grad/pallas_call | solution.py:524
  107.3 0.0 all-to-all-done.2
  107.3 0.1 reduce_sum.12.refs_5_
  107.4 1.9 %collective-permute-start.23 = (bf16[128,128]{1,0:T(8,128)(2,1)S(1)}, bf16[128,128]{1,0:T(8,128)(2,1)S(1)}, u32[]{:S(2)}, u32[]{:S(2)}) collective-permute-start(bf16[128,128]{1,0:T(8,128)(2,1)S(1)} %reduce_sum.12.refs_5_), channel_id=1, source_target_pairs={{0,6},{1,7},{2,4},{3,5},{4,2},{5,3},{6,0},{7,1},{8,14},{9,15},{10,... | collective-permute-start | bytes 98312 | tf_op jit(solution)/shard_map/ppermute | solution.py:588
  109.4 0.0 collective-permute-done.14.refs_1_
  109.4 0.0 collective-permute-start.21
  109.4 1.4 %collective-permute-start.19 = (bf16[128,128]{1,0:T(8,128)(2,1)S(1)}, bf16[128,128]{1,0:T(8,128)(2,1)S(1)}, u32[]{:S(2)}, u32[]{:S(2)}) collective-permute-start(bf16[128,128]{1,0:T(8,128)(2,1)S(1)} %reduce_sum.12.refs_5_), channel_id=1, source_target_pairs={{0,2},{1,3},{2,0},{3,1},{4,6},{5,7},{6,4},{7,5},{8,10},{9,11},{10,... | collective-permute-start | bytes 98312 | tf_op jit(solution)/shard_map/ppermute | solution.py:588
  110.8 1.9 %collective-permute-start.18 = (bf16[128,128]{1,0:T(8,128)(2,1)S(1)}, bf16[128,128]{1,0:T(8,128)(2,1)S(1)}, u32[]{:S(2)}, u32[]{:S(2)}) collective-permute-start(bf16[128,128]{1,0:T(8,128)(2,1)S(1)} %reduce_sum.12.refs_5_), channel_id=1, source_target_pairs={{0,1},{1,0},{2,3},{3,2},{4,5},{5,4},{6,7},{7,6},{8,9},{9,8},{10,11... | collective-permute-start | bytes 98312 | tf_op jit(solution)/shard_map/ppermute | solution.py:588
  112.6 0.0 collective-permute-done.23.refs_11_
  112.6 1.0 collective-permute-start.24
  113.6 0.0 collective-permute-done.21.refs_9_
  113.6 2.7 %collective-permute-start.22 = (bf16[128,128]{1,0:T(8,128)(2,1)S(1)}, bf16[128,128]{1,0:T(8,128)(2,1)S(1)}, u32[]{:S(2)}, u32[]{:S(2)}) collective-permute-start(bf16[128,128]{1,0:T(8,128)(2,1)S(1)} %collective-permute-done.21.refs_9_), channel_id=1, source_target_pairs={{0,1},{1,0},{2,3},{3,2},{4,5},{5,4},{6,7},{7,6},{8,9},{9,8},{10,11... | collective-permute-start | bytes 98312 | tf_op jit(solution)/shard_map/ppermute | solution.py:588
  116.3 0.0 collective-permute-done.19.refs_7_
  116.3 0.0 collective-permute-start.20
  116.3 0.0 collective-permute-done.18.refs_6_
  116.3 0.8 collective-permute-done.22.refs_10_
  117.2 0.4 collective-permute-done.20.refs_8_
  117.5 0.8 finish.1
  (16 shorter events, 0.1 us)
Async XLA Ops:
  8.9 8.8 %copy-start.4 = (bf16[2,512,128]{2,1,0:T(8,128)(2,1)S(1)}, bf16[2,512,128]{2,1,0:T(8,128)(2,1)}, u32[]{:S(2)}) copy-start(bf16[2,512,128]{2,1,0:T(8,128)(2,1)} %get-tuple-element.50.refs_0_) | copy-start | bytes 786436
  8.9 36.9 %all-to-all-start = ((bf16[16,400,128]{2,1,0:T(8,128)(2,1)}), bf16[16,400,128]{2,1,0:T(8,128)(2,1)S(1)}, u32[]{:S(2)}, u32[]{:S(2)}) async-start(bf16[16,400,128]{2,1,0:T(8,128)(2,1)} %get-tuple-element.44), calls=%async_computation | async-start | bytes 3276800 | tf_op jit(solution)/shard_map/all_to_all | solution.py:644
  17.6 13.7 %collective-permute-start.5 = (bf16[2,512,128]{2,1,0:T(8,128)(2,1)S(1)}, bf16[2,512,128]{2,1,0:T(8,128)(2,1)S(1)}, u32[]{:S(2)}, u32[]{:S(2)}) collective-permute-start(bf16[2,512,128]{2,1,0:T(8,128)(2,1)S(1)} %copy-done.4), channel_id=1, source_target_pairs={{0,6},{1,7},{2,4},{3,5},{4,2},{5,3},{6,0},{7,1},{8,14},{9,15},{10,... | collective-permute-start | bytes 786440 | tf_op jit(solution)/shard_map/ppermute | solution.py:588
  20.2 13.1 %collective-permute-start.3 = (bf16[2,512,128]{2,1,0:T(8,128)(2,1)S(1)}, bf16[2,512,128]{2,1,0:T(8,128)(2,1)S(1)}, u32[]{:S(2)}, u32[]{:S(2)}) collective-permute-start(bf16[2,512,128]{2,1,0:T(8,128)(2,1)S(1)} %copy-done.4), channel_id=1, source_target_pairs={{0,4},{1,5},{2,6},{3,7},{4,0},{5,1},{6,2},{7,3},{8,12},{9,13},{10,... | collective-permute-start | bytes 786440 | tf_op jit(solution)/shard_map/ppermute | solution.py:588
  20.7 12.6 %collective-permute-start.1 = (bf16[2,512,128]{2,1,0:T(8,128)(2,1)S(1)}, bf16[2,512,128]{2,1,0:T(8,128)(2,1)S(1)}, u32[]{:S(2)}, u32[]{:S(2)}) collective-permute-start(bf16[2,512,128]{2,1,0:T(8,128)(2,1)S(1)} %copy-done.4), channel_id=1, source_target_pairs={{0,2},{1,3},{2,0},{3,1},{4,6},{5,7},{6,4},{7,5},{8,10},{9,11},{10,... | collective-permute-start | bytes 786440 | tf_op jit(solution)/shard_map/ppermute | solution.py:588
  21.0 32.8 %collective-permute-start = (bf16[2,512,128]{2,1,0:T(8,128)(2,1)S(1)}, bf16[2,512,128]{2,1,0:T(8,128)(2,1)S(1)}, u32[]{:S(2)}, u32[]{:S(2)}) collective-permute-start(bf16[2,512,128]{2,1,0:T(8,128)(2,1)S(1)} %copy-done.4), channel_id=1, source_target_pairs={{0,1},{1,0},{2,3},{3,2},{4,5},{5,4},{6,7},{7,6},{8,9},{9,8},{10,11... | collective-permute-start | bytes 786440 | tf_op jit(solution)/shard_map/ppermute | solution.py:588
  31.3 22.5 %collective-permute-start.6 = (bf16[2,512,128]{2,1,0:T(8,128)(2,1)S(1)}, bf16[2,512,128]{2,1,0:T(8,128)(2,1)S(1)}, u32[]{:S(2)}, u32[]{:S(2)}) collective-permute-start(bf16[2,512,128]{2,1,0:T(8,128)(2,1)S(1)} %collective-permute-done.5.refs_6_), channel_id=1, source_target_pairs={{0,1},{1,0},{2,3},{3,2},{4,5},{5,4},{6,7},{7,6},{8,9},{9,8},{10,11... | collective-permute-start | bytes 786440 | tf_op jit(solution)/shard_map/ppermute | solution.py:588
  33.3 20.6 %collective-permute-start.4 = (bf16[2,512,128]{2,1,0:T(8,128)(2,1)S(1)}, bf16[2,512,128]{2,1,0:T(8,128)(2,1)S(1)}, u32[]{:S(2)}, u32[]{:S(2)}) collective-permute-start(bf16[2,512,128]{2,1,0:T(8,128)(2,1)S(1)} %collective-permute-done.3.refs_4_), channel_id=1, source_target_pairs={{0,1},{1,0},{2,3},{3,2},{4,5},{5,4},{6,7},{7,6},{8,9},{9,8},{10,11... | collective-permute-start | bytes 786440 | tf_op jit(solution)/shard_map/ppermute | solution.py:588
  33.3 20.6 %collective-permute-start.2 = (bf16[2,512,128]{2,1,0:T(8,128)(2,1)S(1)}, bf16[2,512,128]{2,1,0:T(8,128)(2,1)}, u32[]{:S(2)}, u32[]{:S(2)}) collective-permute-start(bf16[2,512,128]{2,1,0:T(8,128)(2,1)S(1)} %collective-permute-done.1.refs_2_), channel_id=1, source_target_pairs={{0,1},{1,0},{2,3},{3,2},{4,5},{5,4},{6,7},{7,6},{8,9},{9,8},{10,11... | collective-permute-start | bytes 786440 | tf_op jit(solution)/shard_map/ppermute | solution.py:588
  45.8 8.0 %copy-start.5 = (s32[16]{0:T(128)S(1)}, s32[16]{0:T(128)}, u32[]{:S(2)}) copy-start(s32[16]{0:T(128)} %order.3) | copy-start | bytes 196
  47.1 24.3 %all-to-all-start.1 = ((bf16[16,256,128]{2,1,0:T(8,128)(2,1)}), bf16[16,256,128]{2,1,0:T(8,128)(2,1)}, u32[]{:S(2)}, u32[]{:S(2)}) async-start(bf16[16,256,128]{2,1,0:T(8,128)(2,1)} %scan.1), calls=%async_computation.1 | async-start | bytes 2097152 | tf_op jit(solution)/shard_map/all_to_all | solution.py:648
  59.7 1.3 %collective-permute-start.7 = (f32[3,8,512]{2,1,0:T(8,128)S(1)}, f32[3,8,512]{2,1,0:T(8,128)S(1)}, u32[]{:S(2)}, u32[]{:S(2)}) collective-permute-start(f32[3,8,512]{2,1,0:T(8,128)S(1)} %get-tuple-element.53), channel_id=1, source_target_pairs={{0,1},{1,0},{2,3},{3,2},{4,5},{5,4},{6,7},{7,6},{8,9},{9,8},{10,11... | collective-permute-start | bytes 147464 | tf_op jit(solution)/shard_map/ppermute | solution.py:588
  61.1 10.3 %collective-permute-start.10 = (f32[3,8,512]{2,1,0:T(8,128)S(1)}, f32[3,8,512]{2,1,0:T(8,128)}, u32[]{:S(2)}, u32[]{:S(2)}) collective-permute-start(f32[3,8,512]{2,1,0:T(8,128)S(1)} %pad_maximum_fusion.refs_8_), channel_id=1, source_target_pairs={{0,4},{1,5},{2,6},{3,7},{4,0},{5,1},{6,2},{7,3},{8,12},{9,13},{10,... | collective-permute-start | bytes 147464 | tf_op jit(solution)/shard_map/ppermute | solution.py:588
  63.9 7.5 %collective-permute-start.9 = (f32[3,8,512]{2,1,0:T(8,128)S(1)}, f32[3,8,512]{2,1,0:T(8,128)}, u32[]{:S(2)}, u32[]{:S(2)}) collective-permute-start(f32[3,8,512]{2,1,0:T(8,128)S(1)} %pad_maximum_fusion.refs_8_), channel_id=1, source_target_pairs={{0,6},{1,7},{2,4},{3,5},{4,2},{5,3},{6,0},{7,1},{8,14},{9,15},{10,... | collective-permute-start | bytes 147464 | tf_op jit(solution)/shard_map/ppermute | solution.py:588
  64.7 6.7 %collective-permute-start.8 = (f32[3,8,512]{2,1,0:T(8,128)S(1)}, f32[3,8,512]{2,1,0:T(8,128)}, u32[]{:S(2)}, u32[]{:S(2)}) collective-permute-start(f32[3,8,512]{2,1,0:T(8,128)S(1)} %pad_maximum_fusion.refs_8_), channel_id=1, source_target_pairs={{0,2},{1,3},{2,0},{3,1},{4,6},{5,7},{6,4},{7,5},{8,10},{9,11},{10,... | collective-permute-start | bytes 147464 | tf_op jit(solution)/shard_map/ppermute | solution.py:588
  82.4 6.4 %collective-permute-start.11 = (bf16[128,512]{1,0:T(8,128)(2,1)}, bf16[128,512]{1,0:T(8,128)(2,1)S(1)}, u32[]{:S(2)}, u32[]{:S(2)}) collective-permute-start(bf16[128,512]{1,0:T(8,128)(2,1)} %get-tuple-element.58), channel_id=1, source_target_pairs={{0,1},{1,0},{2,3},{3,2},{4,5},{5,4},{6,7},{7,6},{8,9},{9,8},{10,11... | collective-permute-start | bytes 393224 | tf_op jit(solution)/shard_map/ppermute | solution.py:588
  83.9 4.9 %collective-permute-start.12 = (bf16[128,512]{1,0:T(8,128)(2,1)}, bf16[128,512]{1,0:T(8,128)(2,1)S(1)}, u32[]{:S(2)}, u32[]{:S(2)}) collective-permute-start(bf16[128,512]{1,0:T(8,128)(2,1)} %get-tuple-element.59), channel_id=1, source_target_pairs={{0,1},{1,0},{2,3},{3,2},{4,5},{5,4},{6,7},{7,6},{8,9},{9,8},{10,11... | collective-permute-start | bytes 393224 | tf_op jit(solution)/shard_map/ppermute | solution.py:588
  84.0 4.8 %collective-permute-start.13 = (bf16[128,512]{1,0:T(8,128)(2,1)}, bf16[128,512]{1,0:T(8,128)(2,1)S(1)}, u32[]{:S(2)}, u32[]{:S(2)}) collective-permute-start(bf16[128,512]{1,0:T(8,128)(2,1)} %get-tuple-element.60), channel_id=1, source_target_pairs={{0,1},{1,0},{2,3},{3,2},{4,5},{5,4},{6,7},{7,6},{8,9},{9,8},{10,11... | collective-permute-start | bytes 393224 | tf_op jit(solution)/shard_map/ppermute | solution.py:588
  84.5 22.9 %all-to-all-start.2 = ((bf16[16,128,128]{2,1,0:T(8,128)(2,1)}), bf16[16,128,128]{2,1,0:T(8,128)(2,1)S(1)}, u32[]{:S(2)}, u32[]{:S(2)}) async-start(bf16[16,128,128]{2,1,0:T(8,128)(2,1)} %get-tuple-element.54), calls=%async_computation.2 | async-start | bytes 1048576 | tf_op jit(solution)/shard_map/all_to_all | solution.py:655
  88.4 21.0 %collective-permute-start.14 = (bf16[128,512]{1,0:T(8,128)(2,1)}, bf16[128,512]{1,0:T(8,128)(2,1)S(1)}, u32[]{:S(2)}, u32[]{:S(2)}) collective-permute-start(bf16[128,512]{1,0:T(8,128)(2,1)} %get-tuple-element.74), channel_id=1, source_target_pairs={{0,1},{1,0},{2,3},{3,2},{4,5},{5,4},{6,7},{7,6},{8,9},{9,8},{10,11... | collective-permute-start | bytes 393224 | tf_op jit(solution)/shard_map/ppermute | solution.py:588
  88.8 0.9 copy-start.1
  89.8 0.9 copy-start.2
  90.7 0.9 copy-start.3
  91.7 17.7 %collective-permute-start.15 = (bf16[128,512]{1,0:T(8,128)(2,1)S(1)}, bf16[128,512]{1,0:T(8,128)(2,1)S(1)}, u32[]{:S(2)}, u32[]{:S(2)}) collective-permute-start(bf16[128,512]{1,0:T(8,128)(2,1)S(1)} %get-tuple-element.61), channel_id=1, source_target_pairs={{0,2},{1,3},{2,0},{3,1},{4,6},{5,7},{6,4},{7,5},{8,10},{9,11},{10,... | collective-permute-start | bytes 393224 | tf_op jit(solution)/shard_map/ppermute | solution.py:588
  92.3 18.5 %collective-permute-start.17 = (bf16[128,512]{1,0:T(8,128)(2,1)S(1)}, bf16[128,512]{1,0:T(8,128)(2,1)S(1)}, u32[]{:S(2)}, u32[]{:S(2)}) collective-permute-start(bf16[128,512]{1,0:T(8,128)(2,1)S(1)} %get-tuple-element.62), channel_id=1, source_target_pairs={{0,4},{1,5},{2,6},{3,7},{4,0},{5,1},{6,2},{7,3},{8,12},{9,13},{10,... | collective-permute-start | bytes 393224 | tf_op jit(solution)/shard_map/ppermute | solution.py:588
  94.8 21.6 %collective-permute-start.16 = (bf16[128,512]{1,0:T(8,128)(2,1)S(1)}, bf16[128,512]{1,0:T(8,128)(2,1)S(1)}, u32[]{:S(2)}, u32[]{:S(2)}) collective-permute-start(bf16[128,512]{1,0:T(8,128)(2,1)S(1)} %get-tuple-element.63), channel_id=1, source_target_pairs={{0,6},{1,7},{2,4},{3,5},{4,2},{5,3},{6,0},{7,1},{8,14},{9,15},{10,... | collective-permute-start | bytes 393224 | tf_op jit(solution)/shard_map/ppermute | solution.py:588
  95.6 21.9 %copy-start = (bf16[128,512]{1,0:T(8,128)(2,1)S(1)}, bf16[128,512]{1,0:T(8,128)(2,1)}, u32[]{:S(2)}) copy-start(bf16[128,512]{1,0:T(8,128)(2,1)} %get-tuple-element.73.refs_0_) | copy-start | bytes 393220
  107.4 5.2 %collective-permute-start.23 = (bf16[128,128]{1,0:T(8,128)(2,1)S(1)}, bf16[128,128]{1,0:T(8,128)(2,1)S(1)}, u32[]{:S(2)}, u32[]{:S(2)}) collective-permute-start(bf16[128,128]{1,0:T(8,128)(2,1)S(1)} %reduce_sum.12.refs_5_), channel_id=1, source_target_pairs={{0,6},{1,7},{2,4},{3,5},{4,2},{5,3},{6,0},{7,1},{8,14},{9,15},{10,... | collective-permute-start | bytes 98312 | tf_op jit(solution)/shard_map/ppermute | solution.py:588
  109.4 4.3 %collective-permute-start.21 = (bf16[128,128]{1,0:T(8,128)(2,1)S(1)}, bf16[128,128]{1,0:T(8,128)(2,1)S(1)}, u32[]{:S(2)}, u32[]{:S(2)}) collective-permute-start(bf16[128,128]{1,0:T(8,128)(2,1)S(1)} %reduce_sum.12.refs_5_), channel_id=1, source_target_pairs={{0,4},{1,5},{2,6},{3,7},{4,0},{5,1},{6,2},{7,3},{8,12},{9,13},{10,... | collective-permute-start | bytes 98312 | tf_op jit(solution)/shard_map/ppermute | solution.py:588
  109.4 6.9 %collective-permute-start.19 = (bf16[128,128]{1,0:T(8,128)(2,1)S(1)}, bf16[128,128]{1,0:T(8,128)(2,1)S(1)}, u32[]{:S(2)}, u32[]{:S(2)}) collective-permute-start(bf16[128,128]{1,0:T(8,128)(2,1)S(1)} %reduce_sum.12.refs_5_), channel_id=1, source_target_pairs={{0,2},{1,3},{2,0},{3,1},{4,6},{5,7},{6,4},{7,5},{8,10},{9,11},{10,... | collective-permute-start | bytes 98312 | tf_op jit(solution)/shard_map/ppermute | solution.py:588
  110.8 5.6 %collective-permute-start.18 = (bf16[128,128]{1,0:T(8,128)(2,1)S(1)}, bf16[128,128]{1,0:T(8,128)(2,1)S(1)}, u32[]{:S(2)}, u32[]{:S(2)}) collective-permute-start(bf16[128,128]{1,0:T(8,128)(2,1)S(1)} %reduce_sum.12.refs_5_), channel_id=1, source_target_pairs={{0,1},{1,0},{2,3},{3,2},{4,5},{5,4},{6,7},{7,6},{8,9},{9,8},{10,11... | collective-permute-start | bytes 98312 | tf_op jit(solution)/shard_map/ppermute | solution.py:588
  112.6 3.7 %collective-permute-start.24 = (bf16[128,128]{1,0:T(8,128)(2,1)S(1)}, bf16[128,128]{1,0:T(8,128)(2,1)S(1)}, u32[]{:S(2)}, u32[]{:S(2)}) collective-permute-start(bf16[128,128]{1,0:T(8,128)(2,1)S(1)} %collective-permute-done.23.refs_11_), channel_id=1, source_target_pairs={{0,1},{1,0},{2,3},{3,2},{4,5},{5,4},{6,7},{7,6},{8,9},{9,8},{10,11... | collective-permute-start | bytes 98312 | tf_op jit(solution)/shard_map/ppermute | solution.py:588
  113.6 3.5 %collective-permute-start.22 = (bf16[128,128]{1,0:T(8,128)(2,1)S(1)}, bf16[128,128]{1,0:T(8,128)(2,1)S(1)}, u32[]{:S(2)}, u32[]{:S(2)}) collective-permute-start(bf16[128,128]{1,0:T(8,128)(2,1)S(1)} %collective-permute-done.21.refs_9_), channel_id=1, source_target_pairs={{0,1},{1,0},{2,3},{3,2},{4,5},{5,4},{6,7},{7,6},{8,9},{9,8},{10,11... | collective-permute-start | bytes 98312 | tf_op jit(solution)/shard_map/ppermute | solution.py:588
  116.3 1.2 %collective-permute-start.20 = (bf16[128,128]{1,0:T(8,128)(2,1)S(1)}, bf16[128,128]{1,0:T(8,128)(2,1)S(1)}, u32[]{:S(2)}, u32[]{:S(2)}) collective-permute-start(bf16[128,128]{1,0:T(8,128)(2,1)S(1)} %collective-permute-done.19.refs_7_), channel_id=1, source_target_pairs={{0,1},{1,0},{2,3},{3,2},{4,5},{5,4},{6,7},{7,6},{8,9},{9,8},{10,11... | collective-permute-start | bytes 98312 | tf_op jit(solution)/shard_map/ppermute | solution.py:588

commit v7 on v6

--- a/solution.py
+++ b/solution.py
@@ -238,7 +238,7 @@
         ],
         compiler_params=pltpu.CompilerParams(vmem_limit_bytes=20 << 20),
         cost_estimate=pl.CostEstimate(
-            flops=4 * 10**9, bytes_accessed=5 * 10**6, transcendentals=10**6
+            flops=10**8, bytes_accessed=10**5, transcendentals=10**4
         ),
         name="attn_stat",
     )(order, recv, *qd)
@@ -328,7 +328,7 @@
         ],
         compiler_params=pltpu.CompilerParams(vmem_limit_bytes=20 << 20),
         cost_estimate=pl.CostEstimate(
-            flops=8 * 10**9, bytes_accessed=6 * 10**6, transcendentals=10**6
+            flops=10**8, bytes_accessed=10**5, transcendentals=10**4
         ),
         name="attn_grad",
     )(order, recv, *qd, *stats)
@@ -598,18 +598,24 @@
     return jnp.stack([top, f * a[1] + g * b[1], f * a[2] + g * b[2]])
 
 
-def gather_heads(v):
+def gather_heads(v, other=None):
     out = [v] + [None] * 7
     for m in (2, 6, 4):
-        out[m] = swap(v, m)
+        out[m] = swap(v, m) if other is None else after(swap(v, m), other)
     for m in (0, 2, 6, 4):
         out[m + 1] = swap(out[m], 1)
     return out
 
 
 def pair_sums_kernel(*refs):
-    for a, b, o in zip(refs[:3], refs[3:6], refs[6:]):
-        o[...] = (a[...].astype(F32) + b[...].astype(F32)).astype(BF)
+    own, mates, outs, (held, sem) = refs[:3], refs[3:6], refs[6:9], refs[9:]
+    moves = [pltpu.make_async_copy(r, held.at[i], sem.at[i]) for i, r in enumerate(own)]
+    for m in moves:
+        m.start()
+    for m in moves:
+        m.wait()
+    for i in range(3):
+        outs[i][...] = (held[i].astype(F32) + mates[i][...].astype(F32)).astype(BF)
 
 
 def pair_sums(parts):
@@ -617,12 +623,16 @@
     out = jax.ShapeDtypeStruct(parts[0].shape, BF)
     sums = pl.pallas_call(
         pair_sums_kernel,
-        in_specs=[VM] * 6,
+        in_specs=[HB] * 3 + [VM] * 3,
         out_specs=[VM] * 3,
         out_shape=[out] * 3,
+        scratch_shapes=[
+            pltpu.VMEM((3,) + parts[0].shape, BF),
+            pltpu.SemaphoreType.DMA((3,)),
+        ],
         compiler_params=pltpu.CompilerParams(vmem_limit_bytes=16 << 20),
         name="pair_sums",
-    )(*parts[2::2], *mates[1:])
+    )(*[pltpu.with_memory_space_constraint(p, pltpu.HBM) for p in parts[2::2]], *mates[1:])
     return [parts[0], mates[0]], sums
 
 
@@ -642,14 +652,15 @@
         queries.reshape(tok, 128), attn_cotangent.reshape(tok, 128),
     )
     recv = lax.all_to_all(send, "seq", 0, 0)
-    qds = gather_heads(qd)
     local = ssd_local(xh, yh, cum, b, c)
-    turned = scan(after(recv, local[2]))
+    qds = gather_heads(qd, local[2])
+    turned = scan(after(recv, qds))
     states = lax.all_to_all(turned, "seq", 0, 0)
     first, mate = attn_stat(pair_order, after(recv, turned), qds)
     stat = join(first, swap(mate, 1))
     rest = [swap(stat, m) for m in (2, 6, 4)]
-    back, *dqt = attn_grad(pair_order, after(recv, states), qds, stat, *rest)
+    back, *dqt = attn_grad(pair_order, recv, qds, stat, *rest)
+    back, *dqt = after([back, *dqt], states)
     kept, sums = pair_sums(dqt)
     dx, da, db, dc = ssd_grad(after(xh, (back, *sums)), yh, states, cum, b, c, local)
     back = lax.all_to_all(back, "seq", 0, 0)

time: 119 us -> 112 us (0.941)
  waiting for transfers between devices: 17.3 us -> 11.1 us
    all_to_all x1, waiting for transfers between devices: 6.64 us -> 0.01 us  [per_device(): states = lax.all_to_all(turned, 'seq', 0, 0)]
    all_to_all x1, waiting for transfers between devices: 0.01 us -> 3.66 us  [per_device(): recv = lax.all_to_all(send, 'seq', 0, 0)]
    ppermute x25, waiting for transfers between devices: 10.7 us -> 7.47 us  [swap(): return lax.ppermute(v, 'head', [(i, i ^ m) for i in range(8)])]
    all_to_all x1, starting transfers between devices: 3.94 us -> 6.83 us  [per_device(): back = lax.all_to_all(back, 'seq', 0, 0)]
    all_to_all x1, starting transfers between devices: 6.71 us -> 4.62 us  [per_device(): states = lax.all_to_all(turned, 'seq', 0, 0)]
    unnamed x12 -> x10, local copies, waits for them, and re-layouts: 2.72 us -> 1.66 us
  transfers between devices with their start and end apart: 28 -> 28, of which waited for: 5 -> 9; matrix products, arithmetic and copies ran while one was open for 0% -> 0% of each run, Pallas kernels for 26% -> 36%
where the time goes in v7:
time: 112 us; the launch traced here: 111 us
  Pallas kernels  50.9 us (45%)
  starting transfers between devices  46.8 us (42%)
  waiting for transfers between devices  11.1 us (10%)
  local copies, waits for them, and re-layouts  1.66 us (1%)
    ppermute x25, starting transfers between devices, swap(): return lax.ppermute(v, 'head', [(i, i ^ m) for i in range(8)])  26.6 us
    pallas_call x1, Pallas kernels, ssd_local(): pl.pallas_call(ssd_local_kernel, grid=(heads // STEP_HEADS,), in_specs=[p...  11.9 us
    pallas_call x1, Pallas kernels, ssd_grad(): pl.pallas_call(ssd_grad_kernel, grid=(heads // STEP_HEADS,), in_specs=[pe...  11.7 us
    pallas_call x1, Pallas kernels, attn_grad(): pl.pallas_call(attn_grad_kernel, in_specs=[SM] + [VM] * 13, out_specs=[HB...  10.5 us
    all_to_all x1, starting transfers between devices, per_device(): recv = lax.all_to_all(send, 'seq', 0, 0)  8.74 us
    pallas_call x1, Pallas kernels, ssd_send(): pl.pallas_call(ssd_send_kernel, grid_spec=pltpu.PrefetchScalarGridSpec(nu...  8.22 us
    ppermute x25, waiting for transfers between devices, swap(): return lax.ppermute(v, 'head', [(i, i ^ m) for i in range(8)])  7.47 us
    all_to_all x1, starting transfers between devices, per_device(): back = lax.all_to_all(back, 'seq', 0, 0)  6.83 us
  transfers between devices with their start and end apart: 28, of which 9 were waited for; matrix products, arithmetic and copies ran while one was open for 0% of the time, Pallas kernels for 36%

profile of v7, /device:TPU:1, one launch (start us, length us, event | category | flops | bytes accessed | tf_op | source)
XLA Modules:
  0.0 111.4 jit_solution(11666101158342069253)
XLA Ops:
  0.6 8.2 %ssd_send.1 = (bf16[16,400,128]{2,1,0:T(8,128)(2,1)}, bf16[16,512,128]{2,1,0:T(8,128)(2,1)}, bf16[16,512,128]{2,1,0:T(8,128)(2,1)}, f32[16,512]{1,0:T(8,128)}, bf16[2,512,128]{2,1,0:T(8,128)(2,1)}) custom-call(bf16[512,16,128]{2,1,0:T(8,128)(2,1)} %x_ref.1, bf16[512,16,128]{2,1,0:T(8,128)(2,1)} %y_ref.1, f32[16,512]{1,0:T(8,128)} %bitcast.22, ...), custom_call_target="tpu_custom_call" | custom-call | flops 3000000000 | bytes 10000000 | tf_op jit(solution)/shard_map/ssd_send/pallas_call | solution.py:105
  8.9 0.0 copy-start
  8.9 8.7 %all-to-all-start = ((bf16[16,400,128]{2,1,0:T(8,128)(2,1)}), bf16[16,400,128]{2,1,0:T(8,128)(2,1)S(1)}, u32[]{:S(2)}, u32[]{:S(2)}) async-start(bf16[16,400,128]{2,1,0:T(8,128)(2,1)} %get-tuple-element.55), calls=%async_computation | async-start | bytes 3276800 | tf_op jit(solution)/shard_map/all_to_all | solution.py:654
  17.6 2.6 %collective-permute-start.5 = (bf16[2,512,128]{2,1,0:T(8,128)(2,1)S(1)}, bf16[2,512,128]{2,1,0:T(8,128)(2,1)S(1)}, u32[]{:S(2)}, u32[]{:S(2)}) collective-permute-start(bf16[2,512,128]{2,1,0:T(8,128)(2,1)S(1)} %copy-done), channel_id=1, source_target_pairs={{0,6},{1,7},{2,4},{3,5},{4,2},{5,3},{6,0},{7,1},{8,14},{9,15},{10,... | collective-permute-start | bytes 786440 | tf_op jit(solution)/shard_map/ppermute | solution.py:588
  20.2 0.5 collective-permute-start.3
  20.7 0.3 collective-permute-start.1
  21.0 1.8 %collective-permute-start = (bf16[2,512,128]{2,1,0:T(8,128)(2,1)S(1)}, bf16[2,512,128]{2,1,0:T(8,128)(2,1)S(1)}, u32[]{:S(2)}, u32[]{:S(2)}) collective-permute-start(bf16[2,512,128]{2,1,0:T(8,128)(2,1)S(1)} %copy-done), channel_id=1, source_target_pairs={{0,1},{1,0},{2,3},{3,2},{4,5},{5,4},{6,7},{7,6},{8,9},{9,8},{10,11... | collective-permute-start | bytes 786440 | tf_op jit(solution)/shard_map/ppermute | solution.py:588
  22.8 11.9 %ssd_local.1 = (bf16[16,512,128]{2,1,0:T(8,128)(2,1)}, bf16[16,6,128,128]{3,2,1,0:T(8,128)(2,1)}, f32[16,512]{1,0:T(8,128)}, f32[512,128]{1,0:T(8,128)}, f32[512,128]{1,0:T(8,128)}) custom-call(bf16[16,512,128]{2,1,0:T(8,128)(2,1)} %get-tuple-element.86.xh, bf16[16,512,128]{2,1,0:T(8,128)(2,1)} %get-tuple-element.57.yh, f32[16,512]{1,0:T(8,128)} %get-tuple-element.58.cum, ...), custom_call_target="tpu_custom_call" | custom-call | flops 4000000000 | bytes 10000000 | tf_op jit(solution)/shard_map/ssd_local/pallas_call | solution.py:425
  34.6 0.0 collective-permute-done.5.refs_6_
  34.7 0.0 copy-start.4
  34.7 0.0 collective-permute-done.3.refs_4_
  34.7 0.0 collective-permute-done.1.refs_2_
  34.7 0.1 collective-permute-start.2
  34.8 0.5 collective-permute-start.4
  35.3 0.1 collective-permute-start.6
  35.4 0.0 collective-permute-done.refs_1_
  35.4 0.9 collective-permute-done.2.refs_3_
  36.3 0.4 collective-permute-done.4.refs_5_
  36.7 0.4 collective-permute-done.6.refs_7_
  37.1 0.7 copy-done.1
  37.8 3.7 %all-to-all-done.recv = bf16[16,400,128]{2,1,0:T(8,128)(2,1)S(1)} async-done(((bf16[16,400,128]{2,1,0:T(8,128)(2,1)}), bf16[16,400,128]{2,1,0:T(8,128)(2,1)S(1)}, u32[]{:S(2)}, u32[]{:S(2)}) %all-to-all-start) | async-done | bytes 1638432 | tf_op jit(solution)/shard_map/all_to_all | solution.py:654
  41.4 1.3 %scan.1 = bf16[16,256,128]{2,1,0:T(8,128)(2,1)} custom-call(bf16[16,400,128]{2,1,0:T(8,128)(2,1)S(1)} %all-to-all-done.recv), custom_call_target="tpu_custom_call" | custom-call | tf_op jit(solution)/shard_map/scan/pallas_call | solution.py:164
  42.7 4.6 %all-to-all-start.1 = ((bf16[16,256,128]{2,1,0:T(8,128)(2,1)}), bf16[16,256,128]{2,1,0:T(8,128)(2,1)}, u32[]{:S(2)}, u32[]{:S(2)}) async-start(bf16[16,256,128]{2,1,0:T(8,128)(2,1)} %scan.1), calls=%async_computation.1 | async-start | bytes 2097152 | tf_op jit(solution)/shard_map/all_to_all | solution.py:658
  47.3 0.0 copy-start.2
  47.3 0.9 copy-done.2
  48.3 5.3 %attn_stat.1 = (f32[3,8,512]{2,1,0:T(8,128)S(1)}, f32[3,8,512]{2,1,0:T(8,128)S(1)}) custom-call(s32[16]{0:T(128)S(1)} %copy-done.4, bf16[16,400,128]{2,1,0:T(8,128)(2,1)S(1)} %all-to-all-done.recv, bf16[2,512,128]{2,1,0:T(8,128)(2,1)S(1)} %copy-done, bf16[2,512,128]{2,1,0:T(8,128)(2,1)S(1)} %collective-permute-done.refs_1_, ...), custom_call_target="tpu_custom_call" | custom-call | flops 100000000 | bytes 100000 | tf_op jit(solution)/shard_map/attn_stat/pallas_call | solution.py:229
  53.6 2.3 %collective-permute-start.7 = (f32[3,8,512]{2,1,0:T(8,128)S(1)}, f32[3,8,512]{2,1,0:T(8,128)S(1)}, u32[]{:S(2)}, u32[]{:S(2)}) collective-permute-start(f32[3,8,512]{2,1,0:T(8,128)S(1)} %get-tuple-element.66), channel_id=1, source_target_pairs={{0,1},{1,0},{2,3},{3,2},{4,5},{5,4},{6,7},{7,6},{8,9},{9,8},{10,11... | collective-permute-start | bytes 147464 | tf_op jit(solution)/shard_map/ppermute | solution.py:588
  55.8 0.9 collective-permute-done.7
  56.8 2.8 %collective-permute-start.10 = (f32[3,8,512]{2,1,0:T(8,128)S(1)}, f32[3,8,512]{2,1,0:T(8,128)S(1)}, u32[]{:S(2)}, u32[]{:S(2)}) collective-permute-start(f32[3,8,512]{2,1,0:T(8,128)S(1)} %pad_maximum_fusion.refs_8_), channel_id=1, source_target_pairs={{0,4},{1,5},{2,6},{3,7},{4,0},{5,1},{6,2},{7,3},{8,12},{9,13},{10,... | collective-permute-start | bytes 147464 | tf_op jit(solution)/shard_map/ppermute | solution.py:588
  59.6 0.9 collective-permute-start.9
  60.5 0.0 collective-permute-start.8
  60.5 1.2 %collective-permute-done.10.refs_11_ = f32[3,8,512]{2,1,0:T(8,128)S(1)} collective-permute-done((f32[3,8,512]{2,1,0:T(8,128)S(1)}, f32[3,8,512]{2,1,0:T(8,128)S(1)}, u32[]{:S(2)}, u32[]{:S(2)}) %collective-permute-start.10) | collective-permute-done | bytes 49184 | tf_op jit(solution)/shard_map/ppermute | solution.py:588
  61.7 2.5 %collective-permute-done.9.refs_10_ = f32[3,8,512]{2,1,0:T(8,128)S(1)} collective-permute-done((f32[3,8,512]{2,1,0:T(8,128)S(1)}, f32[3,8,512]{2,1,0:T(8,128)S(1)}, u32[]{:S(2)}, u32[]{:S(2)}) %collective-permute-start.9) | collective-permute-done | bytes 49184 | tf_op jit(solution)/shard_map/ppermute | solution.py:588
  64.2 0.0 collective-permute-done.8.refs_9_
  64.2 10.5 %attn_grad.1 = (bf16[16,128,128]{2,1,0:T(8,128)(2,1)}, bf16[128,512]{1,0:T(8,128)(2,1)}, bf16[128,512]{1,0:T(8,128)(2,1)}, bf16[128,512]{1,0:T(8,128)(2,1)}, bf1...) custom-call(s32[16]{0:T(128)S(1)} %copy-done.4, ...), custom_call_target="tpu_custom_call" | custom-call | flops 100000000 | bytes 100000 | tf_op jit(solution)/shard_map/attn_grad/pallas_call | solution.py:311
  74.6 0.0 all-to-all-done.1.states
  74.7 1.5 %collective-permute-start.11 = (bf16[128,512]{1,0:T(8,128)(2,1)}, bf16[128,512]{1,0:T(8,128)(2,1)S(1)}, u32[]{:S(2)}, u32[]{:S(2)}) collective-permute-start(bf16[128,512]{1,0:T(8,128)(2,1)} %get-tuple-element.80), channel_id=1, source_target_pairs={{0,1},{1,0},{2,3},{3,2},{4,5},{5,4},{6,7},{7,6},{8,9},{9,8},{10,11... | collective-permute-start | bytes 393224 | tf_op jit(solution)/shard_map/ppermute | solution.py:588
  76.1 0.1 collective-permute-start.12
  76.2 0.4 collective-permute-start.13
  76.6 6.8 %all-to-all-start.2 = ((bf16[16,128,128]{2,1,0:T(8,128)(2,1)}), bf16[16,128,128]{2,1,0:T(8,128)(2,1)S(1)}, u32[]{:S(2)}, u32[]{:S(2)}) async-start(bf16[16,128,128]{2,1,0:T(8,128)(2,1)} %get-tuple-element.76), calls=%async_computation.2 | async-start | bytes 1048576 | tf_op jit(solution)/shard_map/all_to_all | solution.py:666
  83.5 0.4 collective-permute-start.14
  83.9 0.0 collective-permute-done.12.refs_4_
  83.9 0.0 collective-permute-done.13.refs_5_
  83.9 1.2 %pair_sums.1 = (bf16[128,512]{1,0:T(8,128)(2,1)S(1)}, bf16[128,512]{1,0:T(8,128)(2,1)S(1)}, bf16[128,512]{1,0:T(8,128)(2,1)S(1)}) custom-call(bf16[128,512]{1,0:T(8,128)(2,1)} %get-tuple-element.77.refs_0_, bf16[128,512]{1,0:T(8,128)(2,1)} %get-tuple-element.78.refs_1_, bf16[128,512]{1,0:T(8,128)(2,1)} %get-tuple-element.79.refs_2_, ...), custom_call_target="tpu_custom_call" | custom-call | tf_op jit(solution)/shard_map/pair_sums/pallas_call | solution.py:624
  85.1 0.1 collective-permute-start.15
  85.2 2.9 %collective-permute-start.17 = (bf16[128,512]{1,0:T(8,128)(2,1)S(1)}, bf16[128,512]{1,0:T(8,128)(2,1)S(1)}, u32[]{:S(2)}, u32[]{:S(2)}) collective-permute-start(bf16[128,512]{1,0:T(8,128)(2,1)S(1)} %get-tuple-element.84), channel_id=1, source_target_pairs={{0,4},{1,5},{2,6},{3,7},{4,0},{5,1},{6,2},{7,3},{8,12},{9,13},{10,... | collective-permute-start | bytes 393224 | tf_op jit(solution)/shard_map/ppermute | solution.py:588
  88.1 0.9 collective-permute-start.16
  89.0 11.7 %ssd_grad.1 = (bf16[512,16,128]{2,1,0:T(8,128)(2,1)}, f32[16,512]{1,0:T(8,128)}, f32[512,128]{1,0:T(8,128)}, f32[512,128]{1,0:T(8,128)}) custom-call(bf16[16,512,128]{2,1,0:T(8,128)(2,1)} %get-tuple-element.86.xh, bf16[16,512,128]{2,1,0:T(8,128)(2,1)} %get-tuple-element.57.yh, bf16[16,256,128]{2,1,0:T(8,128)(2,1)} %all-to-all-done.1.states, ...), custom_call_target="tpu_custom_call" | custom-call | flops 6000000000 | bytes 10000000 | tf_op jit(solution)/shard_map/ssd_grad/pallas_call | solution.py:524
  100.7 0.1 reduce_sum.12.refs_5_
  100.8 1.8 %collective-permute-start.23 = (bf16[128,128]{1,0:T(8,128)(2,1)S(1)}, bf16[128,128]{1,0:T(8,128)(2,1)S(1)}, u32[]{:S(2)}, u32[]{:S(2)}) collective-permute-start(bf16[128,128]{1,0:T(8,128)(2,1)S(1)} %reduce_sum.12.refs_5_), channel_id=1, source_target_pairs={{0,6},{1,7},{2,4},{3,5},{4,2},{5,3},{6,0},{7,1},{8,14},{9,15},{10,... | collective-permute-start | bytes 98312 | tf_op jit(solution)/shard_map/ppermute | solution.py:588
  102.6 0.0 collective-permute-done.14.refs_1_
  102.7 0.0 collective-permute-start.21
  102.7 1.5 %collective-permute-start.19 = (bf16[128,128]{1,0:T(8,128)(2,1)S(1)}, bf16[128,128]{1,0:T(8,128)(2,1)S(1)}, u32[]{:S(2)}, u32[]{:S(2)}) collective-permute-start(bf16[128,128]{1,0:T(8,128)(2,1)S(1)} %reduce_sum.12.refs_5_), channel_id=1, source_target_pairs={{0,2},{1,3},{2,0},{3,1},{4,6},{5,7},{6,4},{7,5},{8,10},{9,11},{10,... | collective-permute-start | bytes 98312 | tf_op jit(solution)/shard_map/ppermute | solution.py:588
  104.2 0.0 collective-permute-done.17.refs_4_
  104.2 1.9 %collective-permute-start.18 = (bf16[128,128]{1,0:T(8,128)(2,1)S(1)}, bf16[128,128]{1,0:T(8,128)(2,1)S(1)}, u32[]{:S(2)}, u32[]{:S(2)}) collective-permute-start(bf16[128,128]{1,0:T(8,128)(2,1)S(1)} %reduce_sum.12.refs_5_), channel_id=1, source_target_pairs={{0,1},{1,0},{2,3},{3,2},{4,5},{5,4},{6,7},{7,6},{8,9},{9,8},{10,11... | collective-permute-start | bytes 98312 | tf_op jit(solution)/shard_map/ppermute | solution.py:588
  106.0 0.0 collective-permute-done.23.refs_11_
  106.0 1.0 collective-permute-start.24
  107.0 2.3 %collective-permute-start.22 = (bf16[128,128]{1,0:T(8,128)(2,1)S(1)}, bf16[128,128]{1,0:T(8,128)(2,1)S(1)}, u32[]{:S(2)}, u32[]{:S(2)}) collective-permute-start(bf16[128,128]{1,0:T(8,128)(2,1)S(1)} %collective-permute-done.21.refs_9_), channel_id=1, source_target_pairs={{0,1},{1,0},{2,3},{3,2},{4,5},{5,4},{6,7},{7,6},{8,9},{9,8},{10,11... | collective-permute-start | bytes 98312 | tf_op jit(solution)/shard_map/ppermute | solution.py:588
  109.4 0.0 collective-permute-start.20
  109.4 0.0 collective-permute-done.16.refs_3_
  109.4 0.0 collective-permute-done.24.refs_12_
  109.4 0.8 collective-permute-done.22.refs_10_
  110.2 0.4 collective-permute-done.20.refs_8_
  110.6 0.8 finish.1
  (14 shorter events, 0.1 us)
Async XLA Ops:
  8.9 8.8 %copy-start = (bf16[2,512,128]{2,1,0:T(8,128)(2,1)S(1)}, bf16[2,512,128]{2,1,0:T(8,128)(2,1)}, u32[]{:S(2)}) copy-start(bf16[2,512,128]{2,1,0:T(8,128)(2,1)} %get-tuple-element.56.refs_0_) | copy-start | bytes 786436
  8.9 32.5 %all-to-all-start = ((bf16[16,400,128]{2,1,0:T(8,128)(2,1)}), bf16[16,400,128]{2,1,0:T(8,128)(2,1)S(1)}, u32[]{:S(2)}, u32[]{:S(2)}) async-start(bf16[16,400,128]{2,1,0:T(8,128)(2,1)} %get-tuple-element.55), calls=%async_computation | async-start | bytes 3276800 | tf_op jit(solution)/shard_map/all_to_all | solution.py:654
  17.6 17.0 %collective-permute-start.5 = (bf16[2,512,128]{2,1,0:T(8,128)(2,1)S(1)}, bf16[2,512,128]{2,1,0:T(8,128)(2,1)S(1)}, u32[]{:S(2)}, u32[]{:S(2)}) collective-permute-start(bf16[2,512,128]{2,1,0:T(8,128)(2,1)S(1)} %copy-done), channel_id=1, source_target_pairs={{0,6},{1,7},{2,4},{3,5},{4,2},{5,3},{6,0},{7,1},{8,14},{9,15},{10,... | collective-permute-start | bytes 786440 | tf_op jit(solution)/shard_map/ppermute | solution.py:588
  20.2 14.5 %collective-permute-start.3 = (bf16[2,512,128]{2,1,0:T(8,128)(2,1)S(1)}, bf16[2,512,128]{2,1,0:T(8,128)(2,1)S(1)}, u32[]{:S(2)}, u32[]{:S(2)}) collective-permute-start(bf16[2,512,128]{2,1,0:T(8,128)(2,1)S(1)} %copy-done), channel_id=1, source_target_pairs={{0,4},{1,5},{2,6},{3,7},{4,0},{5,1},{6,2},{7,3},{8,12},{9,13},{10,... | collective-permute-start | bytes 786440 | tf_op jit(solution)/shard_map/ppermute | solution.py:588
  20.7 14.0 %collective-permute-start.1 = (bf16[2,512,128]{2,1,0:T(8,128)(2,1)S(1)}, bf16[2,512,128]{2,1,0:T(8,128)(2,1)S(1)}, u32[]{:S(2)}, u32[]{:S(2)}) collective-permute-start(bf16[2,512,128]{2,1,0:T(8,128)(2,1)S(1)} %copy-done), channel_id=1, source_target_pairs={{0,2},{1,3},{2,0},{3,1},{4,6},{5,7},{6,4},{7,5},{8,10},{9,11},{10,... | collective-permute-start | bytes 786440 | tf_op jit(solution)/shard_map/ppermute | solution.py:588
  21.0 14.4 %collective-permute-start = (bf16[2,512,128]{2,1,0:T(8,128)(2,1)S(1)}, bf16[2,512,128]{2,1,0:T(8,128)(2,1)S(1)}, u32[]{:S(2)}, u32[]{:S(2)}) collective-permute-start(bf16[2,512,128]{2,1,0:T(8,128)(2,1)S(1)} %copy-done), channel_id=1, source_target_pairs={{0,1},{1,0},{2,3},{3,2},{4,5},{5,4},{6,7},{7,6},{8,9},{9,8},{10,11... | collective-permute-start | bytes 786440 | tf_op jit(solution)/shard_map/ppermute | solution.py:588
  34.7 12.6 %copy-start.4 = (s32[16]{0:T(128)S(1)}, s32[16]{0:T(128)}, u32[]{:S(2)}) copy-start(s32[16]{0:T(128)} %order.3) | copy-start | bytes 196
  34.7 1.6 %collective-permute-start.2 = (bf16[2,512,128]{2,1,0:T(8,128)(2,1)S(1)}, bf16[2,512,128]{2,1,0:T(8,128)(2,1)S(1)}, u32[]{:S(2)}, u32[]{:S(2)}) collective-permute-start(bf16[2,512,128]{2,1,0:T(8,128)(2,1)S(1)} %collective-permute-done.1.refs_2_), channel_id=1, source_target_pairs={{0,1},{1,0},{2,3},{3,2},{4,5},{5,4},{6,7},{7,6},{8,9},{9,8},{10,11... | collective-permute-start | bytes 786440 | tf_op jit(solution)/shard_map/ppermute | solution.py:588
  34.8 1.9 %collective-permute-start.4 = (bf16[2,512,128]{2,1,0:T(8,128)(2,1)S(1)}, bf16[2,512,128]{2,1,0:T(8,128)(2,1)S(1)}, u32[]{:S(2)}, u32[]{:S(2)}) collective-permute-start(bf16[2,512,128]{2,1,0:T(8,128)(2,1)S(1)} %collective-permute-done.3.refs_4_), channel_id=1, source_target_pairs={{0,1},{1,0},{2,3},{3,2},{4,5},{5,4},{6,7},{7,6},{8,9},{9,8},{10,11... | collective-permute-start | bytes 786440 | tf_op jit(solution)/shard_map/ppermute | solution.py:588
  35.3 1.8 %collective-permute-start.6 = (bf16[2,512,128]{2,1,0:T(8,128)(2,1)S(1)}, bf16[2,512,128]{2,1,0:T(8,128)(2,1)S(1)}, u32[]{:S(2)}, u32[]{:S(2)}) collective-permute-start(bf16[2,512,128]{2,1,0:T(8,128)(2,1)S(1)} %collective-permute-done.5.refs_6_), channel_id=1, source_target_pairs={{0,1},{1,0},{2,3},{3,2},{4,5},{5,4},{6,7},{7,6},{8,9},{9,8},{10,11... | collective-permute-start | bytes 786440 | tf_op jit(solution)/shard_map/ppermute | solution.py:588
  37.1 0.7 copy-start.1
  42.7 32.0 %all-to-all-start.1 = ((bf16[16,256,128]{2,1,0:T(8,128)(2,1)}), bf16[16,256,128]{2,1,0:T(8,128)(2,1)}, u32[]{:S(2)}, u32[]{:S(2)}) async-start(bf16[16,256,128]{2,1,0:T(8,128)(2,1)} %scan.1), calls=%async_computation.1 | async-start | bytes 2097152 | tf_op jit(solution)/shard_map/all_to_all | solution.py:658
  47.3 1.0 copy-start.2
  53.6 3.1 %collective-permute-start.7 = (f32[3,8,512]{2,1,0:T(8,128)S(1)}, f32[3,8,512]{2,1,0:T(8,128)S(1)}, u32[]{:S(2)}, u32[]{:S(2)}) collective-permute-start(f32[3,8,512]{2,1,0:T(8,128)S(1)} %get-tuple-element.66), channel_id=1, source_target_pairs={{0,1},{1,0},{2,3},{3,2},{4,5},{5,4},{6,7},{7,6},{8,9},{9,8},{10,11... | collective-permute-start | bytes 147464 | tf_op jit(solution)/shard_map/ppermute | solution.py:588
  56.8 4.9 %collective-permute-start.10 = (f32[3,8,512]{2,1,0:T(8,128)S(1)}, f32[3,8,512]{2,1,0:T(8,128)S(1)}, u32[]{:S(2)}, u32[]{:S(2)}) collective-permute-start(f32[3,8,512]{2,1,0:T(8,128)S(1)} %pad_maximum_fusion.refs_8_), channel_id=1, source_target_pairs={{0,4},{1,5},{2,6},{3,7},{4,0},{5,1},{6,2},{7,3},{8,12},{9,13},{10,... | collective-permute-start | bytes 147464 | tf_op jit(solution)/shard_map/ppermute | solution.py:588
  59.6 4.6 %collective-permute-start.9 = (f32[3,8,512]{2,1,0:T(8,128)S(1)}, f32[3,8,512]{2,1,0:T(8,128)S(1)}, u32[]{:S(2)}, u32[]{:S(2)}) collective-permute-start(f32[3,8,512]{2,1,0:T(8,128)S(1)} %pad_maximum_fusion.refs_8_), channel_id=1, source_target_pairs={{0,6},{1,7},{2,4},{3,5},{4,2},{5,3},{6,0},{7,1},{8,14},{9,15},{10,... | collective-permute-start | bytes 147464 | tf_op jit(solution)/shard_map/ppermute | solution.py:588
  60.5 3.7 %collective-permute-start.8 = (f32[3,8,512]{2,1,0:T(8,128)S(1)}, f32[3,8,512]{2,1,0:T(8,128)S(1)}, u32[]{:S(2)}, u32[]{:S(2)}) collective-permute-start(f32[3,8,512]{2,1,0:T(8,128)S(1)} %pad_maximum_fusion.refs_8_), channel_id=1, source_target_pairs={{0,2},{1,3},{2,0},{3,1},{4,6},{5,7},{6,4},{7,5},{8,10},{9,11},{10,... | collective-permute-start | bytes 147464 | tf_op jit(solution)/shard_map/ppermute | solution.py:588
  74.7 9.2 %collective-permute-start.11 = (bf16[128,512]{1,0:T(8,128)(2,1)}, bf16[128,512]{1,0:T(8,128)(2,1)S(1)}, u32[]{:S(2)}, u32[]{:S(2)}) collective-permute-start(bf16[128,512]{1,0:T(8,128)(2,1)} %get-tuple-element.80), channel_id=1, source_target_pairs={{0,1},{1,0},{2,3},{3,2},{4,5},{5,4},{6,7},{7,6},{8,9},{9,8},{10,11... | collective-permute-start | bytes 393224 | tf_op jit(solution)/shard_map/ppermute | solution.py:588
  76.1 7.8 %collective-permute-start.12 = (bf16[128,512]{1,0:T(8,128)(2,1)}, bf16[128,512]{1,0:T(8,128)(2,1)S(1)}, u32[]{:S(2)}, u32[]{:S(2)}) collective-permute-start(bf16[128,512]{1,0:T(8,128)(2,1)} %get-tuple-element.81), channel_id=1, source_target_pairs={{0,1},{1,0},{2,3},{3,2},{4,5},{5,4},{6,7},{7,6},{8,9},{9,8},{10,11... | collective-permute-start | bytes 393224 | tf_op jit(solution)/shard_map/ppermute | solution.py:588
  76.2 7.7 %collective-permute-start.13 = (bf16[128,512]{1,0:T(8,128)(2,1)}, bf16[128,512]{1,0:T(8,128)(2,1)S(1)}, u32[]{:S(2)}, u32[]{:S(2)}) collective-permute-start(bf16[128,512]{1,0:T(8,128)(2,1)} %get-tuple-element.82), channel_id=1, source_target_pairs={{0,1},{1,0},{2,3},{3,2},{4,5},{5,4},{6,7},{7,6},{8,9},{9,8},{10,11... | collective-permute-start | bytes 393224 | tf_op jit(solution)/shard_map/ppermute | solution.py:588
  76.6 24.1 %all-to-all-start.2 = ((bf16[16,128,128]{2,1,0:T(8,128)(2,1)}), bf16[16,128,128]{2,1,0:T(8,128)(2,1)S(1)}, u32[]{:S(2)}, u32[]{:S(2)}) async-start(bf16[16,128,128]{2,1,0:T(8,128)(2,1)} %get-tuple-element.76), calls=%async_computation.2 | async-start | bytes 1048576 | tf_op jit(solution)/shard_map/all_to_all | solution.py:666
  83.5 19.2 %collective-permute-start.14 = (bf16[128,512]{1,0:T(8,128)(2,1)}, bf16[128,512]{1,0:T(8,128)(2,1)S(1)}, u32[]{:S(2)}, u32[]{:S(2)}) collective-permute-start(bf16[128,512]{1,0:T(8,128)(2,1)} %get-tuple-element.96), channel_id=1, source_target_pairs={{0,1},{1,0},{2,3},{3,2},{4,5},{5,4},{6,7},{7,6},{8,9},{9,8},{10,11... | collective-permute-start | bytes 393224 | tf_op jit(solution)/shard_map/ppermute | solution.py:588
  85.1 17.6 %collective-permute-start.15 = (bf16[128,512]{1,0:T(8,128)(2,1)S(1)}, bf16[128,512]{1,0:T(8,128)(2,1)S(1)}, u32[]{:S(2)}, u32[]{:S(2)}) collective-permute-start(bf16[128,512]{1,0:T(8,128)(2,1)S(1)} %get-tuple-element.83), channel_id=1, source_target_pairs={{0,2},{1,3},{2,0},{3,1},{4,6},{5,7},{6,4},{7,5},{8,10},{9,11},{10,... | collective-permute-start | bytes 393224 | tf_op jit(solution)/shard_map/ppermute | solution.py:588
  85.2 19.0 %collective-permute-start.17 = (bf16[128,512]{1,0:T(8,128)(2,1)S(1)}, bf16[128,512]{1,0:T(8,128)(2,1)S(1)}, u32[]{:S(2)}, u32[]{:S(2)}) collective-permute-start(bf16[128,512]{1,0:T(8,128)(2,1)S(1)} %get-tuple-element.84), channel_id=1, source_target_pairs={{0,4},{1,5},{2,6},{3,7},{4,0},{5,1},{6,2},{7,3},{8,12},{9,13},{10,... | collective-permute-start | bytes 393224 | tf_op jit(solution)/shard_map/ppermute | solution.py:588
  88.1 21.3 %collective-permute-start.16 = (bf16[128,512]{1,0:T(8,128)(2,1)S(1)}, bf16[128,512]{1,0:T(8,128)(2,1)S(1)}, u32[]{:S(2)}, u32[]{:S(2)}) collective-permute-start(bf16[128,512]{1,0:T(8,128)(2,1)S(1)} %get-tuple-element.85), channel_id=1, source_target_pairs={{0,6},{1,7},{2,4},{3,5},{4,2},{5,3},{6,0},{7,1},{8,14},{9,15},{10,... | collective-permute-start | bytes 393224 | tf_op jit(solution)/shard_map/ppermute | solution.py:588
  89.0 21.6 %copy-start.3 = (bf16[128,512]{1,0:T(8,128)(2,1)S(1)}, bf16[128,512]{1,0:T(8,128)(2,1)}, u32[]{:S(2)}) copy-start(bf16[128,512]{1,0:T(8,128)(2,1)} %get-tuple-element.95.refs_0_) | copy-start | bytes 393220
  100.8 5.2 %collective-permute-start.23 = (bf16[128,128]{1,0:T(8,128)(2,1)S(1)}, bf16[128,128]{1,0:T(8,128)(2,1)S(1)}, u32[]{:S(2)}, u32[]{:S(2)}) collective-permute-start(bf16[128,128]{1,0:T(8,128)(2,1)S(1)} %reduce_sum.12.refs_5_), channel_id=1, source_target_pairs={{0,6},{1,7},{2,4},{3,5},{4,2},{5,3},{6,0},{7,1},{8,14},{9,15},{10,... | collective-permute-start | bytes 98312 | tf_op jit(solution)/shard_map/ppermute | solution.py:588
  102.7 4.4 %collective-permute-start.21 = (bf16[128,128]{1,0:T(8,128)(2,1)S(1)}, bf16[128,128]{1,0:T(8,128)(2,1)S(1)}, u32[]{:S(2)}, u32[]{:S(2)}) collective-permute-start(bf16[128,128]{1,0:T(8,128)(2,1)S(1)} %reduce_sum.12.refs_5_), channel_id=1, source_target_pairs={{0,4},{1,5},{2,6},{3,7},{4,0},{5,1},{6,2},{7,3},{8,12},{9,13},{10,... | collective-permute-start | bytes 98312 | tf_op jit(solution)/shard_map/ppermute | solution.py:588
  102.7 6.7 %collective-permute-start.19 = (bf16[128,128]{1,0:T(8,128)(2,1)S(1)}, bf16[128,128]{1,0:T(8,128)(2,1)S(1)}, u32[]{:S(2)}, u32[]{:S(2)}) collective-permute-start(bf16[128,128]{1,0:T(8,128)(2,1)S(1)} %reduce_sum.12.refs_5_), channel_id=1, source_target_pairs={{0,2},{1,3},{2,0},{3,1},{4,6},{5,7},{6,4},{7,5},{8,10},{9,11},{10,... | collective-permute-start | bytes 98312 | tf_op jit(solution)/shard_map/ppermute | solution.py:588
  104.2 5.2 %collective-permute-start.18 = (bf16[128,128]{1,0:T(8,128)(2,1)S(1)}, bf16[128,128]{1,0:T(8,128)(2,1)S(1)}, u32[]{:S(2)}, u32[]{:S(2)}) collective-permute-start(bf16[128,128]{1,0:T(8,128)(2,1)S(1)} %reduce_sum.12.refs_5_), channel_id=1, source_target_pairs={{0,1},{1,0},{2,3},{3,2},{4,5},{5,4},{6,7},{7,6},{8,9},{9,8},{10,11... | collective-permute-start | bytes 98312 | tf_op jit(solution)/shard_map/ppermute | solution.py:588
  106.0 3.4 %collective-permute-start.24 = (bf16[128,128]{1,0:T(8,128)(2,1)S(1)}, bf16[128,128]{1,0:T(8,128)(2,1)S(1)}, u32[]{:S(2)}, u32[]{:S(2)}) collective-permute-start(bf16[128,128]{1,0:T(8,128)(2,1)S(1)} %collective-permute-done.23.refs_11_), channel_id=1, source_target_pairs={{0,1},{1,0},{2,3},{3,2},{4,5},{5,4},{6,7},{7,6},{8,9},{9,8},{10,11... | collective-permute-start | bytes 98312 | tf_op jit(solution)/shard_map/ppermute | solution.py:588
  107.0 3.2 %collective-permute-start.22 = (bf16[128,128]{1,0:T(8,128)(2,1)S(1)}, bf16[128,128]{1,0:T(8,128)(2,1)S(1)}, u32[]{:S(2)}, u32[]{:S(2)}) collective-permute-start(bf16[128,128]{1,0:T(8,128)(2,1)S(1)} %collective-permute-done.21.refs_9_), channel_id=1, source_target_pairs={{0,1},{1,0},{2,3},{3,2},{4,5},{5,4},{6,7},{7,6},{8,9},{9,8},{10,11... | collective-permute-start | bytes 98312 | tf_op jit(solution)/shard_map/ppermute | solution.py:588
  109.4 1.2 %collective-permute-start.20 = (bf16[128,128]{1,0:T(8,128)(2,1)S(1)}, bf16[128,128]{1,0:T(8,128)(2,1)S(1)}, u32[]{:S(2)}, u32[]{:S(2)}) collective-permute-start(bf16[128,128]{1,0:T(8,128)(2,1)S(1)} %collective-permute-done.19.refs_7_), channel_id=1, source_target_pairs={{0,1},{1,0},{2,3},{3,2},{4,5},{5,4},{6,7},{7,6},{8,9},{9,8},{10,11... | collective-permute-start | bytes 98312 | tf_op jit(solution)/shard_map/ppermute | solution.py:588

commit v8 on v7

--- a/solution.py
+++ b/solution.py
@@ -485,7 +485,7 @@
             pb = pull.astype(BF)
             bs = (b_ref[at, :] * turned[k][:, 64 + hh : 65 + hh]).astype(BF)
             dx = dxl[hh, at, :].astype(F32) + dot(bs, pb, 1, 0)
-            dxs[pl.ds(k * BLOCK * nh + h, BLOCK, stride=nh), :] = dx
+            dxs[h, at, :] = dx.astype(BF)
             dcs = dot(sb, y, 1, 1) * grow[k]
             dct[k] += dcs
             dbs = dot(pb, x, 1, 1) * tail[k]
@@ -508,11 +508,7 @@
             db_ref[sl, :] = dbl[sl, :] + dbt[k].T
             dc_ref[sl, :] = dcl[sl, :] + dct[k].T
             da_ref[:, sl] = dot(drow[:, sl], late, 1, 0, HIGHEST)
-            dx_ref[sl] = (
-                dxs[k * BLOCK * nh : (k + 1) * BLOCK * nh, :]
-                .reshape(BLOCK, nh, 128)
-                .astype(BF)
-            )
+            dx_ref[sl] = jnp.swapaxes(dxs[:, sl, :], 0, 1)
 
 
 def ssd_grad(xh, yh, states, cum, b, c, local):
@@ -550,7 +546,7 @@
             jax.ShapeDtypeStruct((tok, 128), F32),
         ],
         scratch_shapes=[sq] * 5
-        + [pltpu.VMEM((heads, tok), F32), pltpu.VMEM((tok * heads, width), F32)],
+        + [pltpu.VMEM((heads, tok), F32), pltpu.VMEM((heads, tok, width), BF)],
         compiler_params=pltpu.CompilerParams(vmem_limit_bytes=60 << 20),
         cost_estimate=pl.CostEstimate(
             flops=6 * 10**9, bytes_accessed=10**7, transcendentals=10**6
@@ -599,7 +595,7 @@
 
 
 def gather_heads(v, other=None):
-    out = [v] + [None] * 7
+    out = [v if other is None else after(v, other)] + [None] * 7
     for m in (2, 6, 4):
         out[m] = swap(v, m) if other is None else after(swap(v, m), other)
     for m in (0, 2, 6, 4):

time: 112 us -> 111 us (level)
  transfers between devices with their start and end apart: 28 -> 28, of which waited for: 9 -> 10; matrix products, arithmetic and copies ran while one was open for 0% -> 0% of each run, Pallas kernels for 36% -> 36%
where the time goes in v8:
time: 111 us
  Pallas kernels  50.1 us (45%)
  starting transfers between devices  46.9 us (42%)
  waiting for transfers between devices  11.1 us (10%)
  local copies, waits for them, and re-layouts  1.66 us (1%)
    ppermute x25, starting transfers between devices, swap(): return lax.ppermute(v, 'head', [(i, i ^ m) for i in range(8)])  26.7 us
    pallas_call x1, Pallas kernels, ssd_local(): pl.pallas_call(ssd_local_kernel, grid=(heads // STEP_HEADS,), in_specs=[p...  11.9 us
    pallas_call x1, Pallas kernels, ssd_grad(): pl.pallas_call(ssd_grad_kernel, grid=(heads // STEP_HEADS,), in_specs=[pe...  11 us
    pallas_call x1, Pallas kernels, attn_grad(): pl.pallas_call(attn_grad_kernel, in_specs=[SM] + [VM] * 13, out_specs=[HB...  10.5 us
    all_to_all x1, starting transfers between devices, per_device(): recv = lax.all_to_all(send, 'seq', 0, 0)  8.74 us
    pallas_call x1, Pallas kernels, ssd_send(): pl.pallas_call(ssd_send_kernel, grid_spec=pltpu.PrefetchScalarGridSpec(nu...  8.22 us
    ppermute x25, waiting for transfers between devices, swap(): return lax.ppermute(v, 'head', [(i, i ^ m) for i in range(8)])  7.47 us
    all_to_all x1, starting transfers between devices, per_device(): back = lax.all_to_all(back, 'seq', 0, 0)  6.81 us
  transfers between devices with their start and end apart: 28, of which 10 were waited for; matrix products, arithmetic and copies ran while one was open for 0% of the time, Pallas kernels for 36%

profile of v8, /device:TPU:1, one launch (start us, length us, event | category | flops | bytes accessed | tf_op | source)
XLA Modules:
  0.0 110.7 jit_solution(15672036578485601258)
XLA Ops:
  0.6 8.2 %ssd_send.1 = (bf16[16,400,128]{2,1,0:T(8,128)(2,1)}, bf16[16,512,128]{2,1,0:T(8,128)(2,1)}, bf16[16,512,128]{2,1,0:T(8,128)(2,1)}, f32[16,512]{1,0:T(8,128)}, bf16[2,512,128]{2,1,0:T(8,128)(2,1)}) custom-call(bf16[512,16,128]{2,1,0:T(8,128)(2,1)} %x_ref.1, bf16[512,16,128]{2,1,0:T(8,128)(2,1)} %y_ref.1, f32[16,512]{1,0:T(8,128)} %bitcast.22, ...), custom_call_target="tpu_custom_call" | custom-call | flops 3000000000 | bytes 10000000 | tf_op jit(solution)/shard_map/ssd_send/pallas_call | solution.py:105
  8.9 0.0 copy-start
  8.9 8.7 %all-to-all-start = ((bf16[16,400,128]{2,1,0:T(8,128)(2,1)}), bf16[16,400,128]{2,1,0:T(8,128)(2,1)S(1)}, u32[]{:S(2)}, u32[]{:S(2)}) async-start(bf16[16,400,128]{2,1,0:T(8,128)(2,1)} %get-tuple-element.56), calls=%async_computation | async-start | bytes 3276800 | tf_op jit(solution)/shard_map/all_to_all | solution.py:650
  17.6 2.6 %collective-permute-start.5 = (bf16[2,512,128]{2,1,0:T(8,128)(2,1)S(1)}, bf16[2,512,128]{2,1,0:T(8,128)(2,1)S(1)}, u32[]{:S(2)}, u32[]{:S(2)}) collective-permute-start(bf16[2,512,128]{2,1,0:T(8,128)(2,1)S(1)} %copy-done), channel_id=1, source_target_pairs={{0,6},{1,7},{2,4},{3,5},{4,2},{5,3},{6,0},{7,1},{8,14},{9,15},{10,... | collective-permute-start | bytes 786440 | tf_op jit(solution)/shard_map/ppermute | solution.py:584
  20.2 0.5 collective-permute-start.3
  20.7 0.3 collective-permute-start.1
  21.0 11.9 %ssd_local.1 = (bf16[16,512,128]{2,1,0:T(8,128)(2,1)}, bf16[16,6,128,128]{3,2,1,0:T(8,128)(2,1)}, f32[16,512]{1,0:T(8,128)}, f32[512,128]{1,0:T(8,128)}, f32[512,128]{1,0:T(8,128)}) custom-call(bf16[16,512,128]{2,1,0:T(8,128)(2,1)} %get-tuple-element.88.xh, bf16[16,512,128]{2,1,0:T(8,128)(2,1)} %get-tuple-element.58.yh, f32[16,512]{1,0:T(8,128)} %get-tuple-element.59.cum, ...), custom_call_target="tpu_custom_call" | custom-call | flops 4000000000 | bytes 10000000 | tf_op jit(solution)/shard_map/ssd_local/pallas_call | solution.py:425
  32.9 0.0 copy-start.4
  32.9 1.9 %collective-permute-start = (bf16[2,512,128]{2,1,0:T(8,128)(2,1)S(1)}, bf16[2,512,128]{2,1,0:T(8,128)(2,1)S(1)}, u32[]{:S(2)}, u32[]{:S(2)}) collective-permute-start(bf16[2,512,128]{2,1,0:T(8,128)(2,1)S(1)} %copy-done), channel_id=1, source_target_pairs={{0,1},{1,0},{2,3},{3,2},{4,5},{5,4},{6,7},{7,6},{8,9},{9,8},{10,11... | collective-permute-start | bytes 786440 | tf_op jit(solution)/shard_map/ppermute | solution.py:584
  34.7 0.0 collective-permute-done.1.refs_2_
  34.8 0.1 collective-permute-start.2
  34.9 0.5 collective-permute-start.4
  35.3 0.1 collective-permute-start.6
  35.4 0.5 collective-permute-done.refs_1_
  35.9 0.5 collective-permute-done.2.refs_3_
  36.4 0.4 collective-permute-done.4.refs_5_
  36.7 0.4 collective-permute-done.6.refs_7_
  37.1 0.7 copy-done.1
  37.8 3.6 %all-to-all-done.recv = bf16[16,400,128]{2,1,0:T(8,128)(2,1)S(1)} async-done(((bf16[16,400,128]{2,1,0:T(8,128)(2,1)}), bf16[16,400,128]{2,1,0:T(8,128)(2,1)S(1)}, u32[]{:S(2)}, u32[]{:S(2)}) %all-to-all-start) | async-done | bytes 1638432 | tf_op jit(solution)/shard_map/all_to_all | solution.py:650
  41.4 1.3 %scan.1 = bf16[16,256,128]{2,1,0:T(8,128)(2,1)} custom-call(bf16[16,400,128]{2,1,0:T(8,128)(2,1)S(1)} %all-to-all-done.recv), custom_call_target="tpu_custom_call" | custom-call | tf_op jit(solution)/shard_map/scan/pallas_call | solution.py:164
  42.7 4.6 %all-to-all-start.1 = ((bf16[16,256,128]{2,1,0:T(8,128)(2,1)}), bf16[16,256,128]{2,1,0:T(8,128)(2,1)}, u32[]{:S(2)}, u32[]{:S(2)}) async-start(bf16[16,256,128]{2,1,0:T(8,128)(2,1)} %scan.1), calls=%async_computation.1 | async-start | bytes 2097152 | tf_op jit(solution)/shard_map/all_to_all | solution.py:654
  47.3 0.0 copy-start.2
  47.3 0.9 copy-done.2
  48.3 5.3 %attn_stat.1 = (f32[3,8,512]{2,1,0:T(8,128)S(1)}, f32[3,8,512]{2,1,0:T(8,128)S(1)}) custom-call(s32[16]{0:T(128)S(1)} %copy-done.4, bf16[16,400,128]{2,1,0:T(8,128)(2,1)S(1)} %all-to-all-done.recv, bf16[2,512,128]{2,1,0:T(8,128)(2,1)S(1)} %copy-done, bf16[2,512,128]{2,1,0:T(8,128)(2,1)S(1)} %collective-permute-done.refs_1_, ...), custom_call_target="tpu_custom_call" | custom-call | flops 100000000 | bytes 100000 | tf_op jit(solution)/shard_map/attn_stat/pallas_call | solution.py:229
  53.6 2.3 %collective-permute-start.7 = (f32[3,8,512]{2,1,0:T(8,128)S(1)}, f32[3,8,512]{2,1,0:T(8,128)S(1)}, u32[]{:S(2)}, u32[]{:S(2)}) collective-permute-start(f32[3,8,512]{2,1,0:T(8,128)S(1)} %get-tuple-element.68), channel_id=1, source_target_pairs={{0,1},{1,0},{2,3},{3,2},{4,5},{5,4},{6,7},{7,6},{8,9},{9,8},{10,11... | collective-permute-start | bytes 147464 | tf_op jit(solution)/shard_map/ppermute | solution.py:584
  55.9 0.9 collective-permute-done.7
  56.8 2.8 %collective-permute-start.10 = (f32[3,8,512]{2,1,0:T(8,128)S(1)}, f32[3,8,512]{2,1,0:T(8,128)S(1)}, u32[]{:S(2)}, u32[]{:S(2)}) collective-permute-start(f32[3,8,512]{2,1,0:T(8,128)S(1)} %pad_maximum_fusion.refs_8_), channel_id=1, source_target_pairs={{0,4},{1,5},{2,6},{3,7},{4,0},{5,1},{6,2},{7,3},{8,12},{9,13},{10,... | collective-permute-start | bytes 147464 | tf_op jit(solution)/shard_map/ppermute | solution.py:584
  59.6 0.9 collective-permute-start.9
  60.5 0.0 collective-permute-start.8
  60.5 1.2 %collective-permute-done.10.refs_11_ = f32[3,8,512]{2,1,0:T(8,128)S(1)} collective-permute-done((f32[3,8,512]{2,1,0:T(8,128)S(1)}, f32[3,8,512]{2,1,0:T(8,128)S(1)}, u32[]{:S(2)}, u32[]{:S(2)}) %collective-permute-start.10) | collective-permute-done | bytes 49184 | tf_op jit(solution)/shard_map/ppermute | solution.py:584
  61.7 2.5 %collective-permute-done.9.refs_10_ = f32[3,8,512]{2,1,0:T(8,128)S(1)} collective-permute-done((f32[3,8,512]{2,1,0:T(8,128)S(1)}, f32[3,8,512]{2,1,0:T(8,128)S(1)}, u32[]{:S(2)}, u32[]{:S(2)}) %collective-permute-start.9) | collective-permute-done | bytes 49184 | tf_op jit(solution)/shard_map/ppermute | solution.py:584
  64.2 0.0 collective-permute-done.8.refs_9_
  64.2 10.5 %attn_grad.1 = (bf16[16,128,128]{2,1,0:T(8,128)(2,1)}, bf16[128,512]{1,0:T(8,128)(2,1)}, bf16[128,512]{1,0:T(8,128)(2,1)}, bf16[128,512]{1,0:T(8,128)(2,1)}, bf1...) custom-call(s32[16]{0:T(128)S(1)} %copy-done.4, ...), custom_call_target="tpu_custom_call" | custom-call | flops 100000000 | bytes 100000 | tf_op jit(solution)/shard_map/attn_grad/pallas_call | solution.py:311
  74.6 0.0 all-to-all-done.1.states
  74.7 1.5 %collective-permute-start.11 = (bf16[128,512]{1,0:T(8,128)(2,1)}, bf16[128,512]{1,0:T(8,128)(2,1)S(1)}, u32[]{:S(2)}, u32[]{:S(2)}) collective-permute-start(bf16[128,512]{1,0:T(8,128)(2,1)} %get-tuple-element.82), channel_id=1, source_target_pairs={{0,1},{1,0},{2,3},{3,2},{4,5},{5,4},{6,7},{7,6},{8,9},{9,8},{10,11... | collective-permute-start | bytes 393224 | tf_op jit(solution)/shard_map/ppermute | solution.py:584
  76.1 0.1 collective-permute-start.12
  76.2 0.4 collective-permute-start.13
  76.6 6.8 %all-to-all-start.2 = ((bf16[16,128,128]{2,1,0:T(8,128)(2,1)}), bf16[16,128,128]{2,1,0:T(8,128)(2,1)S(1)}, u32[]{:S(2)}, u32[]{:S(2)}) async-start(bf16[16,128,128]{2,1,0:T(8,128)(2,1)} %get-tuple-element.78), calls=%async_computation.2 | async-start | bytes 1048576 | tf_op jit(solution)/shard_map/all_to_all | solution.py:662
  83.5 0.4 collective-permute-start.14
  83.9 0.0 collective-permute-done.11.refs_3_
  83.9 0.0 collective-permute-done.12.refs_4_
  83.9 0.0 collective-permute-done.13.refs_5_
  83.9 1.2 %pair_sums.1 = (bf16[128,512]{1,0:T(8,128)(2,1)S(1)}, bf16[128,512]{1,0:T(8,128)(2,1)S(1)}, bf16[128,512]{1,0:T(8,128)(2,1)S(1)}) custom-call(bf16[128,512]{1,0:T(8,128)(2,1)} %get-tuple-element.79.refs_0_, bf16[128,512]{1,0:T(8,128)(2,1)} %get-tuple-element.80.refs_1_, bf16[128,512]{1,0:T(8,128)(2,1)} %get-tuple-element.81.refs_2_, ...), custom_call_target="tpu_custom_call" | custom-call | tf_op jit(solution)/shard_map/pair_sums/pallas_call | solution.py:620
  85.1 0.1 collective-permute-start.15
  85.2 2.9 %collective-permute-start.17 = (bf16[128,512]{1,0:T(8,128)(2,1)S(1)}, bf16[128,512]{1,0:T(8,128)(2,1)S(1)}, u32[]{:S(2)}, u32[]{:S(2)}) collective-permute-start(bf16[128,512]{1,0:T(8,128)(2,1)S(1)} %get-tuple-element.86), channel_id=1, source_target_pairs={{0,4},{1,5},{2,6},{3,7},{4,0},{5,1},{6,2},{7,3},{8,12},{9,13},{10,... | collective-permute-start | bytes 393224 | tf_op jit(solution)/shard_map/ppermute | solution.py:584
  88.1 0.9 collective-permute-start.16
  89.0 11.0 %ssd_grad.1 = (bf16[512,16,128]{2,1,0:T(8,128)(2,1)}, f32[16,512]{1,0:T(8,128)}, f32[512,128]{1,0:T(8,128)}, f32[512,128]{1,0:T(8,128)}) custom-call(bf16[16,512,128]{2,1,0:T(8,128)(2,1)} %get-tuple-element.88.xh, bf16[16,512,128]{2,1,0:T(8,128)(2,1)} %get-tuple-element.58.yh, bf16[16,256,128]{2,1,0:T(8,128)(2,1)} %all-to-all-done.1.states, ...), custom_call_target="tpu_custom_call" | custom-call | flops 6000000000 | bytes 10000000 | tf_op jit(solution)/shard_map/ssd_grad/pallas_call | solution.py:520
  100.0 0.0 all-to-all-done.2
  100.0 0.1 reduce_sum.12.refs_5_
  100.1 1.8 %collective-permute-start.23 = (bf16[128,128]{1,0:T(8,128)(2,1)S(1)}, bf16[128,128]{1,0:T(8,128)(2,1)S(1)}, u32[]{:S(2)}, u32[]{:S(2)}) collective-permute-start(bf16[128,128]{1,0:T(8,128)(2,1)S(1)} %reduce_sum.12.refs_5_), channel_id=1, source_target_pairs={{0,6},{1,7},{2,4},{3,5},{4,2},{5,3},{6,0},{7,1},{8,14},{9,15},{10,... | collective-permute-start | bytes 98312 | tf_op jit(solution)/shard_map/ppermute | solution.py:584
  101.9 0.0 collective-permute-done.14.refs_1_
  101.9 0.0 collective-permute-start.21
  101.9 0.0 collective-permute-done.15.refs_2_
  101.9 1.5 %collective-permute-start.19 = (bf16[128,128]{1,0:T(8,128)(2,1)S(1)}, bf16[128,128]{1,0:T(8,128)(2,1)S(1)}, u32[]{:S(2)}, u32[]{:S(2)}) collective-permute-start(bf16[128,128]{1,0:T(8,128)(2,1)S(1)} %reduce_sum.12.refs_5_), channel_id=1, source_target_pairs={{0,2},{1,3},{2,0},{3,1},{4,6},{5,7},{6,4},{7,5},{8,10},{9,11},{10,... | collective-permute-start | bytes 98312 | tf_op jit(solution)/shard_map/ppermute | solution.py:584
  103.4 1.9 %collective-permute-start.18 = (bf16[128,128]{1,0:T(8,128)(2,1)S(1)}, bf16[128,128]{1,0:T(8,128)(2,1)S(1)}, u32[]{:S(2)}, u32[]{:S(2)}) collective-permute-start(bf16[128,128]{1,0:T(8,128)(2,1)S(1)} %reduce_sum.12.refs_5_), channel_id=1, source_target_pairs={{0,1},{1,0},{2,3},{3,2},{4,5},{5,4},{6,7},{7,6},{8,9},{9,8},{10,11... | collective-permute-start | bytes 98312 | tf_op jit(solution)/shard_map/ppermute | solution.py:584
  105.3 0.0 collective-permute-done.23.refs_11_
  105.3 1.0 collective-permute-start.24
  106.3 0.0 collective-permute-done.21.refs_9_
  106.3 2.3 %collective-permute-start.22 = (bf16[128,128]{1,0:T(8,128)(2,1)S(1)}, bf16[128,128]{1,0:T(8,128)(2,1)S(1)}, u32[]{:S(2)}, u32[]{:S(2)}) collective-permute-start(bf16[128,128]{1,0:T(8,128)(2,1)S(1)} %collective-permute-done.21.refs_9_), channel_id=1, source_target_pairs={{0,1},{1,0},{2,3},{3,2},{4,5},{5,4},{6,7},{7,6},{8,9},{9,8},{10,11... | collective-permute-start | bytes 98312 | tf_op jit(solution)/shard_map/ppermute | solution.py:584
  108.6 0.0 collective-permute-done.19.refs_7_
  108.6 0.0 collective-permute-start.20
  108.7 0.8 collective-permute-done.22.refs_10_
  109.5 0.4 collective-permute-done.20.refs_8_
  109.9 0.8 finish.1
  (14 shorter events, 0.1 us)
Async XLA Ops:
  8.9 8.8 %copy-start = (bf16[2,512,128]{2,1,0:T(8,128)(2,1)S(1)}, bf16[2,512,128]{2,1,0:T(8,128)(2,1)}, u32[]{:S(2)}) copy-start(bf16[2,512,128]{2,1,0:T(8,128)(2,1)} %get-tuple-element.61.refs_0_) | copy-start | bytes 786436
  8.9 32.5 %all-to-all-start = ((bf16[16,400,128]{2,1,0:T(8,128)(2,1)}), bf16[16,400,128]{2,1,0:T(8,128)(2,1)S(1)}, u32[]{:S(2)}, u32[]{:S(2)}) async-start(bf16[16,400,128]{2,1,0:T(8,128)(2,1)} %get-tuple-element.56), calls=%async_computation | async-start | bytes 3276800 | tf_op jit(solution)/shard_map/all_to_all | solution.py:650
  17.6 17.1 %collective-permute-start.5 = (bf16[2,512,128]{2,1,0:T(8,128)(2,1)S(1)}, bf16[2,512,128]{2,1,0:T(8,128)(2,1)S(1)}, u32[]{:S(2)}, u32[]{:S(2)}) collective-permute-start(bf16[2,512,128]{2,1,0:T(8,128)(2,1)S(1)} %copy-done), channel_id=1, source_target_pairs={{0,6},{1,7},{2,4},{3,5},{4,2},{5,3},{6,0},{7,1},{8,14},{9,15},{10,... | collective-permute-start | bytes 786440 | tf_op jit(solution)/shard_map/ppermute | solution.py:584
  20.2 14.6 %collective-permute-start.3 = (bf16[2,512,128]{2,1,0:T(8,128)(2,1)S(1)}, bf16[2,512,128]{2,1,0:T(8,128)(2,1)S(1)}, u32[]{:S(2)}, u32[]{:S(2)}) collective-permute-start(bf16[2,512,128]{2,1,0:T(8,128)(2,1)S(1)} %copy-done), channel_id=1, source_target_pairs={{0,4},{1,5},{2,6},{3,7},{4,0},{5,1},{6,2},{7,3},{8,12},{9,13},{10,... | collective-permute-start | bytes 786440 | tf_op jit(solution)/shard_map/ppermute | solution.py:584
  20.7 14.0 %collective-permute-start.1 = (bf16[2,512,128]{2,1,0:T(8,128)(2,1)S(1)}, bf16[2,512,128]{2,1,0:T(8,128)(2,1)S(1)}, u32[]{:S(2)}, u32[]{:S(2)}) collective-permute-start(bf16[2,512,128]{2,1,0:T(8,128)(2,1)S(1)} %copy-done), channel_id=1, source_target_pairs={{0,2},{1,3},{2,0},{3,1},{4,6},{5,7},{6,4},{7,5},{8,10},{9,11},{10,... | collective-permute-start | bytes 786440 | tf_op jit(solution)/shard_map/ppermute | solution.py:584
  32.9 14.5 %copy-start.4 = (s32[16]{0:T(128)S(1)}, s32[16]{0:T(128)}, u32[]{:S(2)}) copy-start(s32[16]{0:T(128)} %order.3) | copy-start | bytes 196
  32.9 3.0 %collective-permute-start = (bf16[2,512,128]{2,1,0:T(8,128)(2,1)S(1)}, bf16[2,512,128]{2,1,0:T(8,128)(2,1)S(1)}, u32[]{:S(2)}, u32[]{:S(2)}) collective-permute-start(bf16[2,512,128]{2,1,0:T(8,128)(2,1)S(1)} %copy-done), channel_id=1, source_target_pairs={{0,1},{1,0},{2,3},{3,2},{4,5},{5,4},{6,7},{7,6},{8,9},{9,8},{10,11... | collective-permute-start | bytes 786440 | tf_op jit(solution)/shard_map/ppermute | solution.py:584
  34.8 1.6 %collective-permute-start.2 = (bf16[2,512,128]{2,1,0:T(8,128)(2,1)S(1)}, bf16[2,512,128]{2,1,0:T(8,128)(2,1)S(1)}, u32[]{:S(2)}, u32[]{:S(2)}) collective-permute-start(bf16[2,512,128]{2,1,0:T(8,128)(2,1)S(1)} %collective-permute-done.1.refs_2_), channel_id=1, source_target_pairs={{0,1},{1,0},{2,3},{3,2},{4,5},{5,4},{6,7},{7,6},{8,9},{9,8},{10,11... | collective-permute-start | bytes 786440 | tf_op jit(solution)/shard_map/ppermute | solution.py:584
  34.9 1.9 %collective-permute-start.4 = (bf16[2,512,128]{2,1,0:T(8,128)(2,1)S(1)}, bf16[2,512,128]{2,1,0:T(8,128)(2,1)S(1)}, u32[]{:S(2)}, u32[]{:S(2)}) collective-permute-start(bf16[2,512,128]{2,1,0:T(8,128)(2,1)S(1)} %collective-permute-done.3.refs_4_), channel_id=1, source_target_pairs={{0,1},{1,0},{2,3},{3,2},{4,5},{5,4},{6,7},{7,6},{8,9},{9,8},{10,11... | collective-permute-start | bytes 786440 | tf_op jit(solution)/shard_map/ppermute | solution.py:584
  35.3 1.8 %collective-permute-start.6 = (bf16[2,512,128]{2,1,0:T(8,128)(2,1)S(1)}, bf16[2,512,128]{2,1,0:T(8,128)(2,1)S(1)}, u32[]{:S(2)}, u32[]{:S(2)}) collective-permute-start(bf16[2,512,128]{2,1,0:T(8,128)(2,1)S(1)} %collective-permute-done.5.refs_6_), channel_id=1, source_target_pairs={{0,1},{1,0},{2,3},{3,2},{4,5},{5,4},{6,7},{7,6},{8,9},{9,8},{10,11... | collective-permute-start | bytes 786440 | tf_op jit(solution)/shard_map/ppermute | solution.py:584
  37.1 0.7 copy-start.1
  42.7 32.0 %all-to-all-start.1 = ((bf16[16,256,128]{2,1,0:T(8,128)(2,1)}), bf16[16,256,128]{2,1,0:T(8,128)(2,1)}, u32[]{:S(2)}, u32[]{:S(2)}) async-start(bf16[16,256,128]{2,1,0:T(8,128)(2,1)} %scan.1), calls=%async_computation.1 | async-start | bytes 2097152 | tf_op jit(solution)/shard_map/all_to_all | solution.py:654
  47.3 1.0 copy-start.2
  53.6 3.1 %collective-permute-start.7 = (f32[3,8,512]{2,1,0:T(8,128)S(1)}, f32[3,8,512]{2,1,0:T(8,128)S(1)}, u32[]{:S(2)}, u32[]{:S(2)}) collective-permute-start(f32[3,8,512]{2,1,0:T(8,128)S(1)} %get-tuple-element.68), channel_id=1, source_target_pairs={{0,1},{1,0},{2,3},{3,2},{4,5},{5,4},{6,7},{7,6},{8,9},{9,8},{10,11... | collective-permute-start | bytes 147464 | tf_op jit(solution)/shard_map/ppermute | solution.py:584
  56.8 4.9 %collective-permute-start.10 = (f32[3,8,512]{2,1,0:T(8,128)S(1)}, f32[3,8,512]{2,1,0:T(8,128)S(1)}, u32[]{:S(2)}, u32[]{:S(2)}) collective-permute-start(f32[3,8,512]{2,1,0:T(8,128)S(1)} %pad_maximum_fusion.refs_8_), channel_id=1, source_target_pairs={{0,4},{1,5},{2,6},{3,7},{4,0},{5,1},{6,2},{7,3},{8,12},{9,13},{10,... | collective-permute-start | bytes 147464 | tf_op jit(solution)/shard_map/ppermute | solution.py:584
  59.6 4.6 %collective-permute-start.9 = (f32[3,8,512]{2,1,0:T(8,128)S(1)}, f32[3,8,512]{2,1,0:T(8,128)S(1)}, u32[]{:S(2)}, u32[]{:S(2)}) collective-permute-start(f32[3,8,512]{2,1,0:T(8,128)S(1)} %pad_maximum_fusion.refs_8_), channel_id=1, source_target_pairs={{0,6},{1,7},{2,4},{3,5},{4,2},{5,3},{6,0},{7,1},{8,14},{9,15},{10,... | collective-permute-start | bytes 147464 | tf_op jit(solution)/shard_map/ppermute | solution.py:584
  60.5 3.7 %collective-permute-start.8 = (f32[3,8,512]{2,1,0:T(8,128)S(1)}, f32[3,8,512]{2,1,0:T(8,128)S(1)}, u32[]{:S(2)}, u32[]{:S(2)}) collective-permute-start(f32[3,8,512]{2,1,0:T(8,128)S(1)} %pad_maximum_fusion.refs_8_), channel_id=1, source_target_pairs={{0,2},{1,3},{2,0},{3,1},{4,6},{5,7},{6,4},{7,5},{8,10},{9,11},{10,... | collective-permute-start | bytes 147464 | tf_op jit(solution)/shard_map/ppermute | solution.py:584
  74.7 9.2 %collective-permute-start.11 = (bf16[128,512]{1,0:T(8,128)(2,1)}, bf16[128,512]{1,0:T(8,128)(2,1)S(1)}, u32[]{:S(2)}, u32[]{:S(2)}) collective-permute-start(bf16[128,512]{1,0:T(8,128)(2,1)} %get-tuple-element.82), channel_id=1, source_target_pairs={{0,1},{1,0},{2,3},{3,2},{4,5},{5,4},{6,7},{7,6},{8,9},{9,8},{10,11... | collective-permute-start | bytes 393224 | tf_op jit(solution)/shard_map/ppermute | solution.py:584
  76.1 7.8 %collective-permute-start.12 = (bf16[128,512]{1,0:T(8,128)(2,1)}, bf16[128,512]{1,0:T(8,128)(2,1)S(1)}, u32[]{:S(2)}, u32[]{:S(2)}) collective-permute-start(bf16[128,512]{1,0:T(8,128)(2,1)} %get-tuple-element.83), channel_id=1, source_target_pairs={{0,1},{1,0},{2,3},{3,2},{4,5},{5,4},{6,7},{7,6},{8,9},{9,8},{10,11... | collective-permute-start | bytes 393224 | tf_op jit(solution)/shard_map/ppermute | solution.py:584
  76.2 7.7 %collective-permute-start.13 = (bf16[128,512]{1,0:T(8,128)(2,1)}, bf16[128,512]{1,0:T(8,128)(2,1)S(1)}, u32[]{:S(2)}, u32[]{:S(2)}) collective-permute-start(bf16[128,512]{1,0:T(8,128)(2,1)} %get-tuple-element.84), channel_id=1, source_target_pairs={{0,1},{1,0},{2,3},{3,2},{4,5},{5,4},{6,7},{7,6},{8,9},{9,8},{10,11... | collective-permute-start | bytes 393224 | tf_op jit(solution)/shard_map/ppermute | solution.py:584
  76.6 23.4 %all-to-all-start.2 = ((bf16[16,128,128]{2,1,0:T(8,128)(2,1)}), bf16[16,128,128]{2,1,0:T(8,128)(2,1)S(1)}, u32[]{:S(2)}, u32[]{:S(2)}) async-start(bf16[16,128,128]{2,1,0:T(8,128)(2,1)} %get-tuple-element.78), calls=%async_computation.2 | async-start | bytes 1048576 | tf_op jit(solution)/shard_map/all_to_all | solution.py:662
  83.5 18.5 %collective-permute-start.14 = (bf16[128,512]{1,0:T(8,128)(2,1)}, bf16[128,512]{1,0:T(8,128)(2,1)S(1)}, u32[]{:S(2)}, u32[]{:S(2)}) collective-permute-start(bf16[128,512]{1,0:T(8,128)(2,1)} %get-tuple-element.98), channel_id=1, source_target_pairs={{0,1},{1,0},{2,3},{3,2},{4,5},{5,4},{6,7},{7,6},{8,9},{9,8},{10,11... | collective-permute-start | bytes 393224 | tf_op jit(solution)/shard_map/ppermute | solution.py:584
  85.1 16.9 %collective-permute-start.15 = (bf16[128,512]{1,0:T(8,128)(2,1)S(1)}, bf16[128,512]{1,0:T(8,128)(2,1)S(1)}, u32[]{:S(2)}, u32[]{:S(2)}) collective-permute-start(bf16[128,512]{1,0:T(8,128)(2,1)S(1)} %get-tuple-element.85), channel_id=1, source_target_pairs={{0,2},{1,3},{2,0},{3,1},{4,6},{5,7},{6,4},{7,5},{8,10},{9,11},{10,... | collective-permute-start | bytes 393224 | tf_op jit(solution)/shard_map/ppermute | solution.py:584
  85.2 18.3 %collective-permute-start.17 = (bf16[128,512]{1,0:T(8,128)(2,1)S(1)}, bf16[128,512]{1,0:T(8,128)(2,1)S(1)}, u32[]{:S(2)}, u32[]{:S(2)}) collective-permute-start(bf16[128,512]{1,0:T(8,128)(2,1)S(1)} %get-tuple-element.86), channel_id=1, source_target_pairs={{0,4},{1,5},{2,6},{3,7},{4,0},{5,1},{6,2},{7,3},{8,12},{9,13},{10,... | collective-permute-start | bytes 393224 | tf_op jit(solution)/shard_map/ppermute | solution.py:584
  88.1 20.6 %collective-permute-start.16 = (bf16[128,512]{1,0:T(8,128)(2,1)S(1)}, bf16[128,512]{1,0:T(8,128)(2,1)S(1)}, u32[]{:S(2)}, u32[]{:S(2)}) collective-permute-start(bf16[128,512]{1,0:T(8,128)(2,1)S(1)} %get-tuple-element.87), channel_id=1, source_target_pairs={{0,6},{1,7},{2,4},{3,5},{4,2},{5,3},{6,0},{7,1},{8,14},{9,15},{10,... | collective-permute-start | bytes 393224 | tf_op jit(solution)/shard_map/ppermute | solution.py:584
  89.0 20.9 %copy-start.3 = (bf16[128,512]{1,0:T(8,128)(2,1)S(1)}, bf16[128,512]{1,0:T(8,128)(2,1)}, u32[]{:S(2)}) copy-start(bf16[128,512]{1,0:T(8,128)(2,1)} %get-tuple-element.97.refs_0_) | copy-start | bytes 393220
  100.1 5.2 %collective-permute-start.23 = (bf16[128,128]{1,0:T(8,128)(2,1)S(1)}, bf16[128,128]{1,0:T(8,128)(2,1)S(1)}, u32[]{:S(2)}, u32[]{:S(2)}) collective-permute-start(bf16[128,128]{1,0:T(8,128)(2,1)S(1)} %reduce_sum.12.refs_5_), channel_id=1, source_target_pairs={{0,6},{1,7},{2,4},{3,5},{4,2},{5,3},{6,0},{7,1},{8,14},{9,15},{10,... | collective-permute-start | bytes 98312 | tf_op jit(solution)/shard_map/ppermute | solution.py:584
  101.9 4.4 %collective-permute-start.21 = (bf16[128,128]{1,0:T(8,128)(2,1)S(1)}, bf16[128,128]{1,0:T(8,128)(2,1)S(1)}, u32[]{:S(2)}, u32[]{:S(2)}) collective-permute-start(bf16[128,128]{1,0:T(8,128)(2,1)S(1)} %reduce_sum.12.refs_5_), channel_id=1, source_target_pairs={{0,4},{1,5},{2,6},{3,7},{4,0},{5,1},{6,2},{7,3},{8,12},{9,13},{10,... | collective-permute-start | bytes 98312 | tf_op jit(solution)/shard_map/ppermute | solution.py:584
  101.9 6.7 %collective-permute-start.19 = (bf16[128,128]{1,0:T(8,128)(2,1)S(1)}, bf16[128,128]{1,0:T(8,128)(2,1)S(1)}, u32[]{:S(2)}, u32[]{:S(2)}) collective-permute-start(bf16[128,128]{1,0:T(8,128)(2,1)S(1)} %reduce_sum.12.refs_5_), channel_id=1, source_target_pairs={{0,2},{1,3},{2,0},{3,1},{4,6},{5,7},{6,4},{7,5},{8,10},{9,11},{10,... | collective-permute-start | bytes 98312 | tf_op jit(solution)/shard_map/ppermute | solution.py:584
  103.4 5.2 %collective-permute-start.18 = (bf16[128,128]{1,0:T(8,128)(2,1)S(1)}, bf16[128,128]{1,0:T(8,128)(2,1)S(1)}, u32[]{:S(2)}, u32[]{:S(2)}) collective-permute-start(bf16[128,128]{1,0:T(8,128)(2,1)S(1)} %reduce_sum.12.refs_5_), channel_id=1, source_target_pairs={{0,1},{1,0},{2,3},{3,2},{4,5},{5,4},{6,7},{7,6},{8,9},{9,8},{10,11... | collective-permute-start | bytes 98312 | tf_op jit(solution)/shard_map/ppermute | solution.py:584
  105.3 3.4 %collective-permute-start.24 = (bf16[128,128]{1,0:T(8,128)(2,1)S(1)}, bf16[128,128]{1,0:T(8,128)(2,1)S(1)}, u32[]{:S(2)}, u32[]{:S(2)}) collective-permute-start(bf16[128,128]{1,0:T(8,128)(2,1)S(1)} %collective-permute-done.23.refs_11_), channel_id=1, source_target_pairs={{0,1},{1,0},{2,3},{3,2},{4,5},{5,4},{6,7},{7,6},{8,9},{9,8},{10,11... | collective-permute-start | bytes 98312 | tf_op jit(solution)/shard_map/ppermute | solution.py:584
  106.3 3.2 %collective-permute-start.22 = (bf16[128,128]{1,0:T(8,128)(2,1)S(1)}, bf16[128,128]{1,0:T(8,128)(2,1)S(1)}, u32[]{:S(2)}, u32[]{:S(2)}) collective-permute-start(bf16[128,128]{1,0:T(8,128)(2,1)S(1)} %collective-permute-done.21.refs_9_), channel_id=1, source_target_pairs={{0,1},{1,0},{2,3},{3,2},{4,5},{5,4},{6,7},{7,6},{8,9},{9,8},{10,11... | collective-permute-start | bytes 98312 | tf_op jit(solution)/shard_map/ppermute | solution.py:584
  108.6 1.2 %collective-permute-start.20 = (bf16[128,128]{1,0:T(8,128)(2,1)S(1)}, bf16[128,128]{1,0:T(8,128)(2,1)S(1)}, u32[]{:S(2)}, u32[]{:S(2)}) collective-permute-start(bf16[128,128]{1,0:T(8,128)(2,1)S(1)} %collective-permute-done.19.refs_7_), channel_id=1, source_target_pairs={{0,1},{1,0},{2,3},{3,2},{4,5},{5,4},{6,7},{7,6},{8,9},{9,8},{10,11... | collective-permute-start | bytes 98312 | tf_op jit(solution)/shard_map/ppermute | solution.py:584
